TPU v7x, 256 devices: a whole 4x4x8 slice. The times are simulated.
256 devices in a mesh: row: 32 (over x_hi, z, core), feat: 8 (over y, x_lo).
Axes of the slice: x: 4 (x_hi: 2, x_lo: 2; x = x_hi * 2 + x_lo), y: 4, z: 8, core: 2. Of those that a mesh axis runs over, the one named last changes fastest.
Arguments:
- bin_index: int32 [1024, 98304], P('feat', 'row'), may hold values from 0 to 63
- gradient: bfloat16 [32, 98304], P(None, ('row', 'feat')), may hold values from -6 to 6
- hessian: bfloat16 [98304], P(('row', 'feat')), may hold values from 0.25 to 4
- row_node: int32 [98304], P('row'), may hold values from 0 to 7
Outputs:
- split_gain: float32 [1024, 512], P(('feat', 'row'))
- best_gain: float32 [8], replicated
All inputs are finite; a program needn't handle non-finite values.
Results may differ from a plain program's by a relative error of at most 0.0003.
Values may be sent and summed in bfloat16 or wider, within the bound.
No kernel may reach another device: no remote copies, remote signals or barrier semaphores. Data moves between devices by JAX's collectives and lax.ppermute only.
A program may use at most 128 MiB of HBM per device.

v0:
```python
import functools
import math

import jax
import jax.numpy as jnp
from jax import lax
from jax.sharding import Mesh
from jax.sharding import PartitionSpec as P

BINS = 64
NODES = 8
ROW = ("row_0", "row_1", "row_2")
FEAT = ("feat_0", "feat_1")
ROW_FEAT = ("row_0", "row_1", "row_2", "feat_0", "feat_1")
FEAT_ROW = ("feat_0", "feat_1", "row_0", "row_1", "row_2")


ridge_term = 1.0


def by_axis(x, axes):
    return functools.reduce(lax.psum, axes, x)


def gather_turned(arrays, axis, dims):
    turned = [jnp.moveaxis(a, dim, 0) for a, dim in zip(arrays, dims)]
    both = jnp.concatenate([t.reshape(len(t), -1) for t in turned], axis=1)
    result, at, gathered = (lax.all_gather(both, axis, axis=0, tiled=True), 0, [])
    for t, dim in zip(turned, dims):
        section = result[:, at : at + t[0].size].reshape(-1, *t.shape[1:])
        gathered.append(jnp.moveaxis(section, 0, dim))
        at += t[0].size
    return tuple(gathered)


def one_axis_at_a_time(x, axes):
    for axis in axes:
        x = lax.pmax(x, axis)
    return x


def masked_rows(node_ids, grad_rows, hess_rows):
    stacked = jnp.concatenate([grad_rows, hess_rows[None, :]], 0)
    picked = (node_ids[None, :] == jnp.arange(NODES, dtype=jnp.int32)[:, None]).astype(jnp.bfloat16)
    return (picked[:, None, :] * stacked[None, :, :]).reshape(-1, node_ids.shape[0])


def histogram_block(feature_block, masked):
    levels = jnp.arange(BINS, dtype=jnp.int32)
    onehot = (feature_block[:, None, :] == levels[None, :, None]).astype(jnp.bfloat16)
    return jnp.einsum("fbr,mr->fbm", onehot, masked, preferred_element_type=jnp.float32)


def score_splits(histogram, node_totals):
    left_sums = jnp.cumsum(histogram, axis=1)
    whole_sums = node_totals[None, None]
    right_sums = whole_sums - left_sums

    def part_score(sums):
        return jnp.sum(sums[..., :-1] * sums[..., :-1], axis=-1) / (sums[..., -1] + ridge_term)

    outputs_count = histogram.shape[-1] - 1
    score_terms = part_score(left_sums) + part_score(right_sums) - part_score(whole_sums)
    return jnp.transpose(0.5 / outputs_count * score_terms, (0, 2, 1))


def on_device(bin_index, gradient, hessian, row_node):
    local_features = bin_index.shape[0]
    owned_count = local_features // lax.axis_size(ROW)
    outputs_count = gradient.shape[0]
    shard_rows = gradient.shape[1]
    first_local = lax.axis_index(FEAT) * shard_rows
    local_nodes = lax.dynamic_slice_in_dim(row_node, first_local, shard_rows, 0)
    stacked = jnp.concatenate([gradient, hessian[None, :]], 0)
    picked = (local_nodes[None, :] == jnp.arange(NODES, dtype=jnp.int32)[:, None]).astype(
        jnp.bfloat16
    )
    local_totals = jnp.einsum("nr,mr->nm", picked, stacked, preferred_element_type=jnp.float32)
    node_totals = by_axis(local_totals, ROW_FEAT)
    grad_rows, hess_rows = gather_turned((gradient, hessian), FEAT, (1, 0))
    masked = masked_rows(row_node, grad_rows, hess_rows)
    group_size = math.gcd(owned_count * lax.axis_size(ROW), 16)

    def one_group(step_index):
        feature_block = lax.dynamic_slice_in_dim(bin_index, step_index * group_size, group_size, 0)
        return histogram_block(feature_block, masked).reshape(group_size, -1)

    pieces = lax.map(
        one_group, jnp.arange(owned_count * lax.axis_size(ROW) // group_size, dtype=jnp.int32)
    )
    owned = lax.psum_scatter(
        pieces.reshape(owned_count * lax.axis_size(ROW), -1), ROW, scatter_dimension=0, tiled=True
    )
    histogram = owned.reshape(owned_count, BINS, NODES, outputs_count + 1)
    split_gain = score_splits(histogram, node_totals)
    best_gain = one_axis_at_a_time(jnp.max(split_gain, axis=(0, 2)), ROW_FEAT)
    return (split_gain.reshape(owned_count, NODES * BINS), best_gain)


def solution(mesh):
    split = Mesh(
        mesh.devices.reshape(2, 8, 2, 4, 2), ("row_0", "row_1", "row_2", "feat_0", "feat_1")
    )
    in_specs = (P(FEAT, ROW), P(None, ROW_FEAT), P(ROW_FEAT), P(ROW))
    out_specs = (P(FEAT_ROW, None), P())
    return jax.shard_map(
        on_device, mesh=split, in_specs=in_specs, out_specs=out_specs, check_vma=False
    )
```

profile of v0, /device:TPU:1, one launch (start us, length us, event | category | flops | bytes accessed | tf_op | source)
XLA Modules:
  0.0 492.5 jit_solution(4943222124883276265)
XLA Ops:
  8.6 24.4 %all_gather.3 = bf16[3072,33]{0,1:T(8,128)(2,1)S(1)} all-gather(bf16[384,33]{0,1:T(8,128)(2,1)S(1)} %pad_maximum_fusion.1), channel_id=1, replica_groups=mesh['row_0'=2,'row_1'=8,'row_2'=2,'feat_0'=4,'feat_1'=2] {'feat_0','fea..., dimensions={0}, use_global_device_ids=true | all-gather | bytes 228096 | tf_op jit(solution)/shard_map/all_gather | solution.py:28
  33.8 86.3 %while.11 = (s32[]{:T(128)}, f32[8,16,16896]{2,1,0:T(8,128)}, s32[8]{0:T(128)S(1)}, s32[128,3072]{1,0:T(8,128)}, bf16[33,3072]{1,0:T(8,128)(2,1)S(1)}, /*index=5...) while((s32[]{:T(128)}, f32[8,16,16896]{2,1,0:T(8,128)}, ...), condition=%wide.region_1.0_spmd.clone, body=%wide.region_0.0_spmd.clone.sunk | while | flops 1664901120 | bytes 12736687 | solution.py:88
  34.0 1.7 reshape.73
  37.9 4.8 fusion.28
  43.5 1.1 constant_dynamic-update-slice_fusion.2
  44.8 1.7 reshape.73
  48.8 4.8 fusion.28
  55.6 1.7 reshape.73
  59.5 4.8 fusion.28
  66.4 1.7 reshape.73
  70.3 4.8 fusion.28
  77.2 1.7 reshape.73
  81.1 4.8 fusion.28
  88.0 1.7 reshape.73
  91.9 4.8 fusion.28
  98.7 1.7 reshape.73
  102.7 4.8 fusion.28
  109.5 1.7 reshape.73
  113.4 4.8 fusion.28
  121.7 5.3 %psum.35 = f32[8,33]{1,0:T(8,128)S(1)} all-reduce(f32[8,33]{1,0:T(8,128)S(1)} %fusion.7), channel_id=1, replica_groups=mesh['row_0'=2,'row_1'=8,'row_2'=2,'feat_0'=4,'feat_1'=2] {'row_0'}, use_global_device_ids=true, to_apply=%region_5.6 | all-reduce | flops 264 | bytes 2112 | tf_op jit(solution)/shard_map/psum | solution.py:22
  127.0 16.1 %psum.36 = f32[8,33]{1,0:T(8,128)S(1)} all-reduce(f32[8,33]{1,0:T(8,128)S(1)} %psum.35), channel_id=1, replica_groups=mesh['row_0'=2,'row_1'=8,'row_2'=2,'feat_0'=4,'feat_1'=2] {'row_1'}, use_global_device_ids=true, to_apply=%region_6.7 | all-reduce | flops 264 | bytes 2112 | tf_op jit(solution)/shard_map/psum | solution.py:22
  143.1 13.4 %psum.37 = f32[8,33]{1,0:T(8,128)S(1)} all-reduce(f32[8,33]{1,0:T(8,128)S(1)} %psum.36), channel_id=1, replica_groups=mesh['row_0'=2,'row_1'=8,'row_2'=2,'feat_0'=4,'feat_1'=2] {'row_2'}, use_global_device_ids=true, to_apply=%region_7.8 | all-reduce | flops 264 | bytes 2112 | tf_op jit(solution)/shard_map/psum | solution.py:22
  156.5 6.6 %psum.38 = f32[8,33]{1,0:T(8,128)S(1)} all-reduce(f32[8,33]{1,0:T(8,128)S(1)} %psum.37), channel_id=1, replica_groups=mesh['row_0'=2,'row_1'=8,'row_2'=2,'feat_0'=4,'feat_1'=2] {'feat_0'}, use_global_device_ids=true, to_apply=%region_8.9 | all-reduce | flops 264 | bytes 2112 | tf_op jit(solution)/shard_map/psum | solution.py:22
  163.1 5.8 %psum.39 = f32[8,33]{1,0:T(8,128)S(1)} all-reduce(f32[8,33]{1,0:T(8,128)S(1)} %psum.38), channel_id=1, replica_groups=mesh['row_0'=2,'row_1'=8,'row_2'=2,'feat_0'=4,'feat_1'=2] {'feat_1'}, use_global_device_ids=true, to_apply=%region_9.10 | all-reduce | flops 264 | bytes 2112 | tf_op jit(solution)/shard_map/psum | solution.py:22
  170.6 248.7 %all-reduce.3.cloned.1.call-done = f32[128,16896]{1,0:T(8,128)} async-done(((f32[128,16896]{1,0:T(8,128)}), f32[128,16896]{1,0:T(8,128)}) %all-reduce.3.cloned.1.call-update) | async-done | bytes 8650768
  420.4 1.2 reshape.66
  421.6 25.9 %fusion.22 = f32[4,64,8,33]{3,2,1,0:T(8,128)S(1)} fusion(f32[4,64,8,33]{3,2,1,0:T(8,128)S(1)} %reshape.66), kind=kOutput, calls=%fused_computation.38 | output fusion | flops 4257792 | bytes 540672 | tf_op jit(solution)/shard_map/jit(cumsum)/reduce_window_sum | solution.py:55
  448.7 5.3 %pmax.35 = f32[8]{0:T(128)S(1)} all-reduce(f32[8]{0:T(128)S(1)} %get-tuple-element.58), channel_id=1, replica_groups=mesh['row_0'=2,'row_1'=8,'row_2'=2,'feat_0'=4,'feat_1'=2] {'row_0'}, use_global_device_ids=true, to_apply=%region_13.14 | all-reduce | flops 8 | bytes 64 | tf_op jit(solution)/shard_map/pmax | solution.py:38
  454.0 14.2 %pmax.36 = f32[8]{0:T(128)S(1)} all-reduce(f32[8]{0:T(128)S(1)} %pmax.35), channel_id=1, replica_groups=mesh['row_0'=2,'row_1'=8,'row_2'=2,'feat_0'=4,'feat_1'=2] {'row_1'}, use_global_device_ids=true, to_apply=%region_14.15 | all-reduce | flops 8 | bytes 64 | tf_op jit(solution)/shard_map/pmax | solution.py:38
  468.2 4.1 pmax.37
  472.3 8.4 %pmax.38 = f32[8]{0:T(128)S(1)} all-reduce(f32[8]{0:T(128)S(1)} %pmax.37), channel_id=1, replica_groups=mesh['row_0'=2,'row_1'=8,'row_2'=2,'feat_0'=4,'feat_1'=2] {'feat_0'}, use_global_device_ids=true, to_apply=%region_16.17 | all-reduce | flops 8 | bytes 64 | tf_op jit(solution)/shard_map/pmax | solution.py:38
  481.4 4.3 pmax.39
  (71 shorter events, 35.0 us)
Async XLA Ops:
  7.2 412.1 %all-reduce.3.cloned.1.call-start = ((), (), s32[]{:S(2)}) async-start(), calls=%async_computation | async-start | bytes 17301504
  120.1 0.7 copy-start.1
  120.1 1.5 copy-start
  120.1 49.2 %copy-start.2 = (u32[256]{0:T(256)S(1)}, u32[256]{0:T(256)}, u32[]{:S(2)}) copy-start(u32[256]{0:T(256)} %constant.46) | copy-start | bytes 3076
Sparse Core Ops, SparseCore 0:
  120.3 298.9 all-reduce.2
where the time goes:
time: 496 us; the launch traced here: 493 us
  waiting for transfers between devices  249 us (50%)
  blocking collectives  108 us (22%)
  local copies, waits for them, and re-layouts  47.1 us (9%)
  matrix products  38.9 us (8%)
  other arithmetic  29.7 us (6%)
  between operations  14.8 us (3%)
  loops' own time  5.37 us (1%)
    unnamed x2, waiting for transfers between devices  249 us
    psum x5, blocking collectives, by_axis(): return functools.reduce(lax.psum, axes, x)  47.2 us
    dot_general x8, matrix products, histogram_block(): jnp.einsum('fbr,mr->fbm', onehot, masked, preferred_element_type=jnp.floa...  38.8 us
    pmax x5, blocking collectives, one_axis_at_a_time(): x = lax.pmax(x, axis)  36.3 us
    another operation x1, other arithmetic, score_splits(): left_sums = jnp.cumsum(histogram, axis=1)  25.9 us
    all_gather x1, blocking collectives, gather_turned(): lax.all_gather(both, axis, axis=0, tiled=True)  24.4 us
    mul x8, local copies, waits for them, and re-layouts, masked_rows(): picked[:, None, :] * stacked[None, :, :]  13.8 us
  transfers between devices with their start and end apart: 1, of which 1 were waited for; matrix products, arithmetic and copies ran while one was open for 0% of the time, Pallas kernels for 0%

commit v1 on v0

v1 whole, which is shorter than its diff:
```python
import jax
import jax.numpy as jnp
from jax import lax
from jax.experimental import pallas as pl
from jax.experimental.pallas import tpu as pltpu
from jax.sharding import Mesh
from jax.sharding import PartitionSpec as P

BINS = 64
NODES = 8
OUTPUTS = 32
OWNED = 4
LANES = OWNED * BINS
GRAD_ROWS = NODES * OUTPUTS
SUM_ROWS = GRAD_ROWS + NODES
WIRE_ROWS = GRAD_ROWS + 4 * NODES
STEPS = 8.0
TOP = 32000.0
HESS_UNIT = 512.0
HESS_SPLIT = 4096.0
ROW = ("xh", "z", "c")
FEAT = ("y", "xl")
ALL = ROW + FEAT
NEAR = ("xh", "c", "y", "xl")
f32 = jnp.float32
bf16 = jnp.bfloat16

ridge_term = 1.0


def hist_kernel(place, pay, b00, b01, b10, b11, out, masked):
    row_shards = (b00, b01, b10, b11)
    shard_rows = b00.shape[-1]
    columns = pay.shape[0] // 4
    blocks = shard_rows // columns // 128

    @pl.when(pl.program_id(0) == 0)
    def _():
        node_of_row = lax.broadcasted_iota(jnp.int32, (16, 128), 0).astype(f32).astype(bf16)
        for r in range(4):
            group = (place[0] ^ (r // 2)) * 2 + (place[1] ^ (r % 2))

            def fill(s, carry, r=r, group=group):
                shard = group * columns + s
                for i in range(blocks):
                    at = pl.multiple_of(r * shard_rows + s * (blocks * 128) + i * 128, 128)
                    grad = pay[shard, OUTPUTS * i : OUTPUTS * (i + 1), :]
                    first = OUTPUTS * blocks
                    hess = jnp.broadcast_to(pay[shard, first + i : first + i + 1, :], (16, 128))
                    first = first + blocks
                    node = pay[shard, first + i : first + i + 1, :]
                    wide = jnp.broadcast_to(node, (OUTPUTS, 128))
                    for n in range(NODES):
                        masked[OUTPUTS * n : OUTPUTS * (n + 1), pl.ds(at, 128)] = jnp.where(
                            wide == jnp.array(n, bf16), grad, jnp.zeros_like(grad)
                        )
                    masked[GRAD_ROWS : GRAD_ROWS + 16, pl.ds(at, 128)] = jnp.where(
                        jnp.broadcast_to(node, (16, 128)) == node_of_row,
                        hess,
                        jnp.zeros_like(hess),
                    )
                return carry

            lax.fori_loop(0, columns, fill, 0)

    level = lax.broadcasted_iota(jnp.int32, (BINS, shard_rows), 0).astype(f32).astype(bf16)
    sections = []
    for ref in row_shards:
        parts = [
            jnp.where(
                jnp.broadcast_to(ref[0, f : f + 1, :], (BINS, shard_rows)) <= level,
                jnp.array(1, bf16),
                jnp.array(0, bf16),
            )
            for f in range(OWNED)
        ]
        sections.append(jnp.concatenate(parts, axis=0))
    upto = jnp.concatenate(sections, axis=1)
    sums = lax.dot_general(
        masked[0:SUM_ROWS, :], upto, (((1,), (1,)), ((), ())), preferred_element_type=f32
    )
    grads = sums[0:GRAD_ROWS].reshape(NODES, OUTPUTS, LANES)
    largest = jnp.max(jnp.abs(grads), axis=1)
    octave = jnp.ceil(jnp.log2(jnp.maximum(largest, 1e-30)) * STEPS + 0.01)
    factor = TOP * jnp.exp2(octave * (-1.0 / STEPS))
    scaled = jnp.floor(grads * factor[:, None, :] + 0.5).reshape(GRAD_ROWS, LANES)
    out[0, 0:GRAD_ROWS, :] = scaled.astype(jnp.int32).astype(jnp.int16)
    units = sums[GRAD_ROWS:SUM_ROWS] * HESS_UNIT
    high = jnp.floor(units * (1.0 / HESS_SPLIT))
    low = units - high * HESS_SPLIT
    rest = jnp.concatenate([octave, high, low, jnp.zeros_like(low)], axis=0)
    out[0, GRAD_ROWS:WIRE_ROWS, :] = rest.astype(jnp.int32).astype(jnp.int16)


def local_sums(place, pay, pieces):
    blocks, owned, shard_rows = pieces[0].shape
    bins_spec = pl.BlockSpec((1, owned, shard_rows), lambda j, place: (j, 0, 0))
    return pl.pallas_call(
        hist_kernel,
        out_shape=jax.ShapeDtypeStruct((blocks, WIRE_ROWS, LANES), jnp.int16),
        grid_spec=pltpu.PrefetchScalarGridSpec(
            num_scalar_prefetch=1,
            grid=(blocks,),
            in_specs=[pl.BlockSpec(pay.shape, lambda j, place: (0, 0, 0))] + [bins_spec] * 4,
            out_specs=pl.BlockSpec((1, WIRE_ROWS, LANES), lambda j, place: (j, 0, 0)),
            scratch_shapes=[pltpu.VMEM((GRAD_ROWS + 16, 4 * shard_rows), bf16)],
        ),
        compiler_params=pltpu.CompilerParams(vmem_limit_bytes=56 << 20),
        name="left_sums",
    )(place, pay, *pieces)


def score_kernel(devices, parts, gain_out, best_out):
    left = jnp.zeros((NODES, OUTPUTS, LANES), f32)
    left_hess = jnp.zeros((NODES, LANES), f32)
    for s in range(parts.shape[0]):
        scaled = parts[s, 0:GRAD_ROWS, :].astype(jnp.int32).astype(f32)
        rest = parts[s, GRAD_ROWS:WIRE_ROWS, :].astype(jnp.int32).astype(f32)
        unit = jnp.exp2(rest[0:NODES] * (1.0 / STEPS)) * (1.0 / TOP)
        left = left + scaled.reshape(NODES, OUTPUTS, LANES) * unit[:, None, :]
        left_hess = left_hess + (
            rest[NODES : 2 * NODES] * HESS_SPLIT + rest[2 * NODES : 3 * NODES]
        ) * (1.0 / HESS_UNIT)
    whole = left[:, :, LANES - 1 :]
    whole_hess = left_hess[:, LANES - 1 :]
    right = whole - left
    right_hess = whole_hess - left_hess

    def part_score(sums, hess):
        return jnp.sum(sums * sums, axis=1) / (hess + ridge_term)

    terms = part_score(left, left_hess) + part_score(right, right_hess)
    gain = (0.5 / OUTPUTS) * (terms - part_score(whole, whole_hess))
    for f in range(OWNED):
        for n in range(NODES):
            gain_out[f : f + 1, n * BINS : (n + 1) * BINS] = gain[
                n : n + 1, f * BINS : (f + 1) * BINS
            ]
    best = jnp.max(gain, axis=1, keepdims=True)
    sublane = lax.broadcasted_iota(jnp.int32, (NODES, 128), 0)
    lane = lax.broadcasted_iota(jnp.int32, (NODES, 128), 1)
    turned = jnp.max(jnp.where(sublane == lane, best, -jnp.inf), axis=0, keepdims=True)
    best_out[...] = jnp.broadcast_to(turned[:, 0:NODES], (devices, NODES))


def final_scores(parts, devices):
    return pl.pallas_call(
        lambda *refs: score_kernel(devices, *refs),
        out_shape=(
            jax.ShapeDtypeStruct((OWNED, NODES * BINS), f32),
            jax.ShapeDtypeStruct((devices, NODES), f32),
        ),
        compiler_params=pltpu.CompilerParams(vmem_limit_bytes=48 << 20),
        name="split_scores",
    )(parts)


def on_device(bin_index, gradient, hessian, row_node):
    xh, c = lax.axis_index("xh"), lax.axis_index("c")
    shard_rows = bin_index.shape[1]
    depth = lax.axis_size("z")
    table = bin_index.reshape(2, depth, 2, OWNED, shard_rows)
    pieces = []
    for r in range(4):
        piece = lax.dynamic_index_in_dim(table, xh ^ (r // 2), 0, keepdims=False)
        piece = lax.dynamic_index_in_dim(piece, c ^ (r % 2), 1, keepdims=False)
        pieces.append(piece.astype(bf16))
    pieces[1] = lax.ppermute(pieces[1], "c", [(0, 1), (1, 0)])
    pieces[2] = lax.ppermute(pieces[2], "xh", [(0, 1), (1, 0)])
    pieces[3] = lax.ppermute(pieces[3], ("xh", "c"), [(0, 3), (1, 2), (2, 1), (3, 0)])

    own_rows = gradient.shape[1]
    blocks = own_rows // 128
    nodes = lax.dynamic_slice_in_dim(row_node, lax.axis_index(FEAT) * own_rows, own_rows, 0)
    pay = jnp.concatenate(
        [gradient[:, 128 * i : 128 * (i + 1)] for i in range(blocks)]
        + [hessian.reshape(blocks, 128), nodes.astype(bf16).reshape(blocks, 128)],
        axis=0,
    )
    pay = jnp.pad(pay, ((0, -pay.shape[0] % 8), (0, 0)))
    near = lax.axis_size(NEAR)
    pay = lax.all_to_all(jnp.broadcast_to(pay[None], (near,) + pay.shape), NEAR, 0, 0, tiled=True)

    place = jnp.stack([xh, c]).astype(jnp.int32)
    sums = local_sums(place, pay, pieces)
    parts = lax.all_to_all(sums, "z", 0, 0, tiled=True)
    gain, best = final_scores(parts, lax.axis_size(ALL))
    best = lax.all_to_all(best, ALL, 0, 0, tiled=True)
    return gain, jnp.max(best, axis=0)


def solution(mesh):
    split = Mesh(mesh.devices.reshape(2, 8, 2, 4, 2), ALL)
    in_specs = (P(FEAT, ROW), P(None, ROW + FEAT), P(ROW + FEAT), P(ROW))
    out_specs = (P(FEAT + ROW, None), P())
    return jax.shard_map(
        on_device, mesh=split, in_specs=in_specs, out_specs=out_specs, check_vma=False
    )
```

time: 496 us -> 117 us (0.24)
  waiting for transfers between devices: 249 us -> 14.5 us
  blocking collectives: 108 us -> 58.7 us
  local copies, waits for them, and re-layouts: 47.1 us -> 5.29 us
  matrix products: 38.9 us -> 0 us
  other arithmetic: 29.7 us -> 3.1 us
  Pallas kernels: 0 us -> 21.8 us
  between operations: 14.8 us -> 0.7 us
  starting transfers between devices: 0.04 us -> 12.2 us
  loops' own time: 5.37 us -> 0 us
    unnamed x2 -> x0, waiting for transfers between devices: 249 us -> none
    all_to_all x0 -> x2, blocking collectives: none -> 58.7 us  [the longest x1 39.3 us: on_device(): parts = lax.all_to_all(sums, 'z', 0, 0, tiled=True)]
    psum x5 -> x0, blocking collectives: 47.2 us -> none  [by_axis(): return functools.reduce(lax.psum, axes, x)]
    dot_general x9 -> x0, matrix products: 38.9 us -> none  [the longest x8 38.8 us: histogram_block(): jnp.einsum('fbr,mr->fbm', onehot, masked, preferred_element_type=jnp.floa...]
    pmax x5 -> x0, blocking collectives: 36.3 us -> none  [one_axis_at_a_time(): x = lax.pmax(x, axis)]
    another operation x1, other arithmetic: 25.9 us -> 0.55 us  [on_device(): place = jnp.stack([xh, c]).astype(jnp.int32)]
    all_gather x1 -> x0, blocking collectives: 24.4 us -> none  [gather_turned(): lax.all_gather(both, axis, axis=0, tiled=True)]
    pallas_call x0 -> x2, Pallas kernels: none -> 21.8 us  [the longest x1 20.7 us: local_sums(): pl.pallas_call(hist_kernel, out_shape=jax.ShapeDtypeStruct((blocks, WIRE_...]
  transfers between devices with their start and end apart: 1 -> 4, of which waited for: 1 -> 2; matrix products, arithmetic and copies ran while one was open for 0% -> 3% of each run, Pallas kernels for 0% -> 0%
where the time goes in v1:
time: 117 us; the launch traced here: 116 us
  blocking collectives  58.7 us (50%)
  Pallas kernels  21.8 us (19%)
  waiting for transfers between devices  14.5 us (12%)
  starting transfers between devices  12.2 us (10%)
  local copies, waits for them, and re-layouts  5.29 us (5%)
  other arithmetic  3.1 us (3%)
    all_to_all x1, blocking collectives, on_device(): parts = lax.all_to_all(sums, 'z', 0, 0, tiled=True)  39.3 us
    pallas_call x1, Pallas kernels, local_sums(): pl.pallas_call(hist_kernel, out_shape=jax.ShapeDtypeStruct((blocks, WIRE_...  20.7 us
    all_to_all x1, blocking collectives, on_device(): best = lax.all_to_all(best, ALL, 0, 0, tiled=True)  19.4 us
    ppermute x1, waiting for transfers between devices, on_device(): pieces[2] = lax.ppermute(pieces[2], 'xh', [(0, 1), (1, 0)])  10.1 us
    all_to_all x1, starting transfers between devices, on_device(): lax.all_to_all(jnp.broadcast_to(pay[None], (near,) + pay.shape), NEAR, 0,...  8.59 us
    ppermute x1, waiting for transfers between devices, on_device(): lax.ppermute(pieces[3], ('xh', 'c'), [(0, 3), (1, 2), (2, 1), (3, 0)])  4.37 us
    ppermute x1, starting transfers between devices, on_device(): pieces[2] = lax.ppermute(pieces[2], 'xh', [(0, 1), (1, 0)])  3.02 us
  transfers between devices with their start and end apart: 4, of which 2 were waited for; matrix products, arithmetic and copies ran while one was open for 3% of the time, Pallas kernels for 0%

profile of v1, /device:TPU:1, one launch (start us, length us, event | category | flops | bytes accessed | tf_op | source)
XLA Modules:
  0.0 116.4 jit_solution(2126414388657653553)
XLA Ops:
  0.6 0.7 fusion.5
  1.4 0.8 fusion.4
  2.1 0.7 concatenate.3
  2.9 1.0 broadcast_in_dim.2
  3.9 8.6 %all-to-all-start = ((bf16[32,104,128]{2,1,0:T(8,128)(2,1)}), bf16[32,104,128]{2,1,0:T(8,128)(2,1)S(1)}, u32[]{:S(2)}, u32[]{:S(2)}) async-start(bf16[32,104,128]{2,1,0:T(8,128)(2,1)} %broadcast_in_dim.2), calls=%async_computation | async-start | bytes 1703936 | tf_op jit(solution)/shard_map/all_to_all | solution.py:182
  12.5 1.8 %reshape.30 = s32[2,8,2,4,3072]{4,3,2,1,0:T(4,128)S(1)} reshape(s32[128,3072]{1,0:T(8,128)} %param.4) | data formatting | bytes 3145728 | tf_op jit(solution)/shard_map/reshape | solution.py:162
  14.3 1.0 fusion.3
  15.3 0.2 collective-permute-start
  15.5 3.0 %collective-permute-start.1 = (bf16[8,4,3072]{2,1,0:T(4,128)(2,1)S(1)}, bf16[8,4,3072]{2,1,0:T(4,128)(2,1)S(1)}, u32[]{:S(2)}, u32[]{:S(2)}) collective-permute-start(bf16[8,4,3072]{2,1,0:T(4,128)(2,1)S(1)} %get-tuple-element.7), channel_id=1, source_target_pairs={{0,128},{128,0},{1,129},{129,1},{2,130},{130,2},{3,131},{131,3},{4... | collective-permute-start | bytes 589832 | tf_op jit(solution)/shard_map/ppermute | solution.py:169
  18.6 0.4 collective-permute-start.2
  19.0 0.6 pad_add_fusion.place
  19.5 0.0 collective-permute-done.b01
  19.5 0.0 copy-start.1
  19.5 10.1 %collective-permute-done.1.b10 = bf16[8,4,3072]{2,1,0:T(4,128)(2,1)S(1)} collective-permute-done((bf16[8,4,3072]{2,1,0:T(4,128)(2,1)S(1)}, bf16[8,4,3072]{2,1,0:T(4,128)(2,1)S(1)}, u32[]{:S(2)}, u32[]{:S(2)}) %collective-permute-start.1) | collective-permute-done | bytes 196640 | tf_op jit(solution)/shard_map/ppermute | solution.py:169
  29.7 0.0 copy-start.2
  29.7 4.4 %collective-permute-done.2.b11 = bf16[8,4,3072]{2,1,0:T(4,128)(2,1)S(1)} collective-permute-done((bf16[8,4,3072]{2,1,0:T(4,128)(2,1)S(1)}, bf16[8,4,3072]{2,1,0:T(4,128)(2,1)S(1)}, u32[]{:S(2)}, u32[]{:S(2)}) %collective-permute-start.2) | collective-permute-done | bytes 196640 | tf_op jit(solution)/shard_map/ppermute | solution.py:170
  34.0 0.0 copy-start.3
  34.0 0.0 all-to-all-done.pay
  34.0 0.0 copy-start
  34.0 0.0 copy-done.1
  34.0 0.0 copy-done.2
  34.1 0.7 copy-done.3
  34.7 0.3 copy-done
  35.1 20.7 %left_sums.1 = s16[8,288,256]{2,1,0:T(8,128)(2,1)} custom-call(s32[2]{0:T(128)} %pad_add_fusion.place, bf16[32,104,128]{2,1,0:T(8,128)(2,1)} %copy-done, bf16[8,4,3072]{2,1,0:T(4,128)(2,1)} %get-tuple-element.9.b00, bf16[8,4,3072]{2,1,0:T(4,128)(2,1)} %copy-done.1, bf16[8,4,3072]{2,1,0:T(4,128)(2,1)} %copy-done.2, bf16[8,4,3072]{2,1,0:T(4,128)(2,1)} %copy-done.3), custom_call_target="tpu_custom_call" | custom-call | tf_op jit(solution)/shard_map/left_sums/pallas_call | solution.py:98
  55.8 39.3 %all_to_all.19.refs_0_ = s16[8,288,256]{2,1,0:T(8,128)(2,1)S(1)} all-to-all(s16[8,288,256]{2,1,0:T(8,128)(2,1)} %left_sums.1), channel_id=1, replica_groups=mesh['xh'=2,'z'=8,'c'=2,'y'=4,'xl'=2] {'z'}, dimensions={0} | all-to-all | bytes 2359296 | tf_op jit(solution)/shard_map/all_to_all | solution.py:186
  95.1 1.1 split_scores.1
  96.2 19.4 %all_to_all.20 = f32[256,1,8]{2,1,0:T(1,128)S(1)} all-to-all(f32[256,1,8]{2,1,0:T(1,128)S(1)} %bitcast.32), channel_id=1, replica_groups=mesh['xh'=2,'z'=8,'c'=2,'y'=4,'xl'=2] {'xh','z','c','y','xl'}, dimensions={0} | all-to-all | bytes 16384 | tf_op jit(solution)/shard_map/all_to_all | solution.py:188
  115.6 0.8 reduce_max.9
  (1 shorter events, 0.0 us)
Async XLA Ops:
  3.9 30.1 %all-to-all-start = ((bf16[32,104,128]{2,1,0:T(8,128)(2,1)}), bf16[32,104,128]{2,1,0:T(8,128)(2,1)S(1)}, u32[]{:S(2)}, u32[]{:S(2)}) async-start(bf16[32,104,128]{2,1,0:T(8,128)(2,1)} %broadcast_in_dim.2), calls=%async_computation | async-start | bytes 1703936 | tf_op jit(solution)/shard_map/all_to_all | solution.py:182
  15.3 4.2 %collective-permute-start = (bf16[8,4,3072]{2,1,0:T(4,128)(2,1)S(1)}, bf16[8,4,3072]{2,1,0:T(4,128)(2,1)S(1)}, u32[]{:S(2)}, u32[]{:S(2)}) collective-permute-start(bf16[8,4,3072]{2,1,0:T(4,128)(2,1)S(1)} %get-tuple-element.8), channel_id=1, source_target_pairs={{0,8},{8,0},{1,9},{9,1},{2,10},{10,2},{3,11},{11,3},{4,12},{12,4},... | collective-permute-start | bytes 589832 | tf_op jit(solution)/shard_map/ppermute | solution.py:168
  15.5 14.1 %collective-permute-start.1 = (bf16[8,4,3072]{2,1,0:T(4,128)(2,1)S(1)}, bf16[8,4,3072]{2,1,0:T(4,128)(2,1)S(1)}, u32[]{:S(2)}, u32[]{:S(2)}) collective-permute-start(bf16[8,4,3072]{2,1,0:T(4,128)(2,1)S(1)} %get-tuple-element.7), channel_id=1, source_target_pairs={{0,128},{128,0},{1,129},{129,1},{2,130},{130,2},{3,131},{131,3},{4... | collective-permute-start | bytes 589832 | tf_op jit(solution)/shard_map/ppermute | solution.py:169
  18.6 15.5 %collective-permute-start.2 = (bf16[8,4,3072]{2,1,0:T(4,128)(2,1)S(1)}, bf16[8,4,3072]{2,1,0:T(4,128)(2,1)S(1)}, u32[]{:S(2)}, u32[]{:S(2)}) collective-permute-start(bf16[8,4,3072]{2,1,0:T(4,128)(2,1)S(1)} %get-tuple-element.6), channel_id=1, source_target_pairs={{0,136},{8,128},{128,8},{136,0},{1,137},{9,129},{129,9},{137,1},{2... | collective-permute-start | bytes 589832 | tf_op jit(solution)/shard_map/ppermute | solution.py:170
  19.5 14.5 %copy-start.1 = (bf16[8,4,3072]{2,1,0:T(4,128)(2,1)}, bf16[8,4,3072]{2,1,0:T(4,128)(2,1)S(1)}, u32[]{:S(2)}) copy-start(bf16[8,4,3072]{2,1,0:T(4,128)(2,1)S(1)} %collective-permute-done.b01) | copy-start | bytes 589828
  29.7 4.4 %copy-start.2 = (bf16[8,4,3072]{2,1,0:T(4,128)(2,1)}, bf16[8,4,3072]{2,1,0:T(4,128)(2,1)S(1)}, u32[]{:S(2)}) copy-start(bf16[8,4,3072]{2,1,0:T(4,128)(2,1)S(1)} %collective-permute-done.1.b10) | copy-start | bytes 589828
  34.0 0.7 copy-start.3
  34.0 1.0 copy-start

commit v2 on v1

--- a/solution.py
+++ b/solution.py
@@ -18,29 +18,98 @@
 TOP = 32000.0
 HESS_UNIT = 512.0
 HESS_SPLIT = 4096.0
-ROW = ("xh", "z", "c")
+ROW = ("xh", "zh", "zl", "c")
 FEAT = ("y", "xl")
 ALL = ROW + FEAT
-NEAR = ("xh", "c", "y", "xl")
+NEAR = ("xh", "zl", "y", "xl")
 f32 = jnp.float32
 bf16 = jnp.bfloat16
 
 ridge_term = 1.0
 
 
-def hist_kernel(place, pay, b00, b01, b10, b11, out, masked):
-    row_shards = (b00, b01, b10, b11)
-    shard_rows = b00.shape[-1]
-    columns = pay.shape[0] // 4
+def prep_kernel(place, bins, grad, hess, nodes, own, other, pay):
+    c, column = place[2], place[3]
+    blocks = grad.shape[1] // 128
+    for t in range(bins.shape[0] // (2 * OWNED)):
+        both = bins[t * 2 * OWNED : (t + 1) * 2 * OWNED, :].astype(f32)
+        first, second = both[0:OWNED], both[OWNED : 2 * OWNED]
+        own[t] = jnp.where(c == 0, first, second).astype(bf16)
+        other[t] = jnp.where(c == 0, second, first).astype(bf16)
+    node = nodes[0:blocks, :]
+    for s in range(1, nodes.shape[0] // blocks):
+        node = jnp.where(column == s, nodes[s * blocks : (s + 1) * blocks, :], node)
+    rest = jnp.concatenate(
+        [
+            hess[...].astype(f32),
+            node.astype(f32),
+            jnp.zeros((pay.shape[1] - (OUTPUTS + 2) * blocks, 128), f32),
+        ],
+        axis=0,
+    ).astype(bf16)
+    grads = [grad[:, 128 * i : 128 * (i + 1)] for i in range(blocks)]
+
+    def fill(s, carry):
+        for i in range(blocks):
+            pay[s, OUTPUTS * i : OUTPUTS * (i + 1), :] = grads[i]
+        pay[s, OUTPUTS * blocks :, :] = rest
+        return carry
+
+    lax.fori_loop(0, pay.shape[0], fill, 0)
+
+
+def prepare(place, bin_index, gradient, hessian, row_node, near):
+    features, shard_rows = bin_index.shape
+    blocks = gradient.shape[1] // 128
+    groups = features // (2 * OWNED)
+    pay_rows = OUTPUTS * blocks + -(-2 * blocks // 8) * 8
+    return pl.pallas_call(
+        prep_kernel,
+        out_shape=(
+            jax.ShapeDtypeStruct((groups, OWNED, shard_rows), bf16),
+            jax.ShapeDtypeStruct((groups, OWNED, shard_rows), bf16),
+            jax.ShapeDtypeStruct((near, pay_rows, 128), bf16),
+        ),
+        grid_spec=pltpu.PrefetchScalarGridSpec(num_scalar_prefetch=1),
+        compiler_params=pltpu.CompilerParams(vmem_limit_bytes=32 << 20),
+        name="prepare",
+    )(place, bin_index, gradient, hessian.reshape(blocks, 128), row_node.reshape(-1, 128))
+
+
+def sort_kernel(place, own, other, p0, p1, p2, p3):
+    xh, zl = place[0], place[1]
+    for r, out in enumerate((p0, p1, p2, p3)):
+        for j in range(out.shape[1]):
+            t = ((xh ^ (r // 2)) * out.shape[1] + j) * 2 + (zl ^ (r % 2))
+            out[0, j] = own[t]
+            out[1, j] = other[t]
+
+
+def sort_by_neighbour(place, own, other):
+    groups, owned, shard_rows = own.shape
+    shape = jax.ShapeDtypeStruct((2, groups // 4, owned, shard_rows), bf16)
+    return pl.pallas_call(
+        sort_kernel,
+        out_shape=(shape,) * 4,
+        grid_spec=pltpu.PrefetchScalarGridSpec(num_scalar_prefetch=1),
+        compiler_params=pltpu.CompilerParams(vmem_limit_bytes=32 << 20),
+        name="sort_bins",
+    )(place, own, other)
+
+
+def hist_kernel(place, pay0, pay1, b0, b1, b2, b3, out, masked):
+    shard_rows = b0.shape[-1]
+    columns = pay0.shape[0] // 4
     blocks = shard_rows // columns // 128
 
     @pl.when(pl.program_id(0) == 0)
     def _():
         node_of_row = lax.broadcasted_iota(jnp.int32, (16, 128), 0).astype(f32).astype(bf16)
-        for r in range(4):
-            group = (place[0] ^ (r // 2)) * 2 + (place[1] ^ (r % 2))
-
-            def fill(s, carry, r=r, group=group):
+        for r in range(8):
+            group = (place[0] ^ (r // 4)) * 2 + (place[1] ^ (r // 2 % 2))
+            pay = (pay0, pay1)[r % 2]
+
+            def fill(s, carry, r=r, group=group, pay=pay):
                 shard = group * columns + s
                 for i in range(blocks):
                     at = pl.multiple_of(r * shard_rows + s * (blocks * 128) + i * 128, 128)
@@ -65,16 +134,17 @@
 
     level = lax.broadcasted_iota(jnp.int32, (BINS, shard_rows), 0).astype(f32).astype(bf16)
     sections = []
-    for ref in row_shards:
-        parts = [
-            jnp.where(
-                jnp.broadcast_to(ref[0, f : f + 1, :], (BINS, shard_rows)) <= level,
-                jnp.array(1, bf16),
-                jnp.array(0, bf16),
-            )
-            for f in range(OWNED)
-        ]
-        sections.append(jnp.concatenate(parts, axis=0))
+    for ref in (b0, b1, b2, b3):
+        for half in range(2):
+            parts = [
+                jnp.where(
+                    jnp.broadcast_to(ref[half, 0, f : f + 1, :], (BINS, shard_rows)) <= level,
+                    jnp.array(1, bf16),
+                    jnp.array(0, bf16),
+                )
+                for f in range(OWNED)
+            ]
+            sections.append(jnp.concatenate(parts, axis=0))
     upto = jnp.concatenate(sections, axis=1)
     sums = lax.dot_general(
         masked[0:SUM_ROWS, :], upto, (((1,), (1,)), ((), ())), preferred_element_type=f32
@@ -92,22 +162,23 @@
     out[0, GRAD_ROWS:WIRE_ROWS, :] = rest.astype(jnp.int32).astype(jnp.int16)
 
 
-def local_sums(place, pay, pieces):
-    blocks, owned, shard_rows = pieces[0].shape
-    bins_spec = pl.BlockSpec((1, owned, shard_rows), lambda j, place: (j, 0, 0))
+def local_sums(place, pay0, pay1, pieces):
+    halves, blocks, owned, shard_rows = pieces[0].shape
+    bins_spec = pl.BlockSpec((halves, 1, owned, shard_rows), lambda j, place: (0, j, 0, 0))
+    pay_spec = pl.BlockSpec(pay0.shape, lambda j, place: (0, 0, 0))
     return pl.pallas_call(
         hist_kernel,
         out_shape=jax.ShapeDtypeStruct((blocks, WIRE_ROWS, LANES), jnp.int16),
         grid_spec=pltpu.PrefetchScalarGridSpec(
             num_scalar_prefetch=1,
             grid=(blocks,),
-            in_specs=[pl.BlockSpec(pay.shape, lambda j, place: (0, 0, 0))] + [bins_spec] * 4,
+            in_specs=[pay_spec] * 2 + [bins_spec] * 4,
             out_specs=pl.BlockSpec((1, WIRE_ROWS, LANES), lambda j, place: (j, 0, 0)),
-            scratch_shapes=[pltpu.VMEM((GRAD_ROWS + 16, 4 * shard_rows), bf16)],
+            scratch_shapes=[pltpu.VMEM((GRAD_ROWS + 16, 8 * shard_rows), bf16)],
         ),
         compiler_params=pltpu.CompilerParams(vmem_limit_bytes=56 << 20),
         name="left_sums",
-    )(place, pay, *pieces)
+    )(place, pay0, pay1, *pieces)
 
 
 def score_kernel(devices, parts, gain_out, best_out):
@@ -156,41 +227,26 @@
 
 
 def on_device(bin_index, gradient, hessian, row_node):
-    xh, c = lax.axis_index("xh"), lax.axis_index("c")
-    shard_rows = bin_index.shape[1]
-    depth = lax.axis_size("z")
-    table = bin_index.reshape(2, depth, 2, OWNED, shard_rows)
-    pieces = []
-    for r in range(4):
-        piece = lax.dynamic_index_in_dim(table, xh ^ (r // 2), 0, keepdims=False)
-        piece = lax.dynamic_index_in_dim(piece, c ^ (r % 2), 1, keepdims=False)
-        pieces.append(piece.astype(bf16))
-    pieces[1] = lax.ppermute(pieces[1], "c", [(0, 1), (1, 0)])
-    pieces[2] = lax.ppermute(pieces[2], "xh", [(0, 1), (1, 0)])
-    pieces[3] = lax.ppermute(pieces[3], ("xh", "c"), [(0, 3), (1, 2), (2, 1), (3, 0)])
-
-    own_rows = gradient.shape[1]
-    blocks = own_rows // 128
-    nodes = lax.dynamic_slice_in_dim(row_node, lax.axis_index(FEAT) * own_rows, own_rows, 0)
-    pay = jnp.concatenate(
-        [gradient[:, 128 * i : 128 * (i + 1)] for i in range(blocks)]
-        + [hessian.reshape(blocks, 128), nodes.astype(bf16).reshape(blocks, 128)],
-        axis=0,
-    )
-    pay = jnp.pad(pay, ((0, -pay.shape[0] % 8), (0, 0)))
-    near = lax.axis_size(NEAR)
-    pay = lax.all_to_all(jnp.broadcast_to(pay[None], (near,) + pay.shape), NEAR, 0, 0, tiled=True)
-
-    place = jnp.stack([xh, c]).astype(jnp.int32)
-    sums = local_sums(place, pay, pieces)
-    parts = lax.all_to_all(sums, "z", 0, 0, tiled=True)
+    place = jnp.stack([lax.axis_index("xh"), lax.axis_index("zl"), lax.axis_index("c"), lax.axis_index(FEAT)])
+    swap = [(0, 1), (1, 0)]
+    own, other, pay = prepare(place, bin_index, gradient, hessian, row_node, lax.axis_size(NEAR))
+    other = lax.ppermute(other, "c", swap)
+    pieces = list(sort_by_neighbour(place, own, other))
+    pay = lax.all_to_all(pay, NEAR, 0, 0, tiled=True)
+    pieces[1] = lax.ppermute(pieces[1], "zl", swap)
+    pieces[2] = lax.ppermute(pieces[2], "xh", swap)
+    pieces[3] = lax.ppermute(pieces[3], ("xh", "zl"), [(0, 3), (1, 2), (2, 1), (3, 0)])
+    pay, pieces = lax.optimization_barrier((pay, pieces))
+    pay_other = lax.ppermute(pay, "c", swap)
+    sums = local_sums(place, pay, pay_other, pieces)
+    parts = lax.all_to_all(sums, "zh", 0, 0, tiled=True)
     gain, best = final_scores(parts, lax.axis_size(ALL))
     best = lax.all_to_all(best, ALL, 0, 0, tiled=True)
     return gain, jnp.max(best, axis=0)
 
 
 def solution(mesh):
-    split = Mesh(mesh.devices.reshape(2, 8, 2, 4, 2), ALL)
+    split = Mesh(mesh.devices.reshape(2, 4, 2, 2, 4, 2), ALL)
     in_specs = (P(FEAT, ROW), P(None, ROW + FEAT), P(ROW + FEAT), P(ROW))
     out_specs = (P(FEAT + ROW, None), P())
     return jax.shard_map(

time: 117 us -> 111 us (0.949)
  blocking collectives: 58.7 us -> 45.1 us
  starting transfers between devices: 12.2 us -> 16.5 us
  Pallas kernels: 21.8 us -> 25.2 us
  other arithmetic: 3.1 us -> 0.87 us
  waiting for transfers between devices: 14.5 us -> 16.5 us
    all_to_all x1, blocking collectives: 39.3 us -> 24 us  [on_device(): parts = lax.all_to_all(sums, 'zh', 0, 0, tiled=True)]
    unnamed x8 -> x22, local copies, waits for them, and re-layouts: 1.01 us -> 5.18 us
    ppermute x3 -> x5, starting transfers between devices: 3.65 us -> 7.23 us  [the longest x1 2.73 us: on_device(): pieces[2] = lax.ppermute(pieces[2], 'xh', swap)]
    pallas_call x0 -> x2, Pallas kernels: none -> 2.47 us  [the longest x1 1.87 us: prepare(): pl.pallas_call(prep_kernel, out_shape=(jax.ShapeDtypeStruct((groups, OWNE...]
    ppermute x3 -> x5, waiting for transfers between devices: 14.5 us -> 16.5 us  [the longest x1 6.52 us: on_device(): pieces[1] = lax.ppermute(pieces[1], 'zl', swap)]
    reshape x1 -> x0, local copies, waits for them, and re-layouts: 1.77 us -> none  [on_device(): table = bin_index.reshape(2, depth, 2, OWNED, shard_rows)]
    all_to_all x1, blocking collectives: 19.4 us -> 21.2 us  [on_device(): best = lax.all_to_all(best, ALL, 0, 0, tiled=True)]
  transfers between devices with their start and end apart: 4 -> 6, of which waited for: 2 -> 5; matrix products, arithmetic and copies ran while one was open for 3% -> 0% of each run, Pallas kernels for 0% -> 1%
where the time goes in v2:
time: 111 us; the launch traced here: 110 us
  blocking collectives  45.1 us (41%)
  Pallas kernels  25.2 us (23%)
  starting transfers between devices  16.5 us (15%)
  waiting for transfers between devices  16.5 us (15%)
  local copies, waits for them, and re-layouts  5.18 us (5%)
    all_to_all x1, blocking collectives, on_device(): parts = lax.all_to_all(sums, 'zh', 0, 0, tiled=True)  24 us
    pallas_call x1, Pallas kernels, local_sums(): pl.pallas_call(hist_kernel, out_shape=jax.ShapeDtypeStruct((blocks, WIRE_...  21.8 us
    all_to_all x1, blocking collectives, on_device(): best = lax.all_to_all(best, ALL, 0, 0, tiled=True)  21.2 us
    all_to_all x1, starting transfers between devices, on_device(): pay = lax.all_to_all(pay, NEAR, 0, 0, tiled=True)  9.22 us
    ppermute x1, waiting for transfers between devices, on_device(): pieces[1] = lax.ppermute(pieces[1], 'zl', swap)  6.52 us
    unnamed x22, local copies, waits for them, and re-layouts  5.18 us
    ppermute x1, waiting for transfers between devices, on_device(): lax.ppermute(pieces[3], ('xh', 'zl'), [(0, 3), (1, 2), (2, 1), (3, 0)])  4.77 us
    ppermute x1, starting transfers between devices, on_device(): pieces[2] = lax.ppermute(pieces[2], 'xh', swap)  2.73 us
  transfers between devices with their start and end apart: 6, of which 5 were waited for; matrix products, arithmetic and copies ran while one was open for 0% of the time, Pallas kernels for 1%

profile of v2, /device:TPU:1, one launch (start us, length us, event | category | flops | bytes accessed | tf_op | source)
XLA Modules:
  0.0 110.1 jit_solution(18048819988015901251)
XLA Ops:
  0.6 0.1 pad_add_fusion.place
  0.7 1.4 %copy-done = s32[128,3072]{1,0:T(8,128)S(1)} copy-done((s32[128,3072]{1,0:T(8,128)S(1)}, s32[128,3072]{1,0:T(8,128)}, u32[]{:S(2)}) %copy-start) | copy-done | bytes 1572888
  2.1 0.7 copy-done.2
  2.9 0.7 copy-done.3
  3.6 0.7 copy-done.5
  4.3 1.9 %prepare.1 = (bf16[16,4,3072]{2,1,0:T(4,128)(2,1)S(1)}, bf16[16,4,3072]{2,1,0:T(4,128)(2,1)S(1)}, bf16[32,104,128]{2,1,0:T(8,128)(2,1)}) custom-call(s32[4]{0:T(128)S(1)} %pad_add_fusion.place, s32[128,3072]{1,0:T(8,128)S(1)} %copy-done, bf16[32,384]{1,0:T(8,128)(2,1)S(1)} %copy-done.2, bf16[3,128]{1,0:T(4,128)(2,1)S(1)} %bitcast.11, s32[24,128]{1,0:T(8,128)S(1)} %bitcast.10), custom_call_target="tpu_custom_call" | custom-call | tf_op jit(solution)/shard_map/prepare/pallas_call | solution.py:66
  6.1 9.2 %all-to-all-start = ((bf16[32,104,128]{2,1,0:T(8,128)(2,1)}), bf16[32,104,128]{2,1,0:T(8,128)(2,1)S(1)}, u32[]{:S(2)}, u32[]{:S(2)}) async-start(bf16[32,104,128]{2,1,0:T(8,128)(2,1)} %get-tuple-element.16), calls=%async_computation | async-start | bytes 1703936 | tf_op jit(solution)/shard_map/all_to_all | solution.py:235
  15.4 1.0 collective-permute-start
  16.4 1.3 %collective-permute-done.other = bf16[16,4,3072]{2,1,0:T(4,128)(2,1)S(1)} collective-permute-done((bf16[16,4,3072]{2,1,0:T(4,128)(2,1)S(1)}, bf16[16,4,3072]{2,1,0:T(4,128)(2,1)S(1)}, u32[]{:S(2)}, u32[]{:S(2)}) %collective-permute-start) | collective-permute-done | bytes 393248 | tf_op jit(solution)/shard_map/ppermute | solution.py:233
  17.7 0.0 copy-done.4
  17.8 0.6 sort_bins.1
  18.4 0.0 copy-start.1
  18.4 0.7 copy-done.1
  19.0 1.5 %collective-permute-start.1 = (bf16[2,4,4,3072]{3,2,1,0:T(4,128)(2,1)S(1)}, bf16[2,4,4,3072]{3,2,1,0:T(4,128)(2,1)S(1)}, u32[]{:S(2)}, u32[]{:S(2)}) collective-permute-start(bf16[2,4,4,3072]{3,2,1,0:T(4,128)(2,1)S(1)} %get-tuple-element.20), channel_id=1, source_target_pairs={{0,16},{16,0},{1,17},{17,1},{2,18},{18,2},{3,19},{19,3},{4,20},{20... | collective-permute-start | bytes 589832 | tf_op jit(solution)/shard_map/ppermute | solution.py:236
  20.5 2.7 %collective-permute-start.2 = (bf16[2,4,4,3072]{3,2,1,0:T(4,128)(2,1)S(1)}, bf16[2,4,4,3072]{3,2,1,0:T(4,128)(2,1)S(1)}, u32[]{:S(2)}, u32[]{:S(2)}) collective-permute-start(bf16[2,4,4,3072]{3,2,1,0:T(4,128)(2,1)S(1)} %get-tuple-element.21), channel_id=1, source_target_pairs={{0,128},{128,0},{1,129},{129,1},{2,130},{130,2},{3,131},{131,3},{4... | collective-permute-start | bytes 589832 | tf_op jit(solution)/shard_map/ppermute | solution.py:237
  23.3 0.0 collective-permute-start.3
  23.3 6.5 %collective-permute-done.1.b1 = bf16[2,4,4,3072]{3,2,1,0:T(4,128)(2,1)S(1)} collective-permute-done((bf16[2,4,4,3072]{3,2,1,0:T(4,128)(2,1)S(1)}, bf16[2,4,4,3072]{3,2,1,0:T(4,128)(2,1)S(1)}, u32[]{:S(2)}, u32[]{:S(2)}) %collective-permute-start.1) | collective-permute-done | bytes 196640 | tf_op jit(solution)/shard_map/ppermute | solution.py:236
  29.8 1.9 %collective-permute-done.2.b2 = bf16[2,4,4,3072]{3,2,1,0:T(4,128)(2,1)S(1)} collective-permute-done((bf16[2,4,4,3072]{3,2,1,0:T(4,128)(2,1)S(1)}, bf16[2,4,4,3072]{3,2,1,0:T(4,128)(2,1)S(1)}, u32[]{:S(2)}, u32[]{:S(2)}) %collective-permute-start.2) | collective-permute-done | bytes 196640 | tf_op jit(solution)/shard_map/ppermute | solution.py:237
  31.7 4.8 %collective-permute-done.3.b3 = bf16[2,4,4,3072]{3,2,1,0:T(4,128)(2,1)S(1)} collective-permute-done((bf16[2,4,4,3072]{3,2,1,0:T(4,128)(2,1)S(1)}, bf16[2,4,4,3072]{3,2,1,0:T(4,128)(2,1)S(1)}, u32[]{:S(2)}, u32[]{:S(2)}) %collective-permute-start.3) | collective-permute-done | bytes 196640 | tf_op jit(solution)/shard_map/ppermute | solution.py:238
  36.5 0.0 all-to-all-done.pay0
  36.5 1.9 %collective-permute-start.4 = (bf16[32,104,128]{2,1,0:T(8,128)(2,1)S(1)}, bf16[32,104,128]{2,1,0:T(8,128)(2,1)S(1)}, u32[]{:S(2)}, u32[]{:S(2)}) collective-permute-start(bf16[32,104,128]{2,1,0:T(8,128)(2,1)S(1)} %all-to-all-done.pay0), channel_id=1, source_target_pairs={{0,8},{8,0},{1,9},{9,1},{2,10},{10,2},{3,11},{11,3},{4,12},{12,4},... | collective-permute-start | bytes 2555912 | tf_op jit(solution)/shard_map/ppermute | solution.py:240
  38.4 2.0 %collective-permute-done.4.pay1 = bf16[32,104,128]{2,1,0:T(8,128)(2,1)S(1)} collective-permute-done((bf16[32,104,128]{2,1,0:T(8,128)(2,1)S(1)}, bf16[32,104,128]{2,1,0:T(8,128)(2,1)S(1)}, u32[]{:S(2)}, u32[]{:S(2)}) %collective-permute-start.4) | collective-permute-done | bytes 852000 | tf_op jit(solution)/shard_map/ppermute | solution.py:240
  40.4 0.0 copy-done.8
  40.4 0.0 copy-done.9
  40.4 0.0 copy-done.10
  40.4 0.0 copy-start.7
  40.4 1.0 copy-done.7
  41.4 21.8 %left_sums.1 = s16[4,288,256]{2,1,0:T(8,128)(2,1)} custom-call(s32[4]{0:T(128)} %copy-done.4, bf16[32,104,128]{2,1,0:T(8,128)(2,1)} %copy-done.6, bf16[32,104,128]{2,1,0:T(8,128)(2,1)} %copy-done.7, bf16[2,4,4,3072]{3,2,1,0:T(4,128)(2,1)} %copy-done.1, bf16[2,4,4,3072]{3,2,1,0:T(4,128)(2,1)} %copy-done.8, bf16[2,4,4,3072]{3,2,1,0:T(4,128)(2,1)} %copy-done.9, ...), custom_call_target="tpu_custom_call" | custom-call | tf_op jit(solution)/shard_map/left_sums/pallas_call | solution.py:169
  63.2 24.0 %all_to_all.19.refs_0_ = s16[4,288,256]{2,1,0:T(8,128)(2,1)S(1)} all-to-all(s16[4,288,256]{2,1,0:T(8,128)(2,1)} %left_sums.1), channel_id=1, replica_groups=mesh['xh'=2,'zh'=4,'zl'=2,'c'=2,'y'=4,'xl'=2] {'zh'}, dimensions={0} | all-to-all | bytes 1179648 | tf_op jit(solution)/shard_map/all_to_all | solution.py:242
  87.2 0.9 split_scores.1
  88.1 21.2 %all_to_all.20 = f32[256,1,8]{2,1,0:T(1,128)S(1)} all-to-all(f32[256,1,8]{2,1,0:T(1,128)S(1)} %bitcast.9), channel_id=1, replica_groups=mesh['xh'=2,'zh'=4,'zl'=2,'c'=2,'y'=4,'xl'=2] {'xh','zh','zl','c','y','xl'}, dimensions={0} | all-to-all | bytes 16384 | tf_op jit(solution)/shard_map/all_to_all | solution.py:244
  109.3 0.8 reduce_max.9
  (10 shorter events, 0.0 us)
Async XLA Ops:
  0.7 17.0 %copy-start.4 = (s32[4]{0:T(128)}, s32[4]{0:T(128)S(1)}, u32[]{:S(2)}) copy-start(s32[4]{0:T(128)S(1)} %pad_add_fusion.place) | copy-start | bytes 52
  0.7 1.4 %copy-start = (s32[128,3072]{1,0:T(8,128)S(1)}, s32[128,3072]{1,0:T(8,128)}, u32[]{:S(2)}) copy-start(s32[128,3072]{1,0:T(8,128)} %bins.1) | copy-start | bytes 4718596
  2.1 0.7 copy-start.2
  2.9 0.7 copy-start.3
  3.6 0.7 copy-start.5
  6.1 30.3 %all-to-all-start = ((bf16[32,104,128]{2,1,0:T(8,128)(2,1)}), bf16[32,104,128]{2,1,0:T(8,128)(2,1)S(1)}, u32[]{:S(2)}, u32[]{:S(2)}) async-start(bf16[32,104,128]{2,1,0:T(8,128)(2,1)} %get-tuple-element.16), calls=%async_computation | async-start | bytes 1703936 | tf_op jit(solution)/shard_map/all_to_all | solution.py:235
  15.4 2.4 %collective-permute-start = (bf16[16,4,3072]{2,1,0:T(4,128)(2,1)S(1)}, bf16[16,4,3072]{2,1,0:T(4,128)(2,1)S(1)}, u32[]{:S(2)}, u32[]{:S(2)}) collective-permute-start(bf16[16,4,3072]{2,1,0:T(4,128)(2,1)S(1)} %get-tuple-element.18), channel_id=1, source_target_pairs={{0,8},{8,0},{1,9},{9,1},{2,10},{10,2},{3,11},{11,3},{4,12},{12,4},... | collective-permute-start | bytes 1179656 | tf_op jit(solution)/shard_map/ppermute | solution.py:233
  18.4 0.7 copy-start.1
  19.0 10.8 %collective-permute-start.1 = (bf16[2,4,4,3072]{3,2,1,0:T(4,128)(2,1)S(1)}, bf16[2,4,4,3072]{3,2,1,0:T(4,128)(2,1)S(1)}, u32[]{:S(2)}, u32[]{:S(2)}) collective-permute-start(bf16[2,4,4,3072]{3,2,1,0:T(4,128)(2,1)S(1)} %get-tuple-element.20), channel_id=1, source_target_pairs={{0,16},{16,0},{1,17},{17,1},{2,18},{18,2},{3,19},{19,3},{4,20},{20... | collective-permute-start | bytes 589832 | tf_op jit(solution)/shard_map/ppermute | solution.py:236
  20.5 11.1 %collective-permute-start.2 = (bf16[2,4,4,3072]{3,2,1,0:T(4,128)(2,1)S(1)}, bf16[2,4,4,3072]{3,2,1,0:T(4,128)(2,1)S(1)}, u32[]{:S(2)}, u32[]{:S(2)}) collective-permute-start(bf16[2,4,4,3072]{3,2,1,0:T(4,128)(2,1)S(1)} %get-tuple-element.21), channel_id=1, source_target_pairs={{0,128},{128,0},{1,129},{129,1},{2,130},{130,2},{3,131},{131,3},{4... | collective-permute-start | bytes 589832 | tf_op jit(solution)/shard_map/ppermute | solution.py:237
  23.3 13.2 %collective-permute-start.3 = (bf16[2,4,4,3072]{3,2,1,0:T(4,128)(2,1)S(1)}, bf16[2,4,4,3072]{3,2,1,0:T(4,128)(2,1)S(1)}, u32[]{:S(2)}, u32[]{:S(2)}) collective-permute-start(bf16[2,4,4,3072]{3,2,1,0:T(4,128)(2,1)S(1)} %get-tuple-element.22), channel_id=1, source_target_pairs={{0,144},{16,128},{128,16},{144,0},{1,145},{17,129},{129,17},{145,1... | collective-permute-start | bytes 589832 | tf_op jit(solution)/shard_map/ppermute | solution.py:238
  29.8 10.6 %copy-start.8 = (bf16[2,4,4,3072]{3,2,1,0:T(4,128)(2,1)}, bf16[2,4,4,3072]{3,2,1,0:T(4,128)(2,1)S(1)}, u32[]{:S(2)}) copy-start(bf16[2,4,4,3072]{3,2,1,0:T(4,128)(2,1)S(1)} %collective-permute-done.1.b1) | copy-start | bytes 589828
  31.7 8.7 %copy-start.9 = (bf16[2,4,4,3072]{3,2,1,0:T(4,128)(2,1)}, bf16[2,4,4,3072]{3,2,1,0:T(4,128)(2,1)S(1)}, u32[]{:S(2)}) copy-start(bf16[2,4,4,3072]{3,2,1,0:T(4,128)(2,1)S(1)} %collective-permute-done.2.b2) | copy-start | bytes 589828
  36.5 4.0 %copy-start.10 = (bf16[2,4,4,3072]{3,2,1,0:T(4,128)(2,1)}, bf16[2,4,4,3072]{3,2,1,0:T(4,128)(2,1)S(1)}, u32[]{:S(2)}) copy-start(bf16[2,4,4,3072]{3,2,1,0:T(4,128)(2,1)S(1)} %collective-permute-done.3.b3) | copy-start | bytes 589828
  36.5 4.0 %copy-start.6 = (bf16[32,104,128]{2,1,0:T(8,128)(2,1)}, bf16[32,104,128]{2,1,0:T(8,128)(2,1)S(1)}, u32[]{:S(2)}) copy-start(bf16[32,104,128]{2,1,0:T(8,128)(2,1)S(1)} %all-to-all-done.pay0) | copy-start | bytes 2555908
  36.5 4.0 %collective-permute-start.4 = (bf16[32,104,128]{2,1,0:T(8,128)(2,1)S(1)}, bf16[32,104,128]{2,1,0:T(8,128)(2,1)S(1)}, u32[]{:S(2)}, u32[]{:S(2)}) collective-permute-start(bf16[32,104,128]{2,1,0:T(8,128)(2,1)S(1)} %all-to-all-done.pay0), channel_id=1, source_target_pairs={{0,8},{8,0},{1,9},{9,1},{2,10},{10,2},{3,11},{11,3},{4,12},{12,4},... | collective-permute-start | bytes 2555912 | tf_op jit(solution)/shard_map/ppermute | solution.py:240
  40.4 1.0 copy-start.7

commit v3 on v2

v3 whole, which is shorter than its diff:
```python
import jax
import jax.numpy as jnp
from jax import lax
from jax.experimental import pallas as pl
from jax.experimental.pallas import tpu as pltpu
from jax.sharding import Mesh
from jax.sharding import PartitionSpec as P

BINS = 64
NODES = 8
OUTPUTS = 32
OWNED = 4
LANES = OWNED * BINS
GRAD_ROWS = NODES * OUTPUTS
SUM_ROWS = GRAD_ROWS + NODES
WIRE_ROWS = GRAD_ROWS + 4 * NODES
STEPS = 8.0
TOP = 32000.0
HESS_UNIT = 512.0
HESS_SPLIT = 4096.0
ROW = ("xh", "zh", "zl", "c")
FEAT = ("y", "xl")
ALL = ROW + FEAT
NEAR = ("xh", "zl", "y", "xl")
f32 = jnp.float32
bf16 = jnp.bfloat16

ridge_term = 1.0


def pay_kernel(place, grad_hbm, hess_hbm, nodes_hbm, pay, grad, hess, nodes, sems):
    copies = [
        pltpu.make_async_copy(src, dst, sems.at[i])
        for i, (src, dst) in enumerate(
            ((grad_hbm, grad), (hess_hbm, hess), (nodes_hbm, nodes))
        )
    ]
    for copy in copies:
        copy.start()
    for copy in copies:
        copy.wait()
    column = place[4]
    blocks = grad.shape[1] // 128
    node = nodes[0:blocks, :]
    for s in range(1, nodes.shape[0] // blocks):
        node = jnp.where(column == s, nodes[s * blocks : (s + 1) * blocks, :], node)
    rest = jnp.concatenate(
        [
            hess[...].astype(f32),
            node.astype(f32),
            jnp.zeros((pay.shape[1] - (OUTPUTS + 2) * blocks, 128), f32),
        ],
        axis=0,
    ).astype(bf16)
    grads = [grad[:, 128 * i : 128 * (i + 1)] for i in range(blocks)]
    for s in range(pay.shape[0]):
        for i in range(blocks):
            pay[s, OUTPUTS * i : OUTPUTS * (i + 1), :] = grads[i]
        pay[s, OUTPUTS * blocks :, :] = rest


def payload(place, gradient, hessian, row_node, near):
    blocks = gradient.shape[1] // 128
    pay_rows = OUTPUTS * blocks + -(-2 * blocks // 8) * 8
    hessian = hessian.reshape(blocks, 128)
    row_node = row_node.reshape(-1, 128)
    return pl.pallas_call(
        pay_kernel,
        out_shape=jax.ShapeDtypeStruct((near, pay_rows, 128), bf16),
        grid_spec=pltpu.PrefetchScalarGridSpec(
            num_scalar_prefetch=1,
            in_specs=[pl.BlockSpec(memory_space=pl.ANY)] * 3,
            scratch_shapes=[
                pltpu.VMEM(gradient.shape, bf16),
                pltpu.VMEM(hessian.shape, bf16),
                pltpu.VMEM(row_node.shape, jnp.int32),
                pltpu.SemaphoreType.DMA((3,)),
            ],
        ),
        name="payload",
    )(place, gradient, hessian, row_node)


def cut_kernel(place, bins_hbm, p0, p1, p2, p3, bins, sems):
    xh, zl, c = place[0], place[1], place[2]
    tile = 2 * OWNED
    part = bins.shape[0] // sems.shape[0]
    copies = [
        pltpu.make_async_copy(
            bins_hbm.at[i * part : (i + 1) * part], bins.at[i * part : (i + 1) * part], sems.at[i]
        )
        for i in range(sems.shape[0])
    ]
    for copy in copies:
        copy.start()
    for copy in copies:
        copy.wait()
    depth = p0.shape[1]
    for r, out in enumerate((p0, p1, p2, p3)):
        for j in range(depth):
            t = ((xh ^ (r // 2)) * depth + j) * 2 + (zl ^ (r % 2))
            both = bins[pl.ds(pl.multiple_of(t * tile, tile), tile), :].astype(f32)
            first, second = both[0:OWNED], both[OWNED:tile]
            out[0, j] = jnp.where(c == 0, first, second).astype(bf16)
            out[1, j] = jnp.where(c == 0, second, first).astype(bf16)


def cut_by_neighbour(place, bin_index):
    features, shard_rows = bin_index.shape
    shape = jax.ShapeDtypeStruct((2, features // (8 * OWNED), OWNED, shard_rows), bf16)
    return pl.pallas_call(
        cut_kernel,
        out_shape=(shape,) * 4,
        grid_spec=pltpu.PrefetchScalarGridSpec(
            num_scalar_prefetch=1,
            in_specs=[pl.BlockSpec(memory_space=pl.ANY)],
            scratch_shapes=[
                pltpu.VMEM(bin_index.shape, jnp.int32),
                pltpu.SemaphoreType.DMA((4,)),
            ],
        ),
        compiler_params=pltpu.CompilerParams(vmem_limit_bytes=32 << 20),
        name="cut_bins",
    )(place, bin_index)


def hist_kernel(place, *refs):
    pays, refs = refs[:1], refs[1:]
    pieces, refs = refs[:4], refs[4:]
    out, masked = refs
    columns = pays[0].shape[0] // 4
    blocks = pays[0].shape[1] // OUTPUTS
    run = columns * blocks * 128

    @pl.when(pl.program_id(0) == 0)
    def _():
        node_of_row = lax.broadcasted_iota(jnp.int32, (16, 128), 0).astype(f32).astype(bf16)
        for k, pay in enumerate(pays):
            for r in range(4):
                group = (place[0] ^ (r // 2)) * 2 + (place[1] ^ (r % 2))
                for s in range(columns):
                    shard = group * columns + s
                    for i in range(blocks):
                        at = (k * 4 + r) * run + (s * blocks + i) * 128
                        grad = pay[shard, OUTPUTS * i : OUTPUTS * (i + 1), :]
                        first = OUTPUTS * blocks
                        hess = jnp.broadcast_to(pay[shard, first + i : first + i + 1, :], (16, 128))
                        first = first + blocks
                        node = pay[shard, first + i : first + i + 1, :]
                        wide = jnp.broadcast_to(node, (OUTPUTS, 128))
                        for n in range(NODES):
                            masked[OUTPUTS * n : OUTPUTS * (n + 1), at : at + 128] = jnp.where(
                                wide == jnp.array(n, bf16), grad, jnp.zeros_like(grad)
                            )
                        masked[GRAD_ROWS : GRAD_ROWS + 16, at : at + 128] = jnp.where(
                            jnp.broadcast_to(node, (16, 128)) == node_of_row,
                            hess,
                            jnp.zeros_like(hess),
                        )

    level = lax.broadcasted_iota(jnp.int32, (BINS, run), 0).astype(f32).astype(bf16)
    sections = []
    for piece in pieces:
        rows = piece[0, 0]
        sections.append(
            jnp.concatenate(
                [
                    jnp.where(
                        jnp.broadcast_to(rows[f : f + 1, :], (BINS, run)) <= level,
                        jnp.array(1, bf16),
                        jnp.array(0, bf16),
                    )
                    for f in range(OWNED)
                ],
                axis=0,
            )
        )
    upto = jnp.concatenate(sections, axis=1)
    sums = lax.dot_general(
        masked[0:SUM_ROWS, :], upto, (((1,), (1,)), ((), ())), preferred_element_type=f32
    )
    out[0] = sums


def local_sums(place, core, pay, pieces):
    halves, blocks, owned, shard_rows = pieces[0].shape
    bins_spec = pl.BlockSpec((1, 1, owned, shard_rows), lambda j, place: (core, j, 0, 0))
    pay_spec = pl.BlockSpec(pay.shape, lambda j, place: (0, 0, 0))
    rows = 4 * shard_rows
    flops = 2 * SUM_ROWS * rows * LANES * blocks
    return pl.pallas_call(
        hist_kernel,
        out_shape=jax.ShapeDtypeStruct((blocks, SUM_ROWS, LANES), f32),
        grid_spec=pltpu.PrefetchScalarGridSpec(
            num_scalar_prefetch=1,
            grid=(blocks,),
            in_specs=[pay_spec] + [bins_spec] * 4,
            out_specs=pl.BlockSpec((1, SUM_ROWS, LANES), lambda j, place: (j, 0, 0)),
            scratch_shapes=[pltpu.VMEM((GRAD_ROWS + 16, rows), bf16)],
        ),
        cost_estimate=pl.CostEstimate(flops=2 * flops, bytes_accessed=1 << 21, transcendentals=0),
        compiler_params=pltpu.CompilerParams(vmem_limit_bytes=48 << 20),
        name="left_sums",
    )(place, pay, *pieces)


def wire_kernel(mine, theirs, out):
    sums = mine[0] + theirs[0]
    grads = sums[0:GRAD_ROWS].reshape(NODES, OUTPUTS, LANES)
    largest = jnp.max(jnp.abs(grads), axis=1)
    octave = jnp.ceil(jnp.log2(jnp.maximum(largest, 1e-30)) * STEPS + 0.01)
    factor = TOP * jnp.exp2(octave * (-1.0 / STEPS))
    scaled = jnp.floor(grads * factor[:, None, :] + 0.5).reshape(GRAD_ROWS, LANES)
    out[0, 0:GRAD_ROWS, :] = scaled.astype(jnp.int32).astype(jnp.int16)
    units = sums[GRAD_ROWS:SUM_ROWS] * HESS_UNIT
    high = jnp.floor(units * (1.0 / HESS_SPLIT))
    low = units - high * HESS_SPLIT
    rest = jnp.concatenate([octave, high, low, jnp.zeros_like(low)], axis=0)
    out[0, GRAD_ROWS:WIRE_ROWS, :] = rest.astype(jnp.int32).astype(jnp.int16)


def to_wire(mine, theirs):
    blocks = mine.shape[0]
    sums_spec = pl.BlockSpec((1, SUM_ROWS, LANES), lambda j: (j, 0, 0))
    return pl.pallas_call(
        wire_kernel,
        out_shape=jax.ShapeDtypeStruct((blocks, WIRE_ROWS, LANES), jnp.int16),
        grid=(blocks,),
        in_specs=[sums_spec] * 2,
        out_specs=pl.BlockSpec((1, WIRE_ROWS, LANES), lambda j: (j, 0, 0)),
        compiler_params=pltpu.CompilerParams(vmem_limit_bytes=24 << 20),
        name="to_wire",
    )(mine, theirs)


def score_kernel(devices, parts, gain_out, best_out):
    left = jnp.zeros((NODES, OUTPUTS, LANES), f32)
    left_hess = jnp.zeros((NODES, LANES), f32)
    for s in range(parts.shape[0]):
        scaled = parts[s, 0:GRAD_ROWS, :].astype(jnp.int32).astype(f32)
        rest = parts[s, GRAD_ROWS:WIRE_ROWS, :].astype(jnp.int32).astype(f32)
        unit = jnp.exp2(rest[0:NODES] * (1.0 / STEPS)) * (1.0 / TOP)
        left = left + scaled.reshape(NODES, OUTPUTS, LANES) * unit[:, None, :]
        left_hess = left_hess + (
            rest[NODES : 2 * NODES] * HESS_SPLIT + rest[2 * NODES : 3 * NODES]
        ) * (1.0 / HESS_UNIT)
    whole = left[:, :, LANES - 1 :]
    whole_hess = left_hess[:, LANES - 1 :]
    right = whole - left
    right_hess = whole_hess - left_hess

    def part_score(sums, hess):
        return jnp.sum(sums * sums, axis=1) / (hess + ridge_term)

    terms = part_score(left, left_hess) + part_score(right, right_hess)
    gain = (0.5 / OUTPUTS) * (terms - part_score(whole, whole_hess))
    for f in range(OWNED):
        for n in range(NODES):
            gain_out[f : f + 1, n * BINS : (n + 1) * BINS] = gain[
                n : n + 1, f * BINS : (f + 1) * BINS
            ]
    best = jnp.max(gain, axis=1, keepdims=True)
    sublane = lax.broadcasted_iota(jnp.int32, (NODES, 128), 0)
    lane = lax.broadcasted_iota(jnp.int32, (NODES, 128), 1)
    turned = jnp.max(jnp.where(sublane == lane, best, -jnp.inf), axis=0, keepdims=True)
    best_out[...] = jnp.broadcast_to(turned[:, 0:NODES], (devices, NODES))


def final_scores(parts, devices):
    return pl.pallas_call(
        lambda *refs: score_kernel(devices, *refs),
        out_shape=(
            jax.ShapeDtypeStruct((OWNED, NODES * BINS), f32),
            jax.ShapeDtypeStruct((devices, NODES), f32),
        ),
        compiler_params=pltpu.CompilerParams(vmem_limit_bytes=48 << 20),
        name="split_scores",
    )(parts)


def on_device(bin_index, gradient, hessian, row_node):
    place = jnp.stack([lax.axis_index(name) for name in ("xh", "zl", "c", "y", FEAT)])
    swap = [(0, 1), (1, 0)]
    pay = payload(place, gradient, hessian, row_node, lax.axis_size(NEAR))
    pay = lax.all_to_all(pay, NEAR, 0, 0, tiled=True)
    pieces = list(cut_by_neighbour(place, bin_index))
    pieces[1] = lax.ppermute(pieces[1], "zl", swap)
    pieces[2] = lax.ppermute(pieces[2], "xh", swap)
    pieces[3] = lax.ppermute(pieces[3], ("xh", "zl"), [(0, 3), (1, 2), (2, 1), (3, 0)])
    theirs = lax.ppermute(local_sums(place, 1, pay, pieces), "c", swap)
    sums = to_wire(local_sums(place, 0, pay, pieces), theirs)
    parts = lax.all_to_all(sums, "zh", 0, 0, tiled=True)
    gain, best = final_scores(parts, lax.axis_size(ALL))
    best = lax.all_to_all(best, ALL, 0, 0, tiled=True)
    return gain, jnp.max(best, axis=0)


def solution(mesh):
    split = Mesh(mesh.devices.reshape(2, 4, 2, 2, 4, 2), ALL)
    in_specs = (P(FEAT, ROW), P(None, ROW + FEAT), P(ROW + FEAT), P(ROW))
    out_specs = (P(FEAT + ROW, None), P())
    return jax.shard_map(
        on_device, mesh=split, in_specs=in_specs, out_specs=out_specs, check_vma=False
    )
```

time: 111 us -> 104 us (0.937)
  local copies, waits for them, and re-layouts: 5.18 us -> 0.67 us
  waiting for transfers between devices: 16.5 us -> 15.3 us
    unnamed x22 -> x4, local copies, waits for them, and re-layouts: 5.18 us -> 0.01 us
    ppermute x2 -> x1, waiting for transfers between devices: 3.36 us -> 0.01 us  [on_device(): theirs = lax.ppermute(local_sums(place, 1, pay, pieces), 'c', swap)]
    ppermute x1, waiting for transfers between devices: 6.52 us -> 8.61 us  [on_device(): pieces[1] = lax.ppermute(pieces[1], 'zl', swap)]
    ppermute x2 -> x1, starting transfers between devices: 2.99 us -> 1.95 us  [on_device(): theirs = lax.ppermute(local_sums(place, 1, pay, pieces), 'c', swap)]
    pallas_call x3 -> x5, Pallas kernels: 24.3 us -> 24.6 us  [the longest x2 19.9 us: local_sums(): pl.pallas_call(hist_kernel, out_shape=jax.ShapeDtypeStruct((blocks, SUM_R...]
  transfers between devices with their start and end apart: 6 -> 5, of which waited for: 5 -> 3; matrix products, arithmetic and copies ran while one was open for 0% -> 0% of each run, Pallas kernels for 1% -> 11%
where the time goes in v3:
time: 104 us; the launch traced here: 103 us
  blocking collectives  44.9 us (43%)
  Pallas kernels  25.5 us (25%)
  starting transfers between devices  15.4 us (15%)
  waiting for transfers between devices  15.3 us (15%)
    all_to_all x1, blocking collectives, on_device(): parts = lax.all_to_all(sums, 'zh', 0, 0, tiled=True)  24.4 us
    all_to_all x1, blocking collectives, on_device(): best = lax.all_to_all(best, ALL, 0, 0, tiled=True)  20.6 us
    pallas_call x2, Pallas kernels, local_sums(): pl.pallas_call(hist_kernel, out_shape=jax.ShapeDtypeStruct((blocks, SUM_R...  19.9 us
    all_to_all x1, starting transfers between devices, on_device(): pay = lax.all_to_all(pay, NEAR, 0, 0, tiled=True)  9.24 us
    ppermute x1, waiting for transfers between devices, on_device(): pieces[1] = lax.ppermute(pieces[1], 'zl', swap)  8.61 us
    ppermute x1, waiting for transfers between devices, on_device(): lax.ppermute(pieces[3], ('xh', 'zl'), [(0, 3), (1, 2), (2, 1), (3, 0)])  4.77 us
    ppermute x1, starting transfers between devices, on_device(): pieces[2] = lax.ppermute(pieces[2], 'xh', swap)  2.73 us
    pallas_call x1, Pallas kernels, payload(): pl.pallas_call(pay_kernel, out_shape=jax.ShapeDtypeStruct((near, pay_rows...  2.58 us
  transfers between devices with their start and end apart: 5, of which 3 were waited for; matrix products, arithmetic and copies ran while one was open for 0% of the time, Pallas kernels for 11%

profile of v3, /device:TPU:1, one launch (start us, length us, event | category | flops | bytes accessed | tf_op | source)
XLA Modules:
  0.0 103.3 jit_solution(17085661742555512773)
XLA Ops:
  0.6 0.7 stack.23.place
  1.3 0.0 copy-start
  1.3 0.0 copy-start.1
  1.3 2.6 %payload.1 = bf16[32,104,128]{2,1,0:T(8,128)(2,1)} custom-call(s32[5]{0:T(128)} %stack.23.place, bf16[32,384]{1,0:T(8,128)(2,1)} %grad_hbm.1, bf16[3,128]{1,0:T(4,128)(2,1)} %bitcast.12, s32[24,128]{1,0:T(8,128)} %bitcast.11), custom_call_target="tpu_custom_call" | custom-call | tf_op jit(solution)/shard_map/payload/pallas_call | solution.py:67
  3.9 9.2 %all-to-all-start = ((bf16[32,104,128]{2,1,0:T(8,128)(2,1)}), bf16[32,104,128]{2,1,0:T(8,128)(2,1)S(1)}, u32[]{:S(2)}, u32[]{:S(2)}) async-start(bf16[32,104,128]{2,1,0:T(8,128)(2,1)} %payload.1), calls=%async_computation | async-start | bytes 1703936 | tf_op jit(solution)/shard_map/all_to_all | solution.py:285
  13.1 0.0 copy-done
  13.1 0.0 copy-done.1
  13.2 1.6 %cut_bins.1 = (bf16[2,4,4,3072]{3,2,1,0:T(4,128)(2,1)S(1)}, bf16[2,4,4,3072]{3,2,1,0:T(4,128)(2,1)S(1)}, bf16[2,4,4,3072]{3,2,1,0:T(4,128)(2,1)S(1)}, bf16[2,4,4,3072]{3,2,1,0:T(4,128)(2,1)S(1)}) custom-call(s32[5]{0:T(128)S(1)} %copy-done.1, s32[128,3072]{1,0:T(8,128)S(1)} %copy-done), custom_call_target="tpu_custom_call" | custom-call | tf_op jit(solution)/shard_map/cut_bins/pallas_call | solution.py:111
  14.7 1.3 %collective-permute-start = (bf16[2,4,4,3072]{3,2,1,0:T(4,128)(2,1)S(1)}, bf16[2,4,4,3072]{3,2,1,0:T(4,128)(2,1)S(1)}, u32[]{:S(2)}, u32[]{:S(2)}) collective-permute-start(bf16[2,4,4,3072]{3,2,1,0:T(4,128)(2,1)S(1)} %get-tuple-element.9), channel_id=1, source_target_pairs={{0,16},{16,0},{1,17},{17,1},{2,18},{18,2},{3,19},{19,3},{4,20},{20... | collective-permute-start | bytes 589832 | tf_op jit(solution)/shard_map/ppermute | solution.py:287
  16.1 2.7 %collective-permute-start.1 = (bf16[2,4,4,3072]{3,2,1,0:T(4,128)(2,1)S(1)}, bf16[2,4,4,3072]{3,2,1,0:T(4,128)(2,1)S(1)}, u32[]{:S(2)}, u32[]{:S(2)}) collective-permute-start(bf16[2,4,4,3072]{3,2,1,0:T(4,128)(2,1)S(1)} %get-tuple-element.10), channel_id=1, source_target_pairs={{0,128},{128,0},{1,129},{129,1},{2,130},{130,2},{3,131},{131,3},{4... | collective-permute-start | bytes 589832 | tf_op jit(solution)/shard_map/ppermute | solution.py:288
  18.8 0.2 collective-permute-start.2
  19.0 8.6 %collective-permute-done.refs_2_ = bf16[2,4,4,3072]{3,2,1,0:T(4,128)(2,1)S(1)} collective-permute-done((bf16[2,4,4,3072]{3,2,1,0:T(4,128)(2,1)S(1)}, bf16[2,4,4,3072]{3,2,1,0:T(4,128)(2,1)S(1)}, u32[]{:S(2)}, u32[]{:S(2)}) %collective-permute-start) | collective-permute-done | bytes 196640 | tf_op jit(solution)/shard_map/ppermute | solution.py:287
  27.6 1.9 %collective-permute-done.1.refs_3_ = bf16[2,4,4,3072]{3,2,1,0:T(4,128)(2,1)S(1)} collective-permute-done((bf16[2,4,4,3072]{3,2,1,0:T(4,128)(2,1)S(1)}, bf16[2,4,4,3072]{3,2,1,0:T(4,128)(2,1)S(1)}, u32[]{:S(2)}, u32[]{:S(2)}) %collective-permute-start.1) | collective-permute-done | bytes 196640 | tf_op jit(solution)/shard_map/ppermute | solution.py:288
  29.5 4.8 %collective-permute-done.2.refs_4_ = bf16[2,4,4,3072]{3,2,1,0:T(4,128)(2,1)S(1)} collective-permute-done((bf16[2,4,4,3072]{3,2,1,0:T(4,128)(2,1)S(1)}, bf16[2,4,4,3072]{3,2,1,0:T(4,128)(2,1)S(1)}, u32[]{:S(2)}, u32[]{:S(2)}) %collective-permute-start.2) | collective-permute-done | bytes 196640 | tf_op jit(solution)/shard_map/ppermute | solution.py:289
  34.2 0.0 all-to-all-done.refs_0_
  34.2 10.0 %left_sums.3 = f32[4,264,256]{2,1,0:T(8,128)S(1)} custom-call(s32[5]{0:T(128)S(1)} %copy-done.1, bf16[32,104,128]{2,1,0:T(8,128)(2,1)S(1)} %all-to-all-done.refs_0_, bf16[2,4,4,3072]{3,2,1,0:T(4,128)(2,1)S(1)} %get-tuple-element.8.refs_1_, bf16[2,4,4,3072]{3,2,1,0:T(4,128)(2,1)S(1)} %collective-permute-done.refs_2_, ...), custom_call_target="tpu_custom_call" | custom-call | flops 13287555072 | bytes 2097152 | tf_op jit(solution)/shard_map/left_sums/pallas_call | solution.py:191
  44.2 2.0 %collective-permute-start.3 = (f32[4,264,256]{2,1,0:T(8,128)S(1)}, f32[4,264,256]{2,1,0:T(8,128)S(1)}, u32[]{:S(2)}, u32[]{:S(2)}) collective-permute-start(f32[4,264,256]{2,1,0:T(8,128)S(1)} %left_sums.3), channel_id=1, source_target_pairs={{0,8},{8,0},{1,9},{9,1},{2,10},{10,2},{3,11},{11,3},{4,12},{12,4},... | collective-permute-start | bytes 3244040 | tf_op jit(solution)/shard_map/ppermute | solution.py:290
  46.2 10.0 %left_sums.2.mine = f32[4,264,256]{2,1,0:T(8,128)S(1)} custom-call(s32[5]{0:T(128)S(1)} %copy-done.1, bf16[32,104,128]{2,1,0:T(8,128)(2,1)S(1)} %all-to-all-done.refs_0_, bf16[2,4,4,3072]{3,2,1,0:T(4,128)(2,1)S(1)} %get-tuple-element.8.refs_1_, bf16[2,4,4,3072]{3,2,1,0:T(4,128)(2,1)S(1)} %collective-permute-done.refs_2_, ...), custom_call_target="tpu_custom_call" | custom-call | flops 13287555072 | bytes 2097152 | tf_op jit(solution)/shard_map/left_sums/pallas_call | solution.py:191
  56.1 0.0 collective-permute-done.3.theirs
  56.1 0.5 to_wire.1
  56.6 24.4 %all_to_all.19.refs_0_ = s16[4,288,256]{2,1,0:T(8,128)(2,1)S(1)} all-to-all(s16[4,288,256]{2,1,0:T(8,128)(2,1)S(1)} %to_wire.1), channel_id=1, replica_groups=mesh['xh'=2,'zh'=4,'zl'=2,'c'=2,'y'=4,'xl'=2] {'zh'}, dimensions={0} | all-to-all | bytes 1179648 | tf_op jit(solution)/shard_map/all_to_all | solution.py:292
  81.0 0.9 split_scores.1
  82.0 20.6 %all_to_all.20 = f32[256,1,8]{2,1,0:T(1,128)S(1)} all-to-all(f32[256,1,8]{2,1,0:T(1,128)S(1)} %bitcast.10), channel_id=1, replica_groups=mesh['xh'=2,'zh'=4,'zl'=2,'c'=2,'y'=4,'xl'=2] {'xh','zh','zl','c','y','xl'}, dimensions={0} | all-to-all | bytes 16384 | tf_op jit(solution)/shard_map/all_to_all | solution.py:294
  102.5 0.8 reduce_max.9
Async XLA Ops:
  1.3 11.8 %copy-start = (s32[128,3072]{1,0:T(8,128)S(1)}, s32[128,3072]{1,0:T(8,128)}, u32[]{:S(2)}) copy-start(s32[128,3072]{1,0:T(8,128)} %bins_hbm.1) | copy-start | bytes 4718596
  1.3 11.8 %copy-start.1 = (s32[5]{0:T(128)S(1)}, s32[5]{0:T(128)}, u32[]{:S(2)}) copy-start(s32[5]{0:T(128)} %stack.23.place) | copy-start | bytes 64
  3.9 30.4 %all-to-all-start = ((bf16[32,104,128]{2,1,0:T(8,128)(2,1)}), bf16[32,104,128]{2,1,0:T(8,128)(2,1)S(1)}, u32[]{:S(2)}, u32[]{:S(2)}) async-start(bf16[32,104,128]{2,1,0:T(8,128)(2,1)} %payload.1), calls=%async_computation | async-start | bytes 1703936 | tf_op jit(solution)/shard_map/all_to_all | solution.py:285
  14.7 12.9 %collective-permute-start = (bf16[2,4,4,3072]{3,2,1,0:T(4,128)(2,1)S(1)}, bf16[2,4,4,3072]{3,2,1,0:T(4,128)(2,1)S(1)}, u32[]{:S(2)}, u32[]{:S(2)}) collective-permute-start(bf16[2,4,4,3072]{3,2,1,0:T(4,128)(2,1)S(1)} %get-tuple-element.9), channel_id=1, source_target_pairs={{0,16},{16,0},{1,17},{17,1},{2,18},{18,2},{3,19},{19,3},{4,20},{20... | collective-permute-start | bytes 589832 | tf_op jit(solution)/shard_map/ppermute | solution.py:287
  16.1 13.4 %collective-permute-start.1 = (bf16[2,4,4,3072]{3,2,1,0:T(4,128)(2,1)S(1)}, bf16[2,4,4,3072]{3,2,1,0:T(4,128)(2,1)S(1)}, u32[]{:S(2)}, u32[]{:S(2)}) collective-permute-start(bf16[2,4,4,3072]{3,2,1,0:T(4,128)(2,1)S(1)} %get-tuple-element.10), channel_id=1, source_target_pairs={{0,128},{128,0},{1,129},{129,1},{2,130},{130,2},{3,131},{131,3},{4... | collective-permute-start | bytes 589832 | tf_op jit(solution)/shard_map/ppermute | solution.py:288
  18.8 15.5 %collective-permute-start.2 = (bf16[2,4,4,3072]{3,2,1,0:T(4,128)(2,1)S(1)}, bf16[2,4,4,3072]{3,2,1,0:T(4,128)(2,1)S(1)}, u32[]{:S(2)}, u32[]{:S(2)}) collective-permute-start(bf16[2,4,4,3072]{3,2,1,0:T(4,128)(2,1)S(1)} %get-tuple-element.11), channel_id=1, source_target_pairs={{0,144},{16,128},{128,16},{144,0},{1,145},{17,129},{129,17},{145,1... | collective-permute-start | bytes 589832 | tf_op jit(solution)/shard_map/ppermute | solution.py:289
  44.2 11.9 %collective-permute-start.3 = (f32[4,264,256]{2,1,0:T(8,128)S(1)}, f32[4,264,256]{2,1,0:T(8,128)S(1)}, u32[]{:S(2)}, u32[]{:S(2)}) collective-permute-start(f32[4,264,256]{2,1,0:T(8,128)S(1)} %left_sums.3), channel_id=1, source_target_pairs={{0,8},{8,0},{1,9},{9,1},{2,10},{10,2},{3,11},{11,3},{4,12},{12,4},... | collective-permute-start | bytes 3244040 | tf_op jit(solution)/shard_map/ppermute | solution.py:290

commit v4 on v3

--- a/solution.py
+++ b/solution.py
@@ -11,6 +11,7 @@
 OUTPUTS = 32
 OWNED = 4
 LANES = OWNED * BINS
+DEPTH = 256
 GRAD_ROWS = NODES * OUTPUTS
 SUM_ROWS = GRAD_ROWS + NODES
 WIRE_ROWS = GRAD_ROWS + 4 * NODES
@@ -28,7 +29,7 @@
 ridge_term = 1.0
 
 
-def pay_kernel(place, grad_hbm, hess_hbm, nodes_hbm, pay, grad, hess, nodes, sems):
+def pay_kernel(grad_hbm, hess_hbm, nodes_hbm, pay, grad, hess, nodes, sems):
     copies = [
         pltpu.make_async_copy(src, dst, sems.at[i])
         for i, (src, dst) in enumerate(
@@ -39,7 +40,7 @@
         copy.start()
     for copy in copies:
         copy.wait()
-    column = place[4]
+    column = lax.axis_index(FEAT)
     blocks = grad.shape[1] // 128
     node = nodes[0:blocks, :]
     for s in range(1, nodes.shape[0] // blocks):
@@ -59,7 +60,7 @@
         pay[s, OUTPUTS * blocks :, :] = rest
 
 
-def payload(place, gradient, hessian, row_node, near):
+def payload(gradient, hessian, row_node, near):
     blocks = gradient.shape[1] // 128
     pay_rows = OUTPUTS * blocks + -(-2 * blocks // 8) * 8
     hessian = hessian.reshape(blocks, 128)
@@ -67,22 +68,19 @@
     return pl.pallas_call(
         pay_kernel,
         out_shape=jax.ShapeDtypeStruct((near, pay_rows, 128), bf16),
-        grid_spec=pltpu.PrefetchScalarGridSpec(
-            num_scalar_prefetch=1,
-            in_specs=[pl.BlockSpec(memory_space=pl.ANY)] * 3,
-            scratch_shapes=[
-                pltpu.VMEM(gradient.shape, bf16),
-                pltpu.VMEM(hessian.shape, bf16),
-                pltpu.VMEM(row_node.shape, jnp.int32),
-                pltpu.SemaphoreType.DMA((3,)),
-            ],
-        ),
+        in_specs=[pl.BlockSpec(memory_space=pl.ANY)] * 3,
+        scratch_shapes=[
+            pltpu.VMEM(gradient.shape, bf16),
+            pltpu.VMEM(hessian.shape, bf16),
+            pltpu.VMEM(row_node.shape, jnp.int32),
+            pltpu.SemaphoreType.DMA((3,)),
+        ],
         name="payload",
-    )(place, gradient, hessian, row_node)
-
-
-def cut_kernel(place, bins_hbm, p0, p1, p2, p3, bins, sems):
-    xh, zl, c = place[0], place[1], place[2]
+    )(gradient, hessian, row_node)
+
+
+def cut_kernel(bins_hbm, p0, p1, p2, p3, bins, sems):
+    xh, zl, c = lax.axis_index("xh"), lax.axis_index("zl"), lax.axis_index("c")
     tile = 2 * OWNED
     part = bins.shape[0] // sems.shape[0]
     copies = [
@@ -105,103 +103,91 @@
             out[1, j] = jnp.where(c == 0, second, first).astype(bf16)
 
 
-def cut_by_neighbour(place, bin_index):
+def cut_by_neighbour(bin_index):
     features, shard_rows = bin_index.shape
     shape = jax.ShapeDtypeStruct((2, features // (8 * OWNED), OWNED, shard_rows), bf16)
     return pl.pallas_call(
         cut_kernel,
         out_shape=(shape,) * 4,
-        grid_spec=pltpu.PrefetchScalarGridSpec(
-            num_scalar_prefetch=1,
-            in_specs=[pl.BlockSpec(memory_space=pl.ANY)],
-            scratch_shapes=[
-                pltpu.VMEM(bin_index.shape, jnp.int32),
-                pltpu.SemaphoreType.DMA((4,)),
-            ],
-        ),
+        in_specs=[pl.BlockSpec(memory_space=pl.ANY)],
+        scratch_shapes=[
+            pltpu.VMEM(bin_index.shape, jnp.int32),
+            pltpu.SemaphoreType.DMA((4,)),
+        ],
         compiler_params=pltpu.CompilerParams(vmem_limit_bytes=32 << 20),
         name="cut_bins",
-    )(place, bin_index)
-
-
-def hist_kernel(place, *refs):
-    pays, refs = refs[:1], refs[1:]
-    pieces, refs = refs[:4], refs[4:]
-    out, masked = refs
-    columns = pays[0].shape[0] // 4
-    blocks = pays[0].shape[1] // OUTPUTS
-    run = columns * blocks * 128
-
-    @pl.when(pl.program_id(0) == 0)
-    def _():
+    )(bin_index)
+
+
+def sums_kernel(pay, b0, b1, b2, b3, out):
+    blocks = out.shape[0]
+    columns = pay.shape[0] // 4
+    layers = pay.shape[1] // OUTPUTS
+    tiles = b0.shape[-1] // DEPTH
+    xh, zl = lax.axis_index("xh"), lax.axis_index("zl")
+
+    def body(*sums):
+        level = lax.broadcasted_iota(jnp.int32, (BINS, DEPTH), 0).astype(f32).astype(bf16)
         node_of_row = lax.broadcasted_iota(jnp.int32, (16, 128), 0).astype(f32).astype(bf16)
-        for k, pay in enumerate(pays):
-            for r in range(4):
-                group = (place[0] ^ (r // 2)) * 2 + (place[1] ^ (r % 2))
-                for s in range(columns):
-                    shard = group * columns + s
-                    for i in range(blocks):
-                        at = (k * 4 + r) * run + (s * blocks + i) * 128
-                        grad = pay[shard, OUTPUTS * i : OUTPUTS * (i + 1), :]
-                        first = OUTPUTS * blocks
-                        hess = jnp.broadcast_to(pay[shard, first + i : first + i + 1, :], (16, 128))
-                        first = first + blocks
-                        node = pay[shard, first + i : first + i + 1, :]
-                        wide = jnp.broadcast_to(node, (OUTPUTS, 128))
-                        for n in range(NODES):
-                            masked[OUTPUTS * n : OUTPUTS * (n + 1), at : at + 128] = jnp.where(
-                                wide == jnp.array(n, bf16), grad, jnp.zeros_like(grad)
-                            )
-                        masked[GRAD_ROWS : GRAD_ROWS + 16, at : at + 128] = jnp.where(
-                            jnp.broadcast_to(node, (16, 128)) == node_of_row,
-                            hess,
-                            jnp.zeros_like(hess),
-                        )
-
-    level = lax.broadcasted_iota(jnp.int32, (BINS, run), 0).astype(f32).astype(bf16)
-    sections = []
-    for piece in pieces:
-        rows = piece[0, 0]
-        sections.append(
-            jnp.concatenate(
+        one, zero = jnp.array(1, bf16), jnp.array(0, bf16)
+
+        def by_node(group, layer):
+            shard, i = group * columns + layer // layers, layer % layers
+            grad = pay[shard, OUTPUTS * i : OUTPUTS * (i + 1), :]
+            i = OUTPUTS * layers + i
+            hess = jnp.broadcast_to(pay[shard, i : i + 1, :], (16, 128))
+            i = i + layers
+            node = jnp.broadcast_to(pay[shard, i : i + 1, :], (16, 128))
+            rows = []
+            for n in range(NODES):
+                here = node == jnp.array(n, bf16)
+                rows += [jnp.where(here, grad[k : k + 16], zero) for k in range(0, OUTPUTS, 16)]
+            rows.append(jnp.where(node == node_of_row, hess, zero))
+            return jnp.concatenate(rows, axis=0)
+
+        def upto(bins):
+            return jnp.concatenate(
                 [
-                    jnp.where(
-                        jnp.broadcast_to(rows[f : f + 1, :], (BINS, run)) <= level,
-                        jnp.array(1, bf16),
-                        jnp.array(0, bf16),
-                    )
+                    jnp.where(jnp.broadcast_to(bins[f : f + 1], (BINS, DEPTH)) <= level, one, zero)
                     for f in range(OWNED)
                 ],
                 axis=0,
             )
-        )
-    upto = jnp.concatenate(sections, axis=1)
-    sums = lax.dot_general(
-        masked[0:SUM_ROWS, :], upto, (((1,), (1,)), ((), ())), preferred_element_type=f32
-    )
-    out[0] = sums
-
-
-def local_sums(place, core, pay, pieces):
+
+        for r, piece in enumerate((b0, b1, b2, b3)):
+            group = (xh ^ (r // 2)) * 2 + (zl ^ (r % 2))
+            for t in range(tiles):
+                values = jnp.concatenate(
+                    [by_node(group, t * (DEPTH // 128) + k) for k in range(DEPTH // 128)], axis=1
+                )
+                for j in range(0, blocks, 2):
+                    slot = j // 2 % 2
+                    for m in range(2):
+                        bins = piece[0, j + m, :, t * DEPTH : (t + 1) * DEPTH]
+                        pltpu.matmul_push_rhs(upto(bins), slot, m, transpose=True)
+                    for m in range(2):
+                        pltpu.matmul_acc_lhs(sums[j + m], values, load_staged_rhs=slot)
+        for j in range(blocks):
+            out[j] = pltpu.matmul_pop(sums[j])[0:SUM_ROWS]
+
+    pl.run_scoped(body, *[pltpu.ACC(j % 2)((GRAD_ROWS + 16, LANES), f32) for j in range(blocks)])
+
+
+def local_sums(core, pay, pieces):
     halves, blocks, owned, shard_rows = pieces[0].shape
-    bins_spec = pl.BlockSpec((1, 1, owned, shard_rows), lambda j, place: (core, j, 0, 0))
-    pay_spec = pl.BlockSpec(pay.shape, lambda j, place: (0, 0, 0))
-    rows = 4 * shard_rows
-    flops = 2 * SUM_ROWS * rows * LANES * blocks
-    return pl.pallas_call(
-        hist_kernel,
+    bins_spec = pl.BlockSpec((1, blocks, owned, shard_rows), lambda j: (core, 0, 0, 0))
+    pay_spec = pl.BlockSpec(pay.shape, lambda j: (0, 0, 0))
+    flops = 2 * SUM_ROWS * 4 * shard_rows * LANES * blocks
+    return pl.pallas_call(
+        sums_kernel,
         out_shape=jax.ShapeDtypeStruct((blocks, SUM_ROWS, LANES), f32),
-        grid_spec=pltpu.PrefetchScalarGridSpec(
-            num_scalar_prefetch=1,
-            grid=(blocks,),
-            in_specs=[pay_spec] + [bins_spec] * 4,
-            out_specs=pl.BlockSpec((1, SUM_ROWS, LANES), lambda j, place: (j, 0, 0)),
-            scratch_shapes=[pltpu.VMEM((GRAD_ROWS + 16, rows), bf16)],
-        ),
-        cost_estimate=pl.CostEstimate(flops=2 * flops, bytes_accessed=1 << 21, transcendentals=0),
-        compiler_params=pltpu.CompilerParams(vmem_limit_bytes=48 << 20),
+        grid=(1,),
+        in_specs=[pay_spec] + [bins_spec] * 4,
+        out_specs=pl.BlockSpec((blocks, SUM_ROWS, LANES), lambda j: (0, 0, 0)),
+        cost_estimate=pl.CostEstimate(flops=flops, bytes_accessed=1 << 21, transcendentals=0),
+        compiler_params=pltpu.CompilerParams(vmem_limit_bytes=32 << 20),
         name="left_sums",
-    )(place, pay, *pieces)
+    )(pay, *pieces)
 
 
 def wire_kernel(mine, theirs, out):
@@ -279,16 +265,15 @@
 
 
 def on_device(bin_index, gradient, hessian, row_node):
-    place = jnp.stack([lax.axis_index(name) for name in ("xh", "zl", "c", "y", FEAT)])
     swap = [(0, 1), (1, 0)]
-    pay = payload(place, gradient, hessian, row_node, lax.axis_size(NEAR))
+    pay = payload(gradient, hessian, row_node, lax.axis_size(NEAR))
     pay = lax.all_to_all(pay, NEAR, 0, 0, tiled=True)
-    pieces = list(cut_by_neighbour(place, bin_index))
+    pieces = list(cut_by_neighbour(bin_index))
     pieces[1] = lax.ppermute(pieces[1], "zl", swap)
     pieces[2] = lax.ppermute(pieces[2], "xh", swap)
     pieces[3] = lax.ppermute(pieces[3], ("xh", "zl"), [(0, 3), (1, 2), (2, 1), (3, 0)])
-    theirs = lax.ppermute(local_sums(place, 1, pay, pieces), "c", swap)
-    sums = to_wire(local_sums(place, 0, pay, pieces), theirs)
+    theirs = lax.ppermute(local_sums(1, pay, pieces), "c", swap)
+    sums = to_wire(local_sums(0, pay, pieces), theirs)
     parts = lax.all_to_all(sums, "zh", 0, 0, tiled=True)
     gain, best = final_scores(parts, lax.axis_size(ALL))
     best = lax.all_to_all(best, ALL, 0, 0, tiled=True)

time: 104 us -> 96.7 us (0.930)
  Pallas kernels: 25.5 us -> 18.5 us
    pallas_call x3, Pallas kernels: 21.5 us -> 15.2 us  [the longest x2 14.2 us: local_sums(): pl.pallas_call(sums_kernel, out_shape=jax.ShapeDtypeStruct((blocks, SUM_R...]
  transfers between devices with their start and end apart: 5 -> 5, of which waited for: 3 -> 3; matrix products, arithmetic and copies ran while one was open for 0% -> 0% of each run, Pallas kernels for 11% -> 8%
where the time goes in v4:
time: 96.7 us; the launch traced here: 96.4 us
  blocking collectives  44.9 us (46%)
  Pallas kernels  18.5 us (19%)
  waiting for transfers between devices  15.8 us (16%)
  starting transfers between devices  15.6 us (16%)
    all_to_all x1, blocking collectives, on_device(): parts = lax.all_to_all(sums, 'zh', 0, 0, tiled=True)  24.4 us
    all_to_all x1, blocking collectives, on_device(): best = lax.all_to_all(best, ALL, 0, 0, tiled=True)  20.6 us
    pallas_call x2, Pallas kernels, local_sums(): pl.pallas_call(sums_kernel, out_shape=jax.ShapeDtypeStruct((blocks, SUM_R...  14.2 us
    all_to_all x1, starting transfers between devices, on_device(): pay = lax.all_to_all(pay, NEAR, 0, 0, tiled=True)  9.24 us
    ppermute x1, waiting for transfers between devices, on_device(): pieces[1] = lax.ppermute(pieces[1], 'zl', swap)  9.15 us
    ppermute x1, waiting for transfers between devices, on_device(): lax.ppermute(pieces[3], ('xh', 'zl'), [(0, 3), (1, 2), (2, 1), (3, 0)])  4.77 us
    ppermute x1, starting transfers between devices, on_device(): pieces[2] = lax.ppermute(pieces[2], 'xh', swap)  2.73 us
    ppermute x1, starting transfers between devices, on_device(): theirs = lax.ppermute(local_sums(1, pay, pieces), 'c', swap)  2.13 us
  transfers between devices with their start and end apart: 5, of which 3 were waited for; matrix products, arithmetic and copies ran while one was open for 0% of the time, Pallas kernels for 8%

profile of v4, /device:TPU:1, one launch (start us, length us, event | category | flops | bytes accessed | tf_op | source)
XLA Modules:
  0.0 96.4 jit_solution(12666900215467647418)
XLA Ops:
  0.6 0.0 copy-start
  0.6 1.9 %payload.1 = bf16[32,104,128]{2,1,0:T(8,128)(2,1)} custom-call(bf16[32,384]{1,0:T(8,128)(2,1)} %grad_hbm.1, bf16[3,128]{1,0:T(4,128)(2,1)} %bitcast.7, s32[24,128]{1,0:T(8,128)} %bitcast.6), custom_call_target="tpu_custom_call" | custom-call | tf_op jit(solution)/shard_map/payload/pallas_call | solution.py:68
  2.5 9.2 %all-to-all-start = ((bf16[32,104,128]{2,1,0:T(8,128)(2,1)}), bf16[32,104,128]{2,1,0:T(8,128)(2,1)S(1)}, u32[]{:S(2)}, u32[]{:S(2)}) async-start(bf16[32,104,128]{2,1,0:T(8,128)(2,1)} %payload.1), calls=%async_computation | async-start | bytes 1703936 | tf_op jit(solution)/shard_map/all_to_all | solution.py:270
  11.8 0.0 copy-done
  11.8 1.0 %cut_bins.1 = (bf16[2,4,4,3072]{3,2,1,0:T(4,128)(2,1)S(1)}, bf16[2,4,4,3072]{3,2,1,0:T(4,128)(2,1)S(1)}, bf16[2,4,4,3072]{3,2,1,0:T(4,128)(2,1)S(1)}, bf16[2,4,4,3072]{3,2,1,0:T(4,128)(2,1)S(1)}) custom-call(s32[128,3072]{1,0:T(8,128)S(1)} %copy-done), custom_call_target="tpu_custom_call" | custom-call | tf_op jit(solution)/shard_map/cut_bins/pallas_call | solution.py:109
  12.8 1.3 %collective-permute-start = (bf16[2,4,4,3072]{3,2,1,0:T(4,128)(2,1)S(1)}, bf16[2,4,4,3072]{3,2,1,0:T(4,128)(2,1)S(1)}, u32[]{:S(2)}, u32[]{:S(2)}) collective-permute-start(bf16[2,4,4,3072]{3,2,1,0:T(4,128)(2,1)S(1)} %get-tuple-element.9), channel_id=1, source_target_pairs={{0,16},{16,0},{1,17},{17,1},{2,18},{18,2},{3,19},{19,3},{4,20},{20... | collective-permute-start | bytes 589832 | tf_op jit(solution)/shard_map/ppermute | solution.py:272
  14.2 2.7 %collective-permute-start.1 = (bf16[2,4,4,3072]{3,2,1,0:T(4,128)(2,1)S(1)}, bf16[2,4,4,3072]{3,2,1,0:T(4,128)(2,1)S(1)}, u32[]{:S(2)}, u32[]{:S(2)}) collective-permute-start(bf16[2,4,4,3072]{3,2,1,0:T(4,128)(2,1)S(1)} %get-tuple-element.10), channel_id=1, source_target_pairs={{0,128},{128,0},{1,129},{129,1},{2,130},{130,2},{3,131},{131,3},{4... | collective-permute-start | bytes 589832 | tf_op jit(solution)/shard_map/ppermute | solution.py:273
  16.9 0.2 collective-permute-start.2
  17.1 9.1 %collective-permute-done.b1 = bf16[2,4,4,3072]{3,2,1,0:T(4,128)(2,1)S(1)} collective-permute-done((bf16[2,4,4,3072]{3,2,1,0:T(4,128)(2,1)S(1)}, bf16[2,4,4,3072]{3,2,1,0:T(4,128)(2,1)S(1)}, u32[]{:S(2)}, u32[]{:S(2)}) %collective-permute-start) | collective-permute-done | bytes 196640 | tf_op jit(solution)/shard_map/ppermute | solution.py:272
  26.2 1.9 %collective-permute-done.1.b2 = bf16[2,4,4,3072]{3,2,1,0:T(4,128)(2,1)S(1)} collective-permute-done((bf16[2,4,4,3072]{3,2,1,0:T(4,128)(2,1)S(1)}, bf16[2,4,4,3072]{3,2,1,0:T(4,128)(2,1)S(1)}, u32[]{:S(2)}, u32[]{:S(2)}) %collective-permute-start.1) | collective-permute-done | bytes 196640 | tf_op jit(solution)/shard_map/ppermute | solution.py:273
  28.1 4.8 %collective-permute-done.2.b3 = bf16[2,4,4,3072]{3,2,1,0:T(4,128)(2,1)S(1)} collective-permute-done((bf16[2,4,4,3072]{3,2,1,0:T(4,128)(2,1)S(1)}, bf16[2,4,4,3072]{3,2,1,0:T(4,128)(2,1)S(1)}, u32[]{:S(2)}, u32[]{:S(2)}) %collective-permute-start.2) | collective-permute-done | bytes 196640 | tf_op jit(solution)/shard_map/ppermute | solution.py:274
  32.9 0.0 all-to-all-done.pay
  32.9 7.1 %left_sums.3 = f32[4,264,256]{2,1,0:T(8,128)S(1)} custom-call(bf16[32,104,128]{2,1,0:T(8,128)(2,1)S(1)} %all-to-all-done.pay, bf16[2,4,4,3072]{3,2,1,0:T(4,128)(2,1)S(1)} %get-tuple-element.8.b0, bf16[2,4,4,3072]{3,2,1,0:T(4,128)(2,1)S(1)} %collective-permute-done.b1, bf16[2,4,4,3072]{3,2,1,0:T(4,128)(2,1)S(1)} %collective-permute-done.1.b2, ...), custom_call_target="tpu_custom_call" | custom-call | flops 6643777536 | bytes 2097152 | tf_op jit(solution)/shard_map/left_sums/pallas_call | solution.py:181
  40.0 2.1 %collective-permute-start.3 = (f32[4,264,256]{2,1,0:T(8,128)S(1)}, f32[4,264,256]{2,1,0:T(8,128)S(1)}, u32[]{:S(2)}, u32[]{:S(2)}) collective-permute-start(f32[4,264,256]{2,1,0:T(8,128)S(1)} %left_sums.3), channel_id=1, source_target_pairs={{0,8},{8,0},{1,9},{9,1},{2,10},{10,2},{3,11},{11,3},{4,12},{12,4},... | collective-permute-start | bytes 3244040 | tf_op jit(solution)/shard_map/ppermute | solution.py:275
  42.1 7.1 %left_sums.2.mine = f32[4,264,256]{2,1,0:T(8,128)S(1)} custom-call(bf16[32,104,128]{2,1,0:T(8,128)(2,1)S(1)} %all-to-all-done.pay, bf16[2,4,4,3072]{3,2,1,0:T(4,128)(2,1)S(1)} %get-tuple-element.8.b0, bf16[2,4,4,3072]{3,2,1,0:T(4,128)(2,1)S(1)} %collective-permute-done.b1, bf16[2,4,4,3072]{3,2,1,0:T(4,128)(2,1)S(1)} %collective-permute-done.1.b2, ...), custom_call_target="tpu_custom_call" | custom-call | flops 6643777536 | bytes 2097152 | tf_op jit(solution)/shard_map/left_sums/pallas_call | solution.py:181
  49.2 0.0 collective-permute-done.3.theirs
  49.2 0.5 to_wire.1
  49.7 24.4 %all_to_all.19.refs_0_ = s16[4,288,256]{2,1,0:T(8,128)(2,1)S(1)} all-to-all(s16[4,288,256]{2,1,0:T(8,128)(2,1)S(1)} %to_wire.1), channel_id=1, replica_groups=mesh['xh'=2,'zh'=4,'zl'=2,'c'=2,'y'=4,'xl'=2] {'zh'}, dimensions={0} | all-to-all | bytes 1179648 | tf_op jit(solution)/shard_map/all_to_all | solution.py:277
  74.1 0.9 split_scores.1
  75.1 20.6 %all_to_all.20 = f32[256,1,8]{2,1,0:T(1,128)S(1)} all-to-all(f32[256,1,8]{2,1,0:T(1,128)S(1)} %bitcast.5), channel_id=1, replica_groups=mesh['xh'=2,'zh'=4,'zl'=2,'c'=2,'y'=4,'xl'=2] {'xh','zh','zl','c','y','xl'}, dimensions={0} | all-to-all | bytes 16384 | tf_op jit(solution)/shard_map/all_to_all | solution.py:279
  95.6 0.8 reduce_max.9
Async XLA Ops:
  0.6 11.2 %copy-start = (s32[128,3072]{1,0:T(8,128)S(1)}, s32[128,3072]{1,0:T(8,128)}, u32[]{:S(2)}) copy-start(s32[128,3072]{1,0:T(8,128)} %bins_hbm.1) | copy-start | bytes 4718596
  2.5 30.3 %all-to-all-start = ((bf16[32,104,128]{2,1,0:T(8,128)(2,1)}), bf16[32,104,128]{2,1,0:T(8,128)(2,1)S(1)}, u32[]{:S(2)}, u32[]{:S(2)}) async-start(bf16[32,104,128]{2,1,0:T(8,128)(2,1)} %payload.1), calls=%async_computation | async-start | bytes 1703936 | tf_op jit(solution)/shard_map/all_to_all | solution.py:270
  12.8 13.4 %collective-permute-start = (bf16[2,4,4,3072]{3,2,1,0:T(4,128)(2,1)S(1)}, bf16[2,4,4,3072]{3,2,1,0:T(4,128)(2,1)S(1)}, u32[]{:S(2)}, u32[]{:S(2)}) collective-permute-start(bf16[2,4,4,3072]{3,2,1,0:T(4,128)(2,1)S(1)} %get-tuple-element.9), channel_id=1, source_target_pairs={{0,16},{16,0},{1,17},{17,1},{2,18},{18,2},{3,19},{19,3},{4,20},{20... | collective-permute-start | bytes 589832 | tf_op jit(solution)/shard_map/ppermute | solution.py:272
  14.2 14.0 %collective-permute-start.1 = (bf16[2,4,4,3072]{3,2,1,0:T(4,128)(2,1)S(1)}, bf16[2,4,4,3072]{3,2,1,0:T(4,128)(2,1)S(1)}, u32[]{:S(2)}, u32[]{:S(2)}) collective-permute-start(bf16[2,4,4,3072]{3,2,1,0:T(4,128)(2,1)S(1)} %get-tuple-element.10), channel_id=1, source_target_pairs={{0,128},{128,0},{1,129},{129,1},{2,130},{130,2},{3,131},{131,3},{4... | collective-permute-start | bytes 589832 | tf_op jit(solution)/shard_map/ppermute | solution.py:273
  16.9 16.0 %collective-permute-start.2 = (bf16[2,4,4,3072]{3,2,1,0:T(4,128)(2,1)S(1)}, bf16[2,4,4,3072]{3,2,1,0:T(4,128)(2,1)S(1)}, u32[]{:S(2)}, u32[]{:S(2)}) collective-permute-start(bf16[2,4,4,3072]{3,2,1,0:T(4,128)(2,1)S(1)} %get-tuple-element.11), channel_id=1, source_target_pairs={{0,144},{16,128},{128,16},{144,0},{1,145},{17,129},{129,17},{145,1... | collective-permute-start | bytes 589832 | tf_op jit(solution)/shard_map/ppermute | solution.py:274
  40.0 9.2 %collective-permute-start.3 = (f32[4,264,256]{2,1,0:T(8,128)S(1)}, f32[4,264,256]{2,1,0:T(8,128)S(1)}, u32[]{:S(2)}, u32[]{:S(2)}) collective-permute-start(f32[4,264,256]{2,1,0:T(8,128)S(1)} %left_sums.3), channel_id=1, source_target_pairs={{0,8},{8,0},{1,9},{9,1},{2,10},{10,2},{3,11},{11,3},{4,12},{12,4},... | collective-permute-start | bytes 3244040 | tf_op jit(solution)/shard_map/ppermute | solution.py:275

commit v5 on v4

--- a/solution.py
+++ b/solution.py
@@ -1,3 +1,5 @@
+import functools
+
 import jax
 import jax.numpy as jnp
 from jax import lax
@@ -119,8 +121,9 @@
     )(bin_index)
 
 
-def sums_kernel(pay, b0, b1, b2, b3, out):
-    blocks = out.shape[0]
+def sums_kernel(order, pay, b0, b1, b2, b3, out):
+    blocks = len(order)
+    zh, depth = lax.axis_index("zh"), lax.axis_size("zh")
     columns = pay.shape[0] // 4
     layers = pay.shape[1] // OUTPUTS
     tiles = b0.shape[-1] // DEPTH
@@ -163,7 +166,8 @@
                 for j in range(0, blocks, 2):
                     slot = j // 2 % 2
                     for m in range(2):
-                        bins = piece[0, j + m, :, t * DEPTH : (t + 1) * DEPTH]
+                        keeper = (zh + order[j + m]) % depth
+                        bins = piece[0, keeper, :, t * DEPTH : (t + 1) * DEPTH]
                         pltpu.matmul_push_rhs(upto(bins), slot, m, transpose=True)
                     for m in range(2):
                         pltpu.matmul_acc_lhs(sums[j + m], values, load_staged_rhs=slot)
@@ -173,13 +177,14 @@
     pl.run_scoped(body, *[pltpu.ACC(j % 2)((GRAD_ROWS + 16, LANES), f32) for j in range(blocks)])
 
 
-def local_sums(core, pay, pieces):
-    halves, blocks, owned, shard_rows = pieces[0].shape
-    bins_spec = pl.BlockSpec((1, blocks, owned, shard_rows), lambda j: (core, 0, 0, 0))
+def local_sums(core, order, pay, pieces):
+    halves, depth, owned, shard_rows = pieces[0].shape
+    blocks = len(order)
+    bins_spec = pl.BlockSpec((1, depth, owned, shard_rows), lambda j: (core, 0, 0, 0))
     pay_spec = pl.BlockSpec(pay.shape, lambda j: (0, 0, 0))
     flops = 2 * SUM_ROWS * 4 * shard_rows * LANES * blocks
     return pl.pallas_call(
-        sums_kernel,
+        functools.partial(sums_kernel, order),
         out_shape=jax.ShapeDtypeStruct((blocks, SUM_ROWS, LANES), f32),
         grid=(1,),
         in_specs=[pay_spec] + [bins_spec] * 4,
@@ -190,41 +195,38 @@
     )(pay, *pieces)
 
 
-def wire_kernel(mine, theirs, out):
-    sums = mine[0] + theirs[0]
-    grads = sums[0:GRAD_ROWS].reshape(NODES, OUTPUTS, LANES)
-    largest = jnp.max(jnp.abs(grads), axis=1)
-    octave = jnp.ceil(jnp.log2(jnp.maximum(largest, 1e-30)) * STEPS + 0.01)
-    factor = TOP * jnp.exp2(octave * (-1.0 / STEPS))
-    scaled = jnp.floor(grads * factor[:, None, :] + 0.5).reshape(GRAD_ROWS, LANES)
-    out[0, 0:GRAD_ROWS, :] = scaled.astype(jnp.int32).astype(jnp.int16)
-    units = sums[GRAD_ROWS:SUM_ROWS] * HESS_UNIT
-    high = jnp.floor(units * (1.0 / HESS_SPLIT))
-    low = units - high * HESS_SPLIT
-    rest = jnp.concatenate([octave, high, low, jnp.zeros_like(low)], axis=0)
-    out[0, GRAD_ROWS:WIRE_ROWS, :] = rest.astype(jnp.int32).astype(jnp.int16)
-
-
-def to_wire(mine, theirs):
-    blocks = mine.shape[0]
-    sums_spec = pl.BlockSpec((1, SUM_ROWS, LANES), lambda j: (j, 0, 0))
-    return pl.pallas_call(
-        wire_kernel,
-        out_shape=jax.ShapeDtypeStruct((blocks, WIRE_ROWS, LANES), jnp.int16),
-        grid=(blocks,),
-        in_specs=[sums_spec] * 2,
-        out_specs=pl.BlockSpec((1, WIRE_ROWS, LANES), lambda j: (j, 0, 0)),
+def wire_kernel(first, mine, theirs, *outs):
+    for j, out in enumerate(outs):
+        sums = mine[j] + theirs[first + j]
+        grads = sums[0:GRAD_ROWS].reshape(NODES, OUTPUTS, LANES)
+        largest = jnp.max(jnp.abs(grads), axis=1)
+        octave = jnp.ceil(jnp.log2(jnp.maximum(largest, 1e-30)) * STEPS + 0.01)
+        factor = TOP * jnp.exp2(octave * (-1.0 / STEPS))
+        scaled = jnp.floor(grads * factor[:, None, :] + 0.5).reshape(GRAD_ROWS, LANES)
+        out[0:GRAD_ROWS, :] = scaled.astype(jnp.int32).astype(jnp.int16)
+        units = sums[GRAD_ROWS:SUM_ROWS] * HESS_UNIT
+        high = jnp.floor(units * (1.0 / HESS_SPLIT))
+        low = units - high * HESS_SPLIT
+        rest = jnp.concatenate([octave, high, low, jnp.zeros_like(low)], axis=0)
+        out[GRAD_ROWS:WIRE_ROWS, :] = rest.astype(jnp.int32).astype(jnp.int16)
+
+
+def to_wire(first, mine, theirs):
+    return pl.pallas_call(
+        functools.partial(wire_kernel, first),
+        out_shape=(jax.ShapeDtypeStruct((WIRE_ROWS, LANES), jnp.int16),) * mine.shape[0],
         compiler_params=pltpu.CompilerParams(vmem_limit_bytes=24 << 20),
         name="to_wire",
     )(mine, theirs)
 
 
-def score_kernel(devices, parts, gain_out, best_out):
+def score_kernel(devices, *refs):
+    parts, (gain_out, best_out) = refs[:-2], refs[-2:]
     left = jnp.zeros((NODES, OUTPUTS, LANES), f32)
     left_hess = jnp.zeros((NODES, LANES), f32)
-    for s in range(parts.shape[0]):
-        scaled = parts[s, 0:GRAD_ROWS, :].astype(jnp.int32).astype(f32)
-        rest = parts[s, GRAD_ROWS:WIRE_ROWS, :].astype(jnp.int32).astype(f32)
+    for part in parts:
+        scaled = part[0:GRAD_ROWS, :].astype(jnp.int32).astype(f32)
+        rest = part[GRAD_ROWS:WIRE_ROWS, :].astype(jnp.int32).astype(f32)
         unit = jnp.exp2(rest[0:NODES] * (1.0 / STEPS)) * (1.0 / TOP)
         left = left + scaled.reshape(NODES, OUTPUTS, LANES) * unit[:, None, :]
         left_hess = left_hess + (
@@ -254,14 +256,14 @@
 
 def final_scores(parts, devices):
     return pl.pallas_call(
-        lambda *refs: score_kernel(devices, *refs),
+        functools.partial(score_kernel, devices),
         out_shape=(
             jax.ShapeDtypeStruct((OWNED, NODES * BINS), f32),
             jax.ShapeDtypeStruct((devices, NODES), f32),
         ),
         compiler_params=pltpu.CompilerParams(vmem_limit_bytes=48 << 20),
         name="split_scores",
-    )(parts)
+    )(*parts)
 
 
 def on_device(bin_index, gradient, hessian, row_node):
@@ -272,9 +274,18 @@
     pieces[1] = lax.ppermute(pieces[1], "zl", swap)
     pieces[2] = lax.ppermute(pieces[2], "xh", swap)
     pieces[3] = lax.ppermute(pieces[3], ("xh", "zl"), [(0, 3), (1, 2), (2, 1), (3, 0)])
-    theirs = lax.ppermute(local_sums(1, pay, pieces), "c", swap)
-    sums = to_wire(local_sums(0, pay, pieces), theirs)
-    parts = lax.all_to_all(sums, "zh", 0, 0, tiled=True)
+    depth = lax.axis_size("zh")
+
+    def ahead(x, d):
+        return lax.ppermute(x, "zh", [(i, (i + d) % depth) for i in range(depth)])
+
+    theirs = lax.ppermute(local_sums(1, (2, 1, 3, 0), pay, pieces), "c", swap)
+    two, one = to_wire(0, local_sums(0, (2, 1), pay, pieces), theirs)
+    pay, two, one = lax.optimization_barrier((pay, two, one))
+    two, one = ahead(two, 2), ahead(one, 1)
+    three, own = to_wire(2, local_sums(0, (3, 0), pay, pieces), theirs)
+    one, two, three = lax.optimization_barrier((one, two, three))
+    parts = (own, one, ahead(three, 3), two)
     gain, best = final_scores(parts, lax.axis_size(ALL))
     best = lax.all_to_all(best, ALL, 0, 0, tiled=True)
     return gain, jnp.max(best, axis=0)

time: 96.7 us -> 98 us (1.013)
  blocking collectives: 44.9 us -> 24.7 us
  starting transfers between devices: 15.6 us -> 27.8 us
  waiting for transfers between devices: 15.8 us -> 25.1 us
    all_to_all x1 -> x0, blocking collectives: 24.4 us -> none  [on_device(): parts = lax.all_to_all(sums, 'zh', 0, 0, tiled=True)]
    ppermute x1 -> x4, starting transfers between devices: 2.13 us -> 14.3 us  [the longest x3 12.2 us: ahead(): return lax.ppermute(x, 'zh', [(i, (i + d) % depth) for i in range(depth)])]
    ppermute x1 -> x4, waiting for transfers between devices: 0.01 us -> 9.26 us  [the longest x3 9.26 us: ahead(): return lax.ppermute(x, 'zh', [(i, (i + d) % depth) for i in range(depth)])]
    all_to_all x1, blocking collectives: 20.6 us -> 24.7 us  [on_device(): best = lax.all_to_all(best, ALL, 0, 0, tiled=True)]
    pallas_call x4 -> x6, Pallas kernels: 15.6 us -> 15.8 us  [the longest x3 14.4 us: local_sums(): pl.pallas_call(functools.partial(sums_kernel, order), out_shape=jax.Shape...]
  transfers between devices with their start and end apart: 5 -> 8, of which waited for: 3 -> 6; matrix products, arithmetic and copies ran while one was open for 0% -> 0% of each run, Pallas kernels for 8% -> 9%
where the time goes in v5:
time: 98 us; the launch traced here: 97.8 us
  starting transfers between devices  27.8 us (28%)
  waiting for transfers between devices  25.1 us (26%)
  blocking collectives  24.7 us (25%)
  Pallas kernels  18.7 us (19%)
    all_to_all x1, blocking collectives, on_device(): best = lax.all_to_all(best, ALL, 0, 0, tiled=True)  24.7 us
    pallas_call x3, Pallas kernels, local_sums(): pl.pallas_call(functools.partial(sums_kernel, order), out_shape=jax.Shape...  14.4 us
    ppermute x3, starting transfers between devices, ahead(): return lax.ppermute(x, 'zh', [(i, (i + d) % depth) for i in range(depth)])  12.2 us
    ppermute x3, waiting for transfers between devices, ahead(): return lax.ppermute(x, 'zh', [(i, (i + d) % depth) for i in range(depth)])  9.26 us
    all_to_all x1, starting transfers between devices, on_device(): pay = lax.all_to_all(pay, NEAR, 0, 0, tiled=True)  9.24 us
    ppermute x1, waiting for transfers between devices, on_device(): pieces[1] = lax.ppermute(pieces[1], 'zl', swap)  9.15 us
    ppermute x1, waiting for transfers between devices, on_device(): lax.ppermute(pieces[3], ('xh', 'zl'), [(0, 3), (1, 2), (2, 1), (3, 0)])  4.77 us
    ppermute x1, starting transfers between devices, on_device(): pieces[2] = lax.ppermute(pieces[2], 'xh', swap)  2.73 us
  transfers between devices with their start and end apart: 8, of which 6 were waited for; matrix products, arithmetic and copies ran while one was open for 0% of the time, Pallas kernels for 9%

profile of v5, /device:TPU:1, one launch (start us, length us, event | category | flops | bytes accessed | tf_op | source)
XLA Modules:
  0.0 97.8 jit_solution(8875138325841391320)
XLA Ops:
  0.6 0.0 copy-start
  0.6 1.9 %payload.1 = bf16[32,104,128]{2,1,0:T(8,128)(2,1)} custom-call(bf16[32,384]{1,0:T(8,128)(2,1)} %grad_hbm.1, bf16[3,128]{1,0:T(4,128)(2,1)} %bitcast.7, s32[24,128]{1,0:T(8,128)} %bitcast.6), custom_call_target="tpu_custom_call" | custom-call | tf_op jit(solution)/shard_map/payload/pallas_call | solution.py:70
  2.6 9.2 %all-to-all-start = ((bf16[32,104,128]{2,1,0:T(8,128)(2,1)}), bf16[32,104,128]{2,1,0:T(8,128)(2,1)S(1)}, u32[]{:S(2)}, u32[]{:S(2)}) async-start(bf16[32,104,128]{2,1,0:T(8,128)(2,1)} %payload.1), calls=%async_computation | async-start | bytes 1703936 | tf_op jit(solution)/shard_map/all_to_all | solution.py:272
  11.8 0.0 copy-done
  11.8 1.0 %cut_bins.1 = (bf16[2,4,4,3072]{3,2,1,0:T(4,128)(2,1)S(1)}, bf16[2,4,4,3072]{3,2,1,0:T(4,128)(2,1)S(1)}, bf16[2,4,4,3072]{3,2,1,0:T(4,128)(2,1)S(1)}, bf16[2,4,4,3072]{3,2,1,0:T(4,128)(2,1)S(1)}) custom-call(s32[128,3072]{1,0:T(8,128)S(1)} %copy-done), custom_call_target="tpu_custom_call" | custom-call | tf_op jit(solution)/shard_map/cut_bins/pallas_call | solution.py:111
  12.9 1.3 %collective-permute-start = (bf16[2,4,4,3072]{3,2,1,0:T(4,128)(2,1)S(1)}, bf16[2,4,4,3072]{3,2,1,0:T(4,128)(2,1)S(1)}, u32[]{:S(2)}, u32[]{:S(2)}) collective-permute-start(bf16[2,4,4,3072]{3,2,1,0:T(4,128)(2,1)S(1)} %get-tuple-element.19), channel_id=1, source_target_pairs={{0,16},{16,0},{1,17},{17,1},{2,18},{18,2},{3,19},{19,3},{4,20},{20... | collective-permute-start | bytes 589832 | tf_op jit(solution)/shard_map/ppermute | solution.py:274
  14.2 2.7 %collective-permute-start.1 = (bf16[2,4,4,3072]{3,2,1,0:T(4,128)(2,1)S(1)}, bf16[2,4,4,3072]{3,2,1,0:T(4,128)(2,1)S(1)}, u32[]{:S(2)}, u32[]{:S(2)}) collective-permute-start(bf16[2,4,4,3072]{3,2,1,0:T(4,128)(2,1)S(1)} %get-tuple-element.20), channel_id=1, source_target_pairs={{0,128},{128,0},{1,129},{129,1},{2,130},{130,2},{3,131},{131,3},{4... | collective-permute-start | bytes 589832 | tf_op jit(solution)/shard_map/ppermute | solution.py:275
  16.9 0.2 collective-permute-start.2
  17.1 9.1 %collective-permute-done.b1 = bf16[2,4,4,3072]{3,2,1,0:T(4,128)(2,1)S(1)} collective-permute-done((bf16[2,4,4,3072]{3,2,1,0:T(4,128)(2,1)S(1)}, bf16[2,4,4,3072]{3,2,1,0:T(4,128)(2,1)S(1)}, u32[]{:S(2)}, u32[]{:S(2)}) %collective-permute-start) | collective-permute-done | bytes 196640 | tf_op jit(solution)/shard_map/ppermute | solution.py:274
  26.3 1.9 %collective-permute-done.1.b2 = bf16[2,4,4,3072]{3,2,1,0:T(4,128)(2,1)S(1)} collective-permute-done((bf16[2,4,4,3072]{3,2,1,0:T(4,128)(2,1)S(1)}, bf16[2,4,4,3072]{3,2,1,0:T(4,128)(2,1)S(1)}, u32[]{:S(2)}, u32[]{:S(2)}) %collective-permute-start.1) | collective-permute-done | bytes 196640 | tf_op jit(solution)/shard_map/ppermute | solution.py:275
  28.1 4.8 %collective-permute-done.2.b3 = bf16[2,4,4,3072]{3,2,1,0:T(4,128)(2,1)S(1)} collective-permute-done((bf16[2,4,4,3072]{3,2,1,0:T(4,128)(2,1)S(1)}, bf16[2,4,4,3072]{3,2,1,0:T(4,128)(2,1)S(1)}, u32[]{:S(2)}, u32[]{:S(2)}) %collective-permute-start.2) | collective-permute-done | bytes 196640 | tf_op jit(solution)/shard_map/ppermute | solution.py:276
  32.9 0.0 all-to-all-done.pay
  32.9 7.1 %left_sums.4 = f32[4,264,256]{2,1,0:T(8,128)S(1)} custom-call(bf16[32,104,128]{2,1,0:T(8,128)(2,1)S(1)} %all-to-all-done.pay, bf16[2,4,4,3072]{3,2,1,0:T(4,128)(2,1)S(1)} %get-tuple-element.18.b0, bf16[2,4,4,3072]{3,2,1,0:T(4,128)(2,1)S(1)} %collective-permute-done.b1, bf16[2,4,4,3072]{3,2,1,0:T(4,128)(2,1)S(1)} %collective-permute-done.1.b2, ...), custom_call_target="tpu_custom_call" | custom-call | flops 6643777536 | bytes 2097152 | tf_op jit(solution)/shard_map/left_sums/pallas_call | solution.py:186
  40.0 2.1 %collective-permute-start.3 = (f32[4,264,256]{2,1,0:T(8,128)S(1)}, f32[4,264,256]{2,1,0:T(8,128)S(1)}, u32[]{:S(2)}, u32[]{:S(2)}) collective-permute-start(f32[4,264,256]{2,1,0:T(8,128)S(1)} %left_sums.4), channel_id=1, source_target_pairs={{0,8},{8,0},{1,9},{9,1},{2,10},{10,2},{3,11},{11,3},{4,12},{12,4},... | collective-permute-start | bytes 3244040 | tf_op jit(solution)/shard_map/ppermute | solution.py:282
  42.2 3.7 %left_sums.3.mine = f32[2,264,256]{2,1,0:T(8,128)S(1)} custom-call(bf16[32,104,128]{2,1,0:T(8,128)(2,1)S(1)} %all-to-all-done.pay, bf16[2,4,4,3072]{3,2,1,0:T(4,128)(2,1)S(1)} %get-tuple-element.18.b0, bf16[2,4,4,3072]{3,2,1,0:T(4,128)(2,1)S(1)} %collective-permute-done.b1, bf16[2,4,4,3072]{3,2,1,0:T(4,128)(2,1)S(1)} %collective-permute-done.1.b2, ...), custom_call_target="tpu_custom_call" | custom-call | flops 3321888768 | bytes 2097152 | tf_op jit(solution)/shard_map/left_sums/pallas_call | solution.py:186
  45.8 0.0 collective-permute-done.3.theirs
  45.8 0.2 to_wire.2
  46.0 3.1 %collective-permute-start.4 = (s16[288,256]{1,0:T(8,128)(2,1)S(1)}, s16[288,256]{1,0:T(8,128)(2,1)S(1)}, u32[]{:S(2)}, u32[]{:S(2)}) collective-permute-start(s16[288,256]{1,0:T(8,128)(2,1)S(1)} %get-tuple-element.26), channel_id=1, source_target_pairs={{0,32},{32,64},{64,96},{96,0},{1,33},{33,65},{65,97},{97,1},{2,34}... | collective-permute-start | bytes 442376 | tf_op jit(solution)/shard_map/ppermute | solution.py:280
  49.1 4.2 %collective-permute-start.5 = (s16[288,256]{1,0:T(8,128)(2,1)S(1)}, s16[288,256]{1,0:T(8,128)(2,1)S(1)}, u32[]{:S(2)}, u32[]{:S(2)}) collective-permute-start(s16[288,256]{1,0:T(8,128)(2,1)S(1)} %get-tuple-element.27), channel_id=1, source_target_pairs={{0,64},{32,96},{64,0},{96,32},{1,65},{33,97},{65,1},{97,33},{2,66}... | collective-permute-start | bytes 442376 | tf_op jit(solution)/shard_map/ppermute | solution.py:280
  53.3 3.6 %left_sums.5.mine = f32[2,264,256]{2,1,0:T(8,128)S(1)} custom-call(bf16[32,104,128]{2,1,0:T(8,128)(2,1)S(1)} %all-to-all-done.pay, bf16[2,4,4,3072]{3,2,1,0:T(4,128)(2,1)S(1)} %get-tuple-element.18.b0, bf16[2,4,4,3072]{3,2,1,0:T(4,128)(2,1)S(1)} %collective-permute-done.b1, bf16[2,4,4,3072]{3,2,1,0:T(4,128)(2,1)S(1)} %collective-permute-done.1.b2, ...), custom_call_target="tpu_custom_call" | custom-call | flops 3321888768 | bytes 2097152 | tf_op jit(solution)/shard_map/left_sums/pallas_call | solution.py:186
  57.0 0.2 to_wire.3
  57.2 1.1 %collective-permute-done.4.refs_1_ = s16[288,256]{1,0:T(8,128)(2,1)S(1)} collective-permute-done((s16[288,256]{1,0:T(8,128)(2,1)S(1)}, s16[288,256]{1,0:T(8,128)(2,1)S(1)}, u32[]{:S(2)}, u32[]{:S(2)}) %collective-permute-start.4) | collective-permute-done | bytes 147488 | tf_op jit(solution)/shard_map/ppermute | solution.py:280
  58.3 5.3 %collective-permute-done.5.refs_3_ = s16[288,256]{1,0:T(8,128)(2,1)S(1)} collective-permute-done((s16[288,256]{1,0:T(8,128)(2,1)S(1)}, s16[288,256]{1,0:T(8,128)(2,1)S(1)}, u32[]{:S(2)}, u32[]{:S(2)}) %collective-permute-start.5) | collective-permute-done | bytes 147488 | tf_op jit(solution)/shard_map/ppermute | solution.py:280
  63.7 4.9 %collective-permute-start.6 = (s16[288,256]{1,0:T(8,128)(2,1)S(1)}, s16[288,256]{1,0:T(8,128)(2,1)S(1)}, u32[]{:S(2)}, u32[]{:S(2)}) collective-permute-start(s16[288,256]{1,0:T(8,128)(2,1)S(1)} %get-tuple-element.30), channel_id=1, source_target_pairs={{0,96},{32,0},{64,32},{96,64},{1,97},{33,1},{65,33},{97,65},{2,98}... | collective-permute-start | bytes 442376 | tf_op jit(solution)/shard_map/ppermute | solution.py:280
  68.5 2.8 %collective-permute-done.6.refs_2_ = s16[288,256]{1,0:T(8,128)(2,1)S(1)} collective-permute-done((s16[288,256]{1,0:T(8,128)(2,1)S(1)}, s16[288,256]{1,0:T(8,128)(2,1)S(1)}, u32[]{:S(2)}, u32[]{:S(2)}) %collective-permute-start.6) | collective-permute-done | bytes 147488 | tf_op jit(solution)/shard_map/ppermute | solution.py:280
  71.3 0.9 split_scores.1
  72.3 24.7 %all_to_all.14 = f32[256,1,8]{2,1,0:T(1,128)S(1)} all-to-all(f32[256,1,8]{2,1,0:T(1,128)S(1)} %bitcast.5), channel_id=1, replica_groups=mesh['xh'=2,'zh'=4,'zl'=2,'c'=2,'y'=4,'xl'=2] {'xh','zh','zl','c','y','xl'}, dimensions={0} | all-to-all | bytes 16384 | tf_op jit(solution)/shard_map/all_to_all | solution.py:290
  97.0 0.8 reduce_max.9
Async XLA Ops:
  0.6 11.2 %copy-start = (s32[128,3072]{1,0:T(8,128)S(1)}, s32[128,3072]{1,0:T(8,128)}, u32[]{:S(2)}) copy-start(s32[128,3072]{1,0:T(8,128)} %bins_hbm.1) | copy-start | bytes 4718596
  2.6 30.3 %all-to-all-start = ((bf16[32,104,128]{2,1,0:T(8,128)(2,1)}), bf16[32,104,128]{2,1,0:T(8,128)(2,1)S(1)}, u32[]{:S(2)}, u32[]{:S(2)}) async-start(bf16[32,104,128]{2,1,0:T(8,128)(2,1)} %payload.1), calls=%async_computation | async-start | bytes 1703936 | tf_op jit(solution)/shard_map/all_to_all | solution.py:272
  12.9 13.4 %collective-permute-start = (bf16[2,4,4,3072]{3,2,1,0:T(4,128)(2,1)S(1)}, bf16[2,4,4,3072]{3,2,1,0:T(4,128)(2,1)S(1)}, u32[]{:S(2)}, u32[]{:S(2)}) collective-permute-start(bf16[2,4,4,3072]{3,2,1,0:T(4,128)(2,1)S(1)} %get-tuple-element.19), channel_id=1, source_target_pairs={{0,16},{16,0},{1,17},{17,1},{2,18},{18,2},{3,19},{19,3},{4,20},{20... | collective-permute-start | bytes 589832 | tf_op jit(solution)/shard_map/ppermute | solution.py:274
  14.2 14.0 %collective-permute-start.1 = (bf16[2,4,4,3072]{3,2,1,0:T(4,128)(2,1)S(1)}, bf16[2,4,4,3072]{3,2,1,0:T(4,128)(2,1)S(1)}, u32[]{:S(2)}, u32[]{:S(2)}) collective-permute-start(bf16[2,4,4,3072]{3,2,1,0:T(4,128)(2,1)S(1)} %get-tuple-element.20), channel_id=1, source_target_pairs={{0,128},{128,0},{1,129},{129,1},{2,130},{130,2},{3,131},{131,3},{4... | collective-permute-start | bytes 589832 | tf_op jit(solution)/shard_map/ppermute | solution.py:275
  16.9 16.0 %collective-permute-start.2 = (bf16[2,4,4,3072]{3,2,1,0:T(4,128)(2,1)S(1)}, bf16[2,4,4,3072]{3,2,1,0:T(4,128)(2,1)S(1)}, u32[]{:S(2)}, u32[]{:S(2)}) collective-permute-start(bf16[2,4,4,3072]{3,2,1,0:T(4,128)(2,1)S(1)} %get-tuple-element.21), channel_id=1, source_target_pairs={{0,144},{16,128},{128,16},{144,0},{1,145},{17,129},{129,17},{145,1... | collective-permute-start | bytes 589832 | tf_op jit(solution)/shard_map/ppermute | solution.py:276
  40.0 5.8 %collective-permute-start.3 = (f32[4,264,256]{2,1,0:T(8,128)S(1)}, f32[4,264,256]{2,1,0:T(8,128)S(1)}, u32[]{:S(2)}, u32[]{:S(2)}) collective-permute-start(f32[4,264,256]{2,1,0:T(8,128)S(1)} %left_sums.4), channel_id=1, source_target_pairs={{0,8},{8,0},{1,9},{9,1},{2,10},{10,2},{3,11},{11,3},{4,12},{12,4},... | collective-permute-start | bytes 3244040 | tf_op jit(solution)/shard_map/ppermute | solution.py:282
  46.0 12.3 %collective-permute-start.4 = (s16[288,256]{1,0:T(8,128)(2,1)S(1)}, s16[288,256]{1,0:T(8,128)(2,1)S(1)}, u32[]{:S(2)}, u32[]{:S(2)}) collective-permute-start(s16[288,256]{1,0:T(8,128)(2,1)S(1)} %get-tuple-element.26), channel_id=1, source_target_pairs={{0,32},{32,64},{64,96},{96,0},{1,33},{33,65},{65,97},{97,1},{2,34}... | collective-permute-start | bytes 442376 | tf_op jit(solution)/shard_map/ppermute | solution.py:280
  49.1 14.6 %collective-permute-start.5 = (s16[288,256]{1,0:T(8,128)(2,1)S(1)}, s16[288,256]{1,0:T(8,128)(2,1)S(1)}, u32[]{:S(2)}, u32[]{:S(2)}) collective-permute-start(s16[288,256]{1,0:T(8,128)(2,1)S(1)} %get-tuple-element.27), channel_id=1, source_target_pairs={{0,64},{32,96},{64,0},{96,32},{1,65},{33,97},{65,1},{97,33},{2,66}... | collective-permute-start | bytes 442376 | tf_op jit(solution)/shard_map/ppermute | solution.py:280
  63.7 7.7 %collective-permute-start.6 = (s16[288,256]{1,0:T(8,128)(2,1)S(1)}, s16[288,256]{1,0:T(8,128)(2,1)S(1)}, u32[]{:S(2)}, u32[]{:S(2)}) collective-permute-start(s16[288,256]{1,0:T(8,128)(2,1)S(1)} %get-tuple-element.30), channel_id=1, source_target_pairs={{0,96},{32,0},{64,32},{96,64},{1,97},{33,1},{65,33},{97,65},{2,98}... | collective-permute-start | bytes 442376 | tf_op jit(solution)/shard_map/ppermute | solution.py:280

commit v6 on v4

--- a/solution.py
+++ b/solution.py
@@ -1,3 +1,5 @@
+import functools
+
 import jax
 import jax.numpy as jnp
 from jax import lax
@@ -119,11 +121,12 @@
     )(bin_index)
 
 
-def sums_kernel(pay, b0, b1, b2, b3, out):
+def sums_kernel(places, pay, *refs):
+    pieces, before, out = refs[: len(places)], refs[len(places) : -1], refs[-1]
     blocks = out.shape[0]
     columns = pay.shape[0] // 4
     layers = pay.shape[1] // OUTPUTS
-    tiles = b0.shape[-1] // DEPTH
+    tiles = pieces[0].shape[-1] // DEPTH
     xh, zl = lax.axis_index("xh"), lax.axis_index("zl")
 
     def body(*sums):
@@ -154,7 +157,7 @@
                 axis=0,
             )
 
-        for r, piece in enumerate((b0, b1, b2, b3)):
+        for r, piece in zip(places, pieces):
             group = (xh ^ (r // 2)) * 2 + (zl ^ (r % 2))
             for t in range(tiles):
                 values = jnp.concatenate(
@@ -168,26 +171,31 @@
                     for m in range(2):
                         pltpu.matmul_acc_lhs(sums[j + m], values, load_staged_rhs=slot)
         for j in range(blocks):
-            out[j] = pltpu.matmul_pop(sums[j])[0:SUM_ROWS]
+            total = pltpu.matmul_pop(sums[j])[0:SUM_ROWS]
+            for term in before:
+                total = total + term[j]
+            out[j] = total
 
     pl.run_scoped(body, *[pltpu.ACC(j % 2)((GRAD_ROWS + 16, LANES), f32) for j in range(blocks)])
 
 
-def local_sums(core, pay, pieces):
+def local_sums(core, places, pay, pieces, before=()):
     halves, blocks, owned, shard_rows = pieces[0].shape
     bins_spec = pl.BlockSpec((1, blocks, owned, shard_rows), lambda j: (core, 0, 0, 0))
     pay_spec = pl.BlockSpec(pay.shape, lambda j: (0, 0, 0))
-    flops = 2 * SUM_ROWS * 4 * shard_rows * LANES * blocks
-    return pl.pallas_call(
-        sums_kernel,
+    flops = 2 * SUM_ROWS * len(places) * shard_rows * LANES * blocks
+    return pl.pallas_call(
+        functools.partial(sums_kernel, places),
         out_shape=jax.ShapeDtypeStruct((blocks, SUM_ROWS, LANES), f32),
         grid=(1,),
-        in_specs=[pay_spec] + [bins_spec] * 4,
+        in_specs=[pay_spec]
+        + [bins_spec] * len(places)
+        + [pl.BlockSpec((blocks, SUM_ROWS, LANES), lambda j: (0, 0, 0))] * len(before),
         out_specs=pl.BlockSpec((blocks, SUM_ROWS, LANES), lambda j: (0, 0, 0)),
         cost_estimate=pl.CostEstimate(flops=flops, bytes_accessed=1 << 21, transcendentals=0),
         compiler_params=pltpu.CompilerParams(vmem_limit_bytes=32 << 20),
         name="left_sums",
-    )(pay, *pieces)
+    )(pay, *pieces, *before)
 
 
 def wire_kernel(mine, theirs, out):
@@ -272,8 +280,11 @@
     pieces[1] = lax.ppermute(pieces[1], "zl", swap)
     pieces[2] = lax.ppermute(pieces[2], "xh", swap)
     pieces[3] = lax.ppermute(pieces[3], ("xh", "zl"), [(0, 3), (1, 2), (2, 1), (3, 0)])
-    theirs = lax.ppermute(local_sums(1, pay, pieces), "c", swap)
-    sums = to_wire(local_sums(0, pay, pieces), theirs)
+    near = [local_sums(core, (0,), pay, pieces[:1]) for core in range(2)]
+    near, pieces[1:] = lax.optimization_barrier((near, pieces[1:]))
+    theirs = local_sums(1, (1, 2, 3), pay, pieces[1:], (near[1],))
+    theirs = lax.ppermute(theirs, "c", swap)
+    sums = to_wire(local_sums(0, (1, 2, 3), pay, pieces[1:], (near[0],)), theirs)
     parts = lax.all_to_all(sums, "zh", 0, 0, tiled=True)
     gain, best = final_scores(parts, lax.axis_size(ALL))
     best = lax.all_to_all(best, ALL, 0, 0, tiled=True)

time: 96.7 us -> 93.2 us (0.964)
  waiting for transfers between devices: 15.8 us -> 11.9 us
    all_to_all x1, waiting for transfers between devices: 0.01 us -> 9.31 us  [on_device(): pay = lax.all_to_all(pay, NEAR, 0, 0, tiled=True)]
    ppermute x1, waiting for transfers between devices: 9.15 us -> 0.01 us  [on_device(): pieces[1] = lax.ppermute(pieces[1], 'zl', swap)]
    ppermute x1, waiting for transfers between devices: 4.77 us -> 2.61 us  [on_device(): lax.ppermute(pieces[3], ('xh', 'zl'), [(0, 3), (1, 2), (2, 1), (3, 0)])]
    ppermute x1, waiting for transfers between devices: 1.88 us -> 0.01 us  [on_device(): pieces[2] = lax.ppermute(pieces[2], 'xh', swap)]
    pallas_call x2 -> x4, Pallas kernels: 14.2 us -> 14.6 us  [local_sums(): pl.pallas_call(functools.partial(sums_kernel, places), out_shape=jax.Shap...]
  transfers between devices with their start and end apart: 5 -> 5, of which waited for: 3 -> 2; matrix products, arithmetic and copies ran while one was open for 0% -> 0% of each run, Pallas kernels for 8% -> 11%
where the time goes in v6:
time: 93.2 us; the launch traced here: 93 us
  blocking collectives  44.9 us (48%)
  Pallas kernels  19 us (20%)
  starting transfers between devices  15.6 us (17%)
  waiting for transfers between devices  11.9 us (13%)
    all_to_all x1, blocking collectives, on_device(): parts = lax.all_to_all(sums, 'zh', 0, 0, tiled=True)  24.4 us
    all_to_all x1, blocking collectives, on_device(): best = lax.all_to_all(best, ALL, 0, 0, tiled=True)  20.6 us
    pallas_call x4, Pallas kernels, local_sums(): pl.pallas_call(functools.partial(sums_kernel, places), out_shape=jax.Shap...  14.6 us
    all_to_all x1, waiting for transfers between devices, on_device(): pay = lax.all_to_all(pay, NEAR, 0, 0, tiled=True)  9.31 us
    all_to_all x1, starting transfers between devices, on_device(): pay = lax.all_to_all(pay, NEAR, 0, 0, tiled=True)  9.24 us
    ppermute x1, starting transfers between devices, on_device(): pieces[2] = lax.ppermute(pieces[2], 'xh', swap)  2.73 us
    ppermute x1, waiting for transfers between devices, on_device(): lax.ppermute(pieces[3], ('xh', 'zl'), [(0, 3), (1, 2), (2, 1), (3, 0)])  2.61 us
    ppermute x1, starting transfers between devices, on_device(): theirs = lax.ppermute(theirs, 'c', swap)  2.14 us
  transfers between devices with their start and end apart: 5, of which 2 were waited for; matrix products, arithmetic and copies ran while one was open for 0% of the time, Pallas kernels for 11%

profile of v6, /device:TPU:1, one launch (start us, length us, event | category | flops | bytes accessed | tf_op | source)
XLA Modules:
  0.0 93.0 jit_solution(8609859416169598776)
XLA Ops:
  0.6 0.0 copy-start
  0.6 1.9 %payload.1 = bf16[32,104,128]{2,1,0:T(8,128)(2,1)} custom-call(bf16[32,384]{1,0:T(8,128)(2,1)} %grad_hbm.1, bf16[3,128]{1,0:T(4,128)(2,1)} %bitcast.7, s32[24,128]{1,0:T(8,128)} %bitcast.6), custom_call_target="tpu_custom_call" | custom-call | tf_op jit(solution)/shard_map/payload/pallas_call | solution.py:70
  2.5 9.2 %all-to-all-start = ((bf16[32,104,128]{2,1,0:T(8,128)(2,1)}), bf16[32,104,128]{2,1,0:T(8,128)(2,1)S(1)}, u32[]{:S(2)}, u32[]{:S(2)}) async-start(bf16[32,104,128]{2,1,0:T(8,128)(2,1)} %payload.1), calls=%async_computation | async-start | bytes 1703936 | tf_op jit(solution)/shard_map/all_to_all | solution.py:278
  11.8 0.0 copy-done
  11.8 1.0 %cut_bins.1 = (bf16[2,4,4,3072]{3,2,1,0:T(4,128)(2,1)S(1)}, bf16[2,4,4,3072]{3,2,1,0:T(4,128)(2,1)S(1)}, bf16[2,4,4,3072]{3,2,1,0:T(4,128)(2,1)S(1)}, bf16[2,4,4,3072]{3,2,1,0:T(4,128)(2,1)S(1)}) custom-call(s32[128,3072]{1,0:T(8,128)S(1)} %copy-done), custom_call_target="tpu_custom_call" | custom-call | tf_op jit(solution)/shard_map/cut_bins/pallas_call | solution.py:111
  12.8 1.3 %collective-permute-start = (bf16[2,4,4,3072]{3,2,1,0:T(4,128)(2,1)S(1)}, bf16[2,4,4,3072]{3,2,1,0:T(4,128)(2,1)S(1)}, u32[]{:S(2)}, u32[]{:S(2)}) collective-permute-start(bf16[2,4,4,3072]{3,2,1,0:T(4,128)(2,1)S(1)} %get-tuple-element.14), channel_id=1, source_target_pairs={{0,16},{16,0},{1,17},{17,1},{2,18},{18,2},{3,19},{19,3},{4,20},{20... | collective-permute-start | bytes 589832 | tf_op jit(solution)/shard_map/ppermute | solution.py:280
  14.2 2.7 %collective-permute-start.1 = (bf16[2,4,4,3072]{3,2,1,0:T(4,128)(2,1)S(1)}, bf16[2,4,4,3072]{3,2,1,0:T(4,128)(2,1)S(1)}, u32[]{:S(2)}, u32[]{:S(2)}) collective-permute-start(bf16[2,4,4,3072]{3,2,1,0:T(4,128)(2,1)S(1)} %get-tuple-element.15), channel_id=1, source_target_pairs={{0,128},{128,0},{1,129},{129,1},{2,130},{130,2},{3,131},{131,3},{4... | collective-permute-start | bytes 589832 | tf_op jit(solution)/shard_map/ppermute | solution.py:281
  16.9 0.2 collective-permute-start.2
  17.1 9.3 %all-to-all-done.pay = bf16[32,104,128]{2,1,0:T(8,128)(2,1)S(1)} async-done(((bf16[32,104,128]{2,1,0:T(8,128)(2,1)}), bf16[32,104,128]{2,1,0:T(8,128)(2,1)S(1)}, u32[]{:S(2)}, u32[]{:S(2)}) %all-to-all-start) | async-done | bytes 852000 | tf_op jit(solution)/shard_map/all_to_all | solution.py:278
  26.4 1.9 %left_sums.5.refs_3_ = f32[4,264,256]{2,1,0:T(8,128)S(1)} custom-call(bf16[32,104,128]{2,1,0:T(8,128)(2,1)S(1)} %all-to-all-done.pay, bf16[2,4,4,3072]{3,2,1,0:T(4,128)(2,1)S(1)} %get-tuple-element.13.refs_0_), custom_call_target="tpu_custom_call" | custom-call | flops 1660944384 | bytes 2097152 | tf_op jit(solution)/shard_map/left_sums/pallas_call | solution.py:187
  28.3 1.9 %left_sums.4.refs_3_ = f32[4,264,256]{2,1,0:T(8,128)S(1)} custom-call(bf16[32,104,128]{2,1,0:T(8,128)(2,1)S(1)} %all-to-all-done.pay, bf16[2,4,4,3072]{3,2,1,0:T(4,128)(2,1)S(1)} %get-tuple-element.13.refs_0_), custom_call_target="tpu_custom_call" | custom-call | flops 1660944384 | bytes 2097152 | tf_op jit(solution)/shard_map/left_sums/pallas_call | solution.py:187
  30.3 0.0 collective-permute-done.refs_0_
  30.3 0.0 collective-permute-done.1.refs_1_
  30.3 2.6 %collective-permute-done.2.refs_2_ = bf16[2,4,4,3072]{3,2,1,0:T(4,128)(2,1)S(1)} collective-permute-done((bf16[2,4,4,3072]{3,2,1,0:T(4,128)(2,1)S(1)}, bf16[2,4,4,3072]{3,2,1,0:T(4,128)(2,1)S(1)}, u32[]{:S(2)}, u32[]{:S(2)}) %collective-permute-start.2) | collective-permute-done | bytes 196640 | tf_op jit(solution)/shard_map/ppermute | solution.py:282
  32.9 5.4 %left_sums.7 = f32[4,264,256]{2,1,0:T(8,128)S(1)} custom-call(bf16[32,104,128]{2,1,0:T(8,128)(2,1)S(1)} %all-to-all-done.pay, bf16[2,4,4,3072]{3,2,1,0:T(4,128)(2,1)S(1)} %collective-permute-done.refs_0_, bf16[2,4,4,3072]{3,2,1,0:T(4,128)(2,1)S(1)} %collective-permute-done.1.refs_1_, bf16[2,4,4,3072]{3,2,1,0:T(4,128)(2,1)S(1)} %collective-permute-done.2.refs_2_, ...), custom_call_target="tpu_custom_call" | custom-call | flops 4982833152 | bytes 2097152 | tf_op jit(solution)/shard_map/left_sums/pallas_call | solution.py:187
  38.3 2.1 %collective-permute-start.3 = (f32[4,264,256]{2,1,0:T(8,128)S(1)}, f32[4,264,256]{2,1,0:T(8,128)S(1)}, u32[]{:S(2)}, u32[]{:S(2)}) collective-permute-start(f32[4,264,256]{2,1,0:T(8,128)S(1)} %left_sums.7), channel_id=1, source_target_pairs={{0,8},{8,0},{1,9},{9,1},{2,10},{10,2},{3,11},{11,3},{4,12},{12,4},... | collective-permute-start | bytes 3244040 | tf_op jit(solution)/shard_map/ppermute | solution.py:286
  40.4 5.4 %left_sums.6.mine = f32[4,264,256]{2,1,0:T(8,128)S(1)} custom-call(bf16[32,104,128]{2,1,0:T(8,128)(2,1)S(1)} %all-to-all-done.pay, bf16[2,4,4,3072]{3,2,1,0:T(4,128)(2,1)S(1)} %collective-permute-done.refs_0_, bf16[2,4,4,3072]{3,2,1,0:T(4,128)(2,1)S(1)} %collective-permute-done.1.refs_1_, bf16[2,4,4,3072]{3,2,1,0:T(4,128)(2,1)S(1)} %collective-permute-done.2.refs_2_, ...), custom_call_target="tpu_custom_call" | custom-call | flops 4982833152 | bytes 2097152 | tf_op jit(solution)/shard_map/left_sums/pallas_call | solution.py:187
  45.8 0.0 collective-permute-done.3.theirs
  45.8 0.5 to_wire.1
  46.3 24.4 %all_to_all.19.refs_0_ = s16[4,288,256]{2,1,0:T(8,128)(2,1)S(1)} all-to-all(s16[4,288,256]{2,1,0:T(8,128)(2,1)S(1)} %to_wire.1), channel_id=1, replica_groups=mesh['xh'=2,'zh'=4,'zl'=2,'c'=2,'y'=4,'xl'=2] {'zh'}, dimensions={0} | all-to-all | bytes 1179648 | tf_op jit(solution)/shard_map/all_to_all | solution.py:288
  70.7 0.9 %split_scores.1 = (f32[4,512]{1,0:T(4,128)}, f32[256,8]{1,0:T(8,128)S(1)}) custom-call(s16[4,288,256]{2,1,0:T(8,128)(2,1)S(1)} %all_to_all.19.refs_0_), custom_call_target="tpu_custom_call" | custom-call | tf_op jit(solution)/shard_map/split_scores/pallas_call | solution.py:264
  71.6 20.6 %all_to_all.20 = f32[256,1,8]{2,1,0:T(1,128)S(1)} all-to-all(f32[256,1,8]{2,1,0:T(1,128)S(1)} %bitcast.5), channel_id=1, replica_groups=mesh['xh'=2,'zh'=4,'zl'=2,'c'=2,'y'=4,'xl'=2] {'xh','zh','zl','c','y','xl'}, dimensions={0} | all-to-all | bytes 16384 | tf_op jit(solution)/shard_map/all_to_all | solution.py:290
  92.2 0.8 reduce_max.9
Async XLA Ops:
  0.6 11.2 %copy-start = (s32[128,3072]{1,0:T(8,128)S(1)}, s32[128,3072]{1,0:T(8,128)}, u32[]{:S(2)}) copy-start(s32[128,3072]{1,0:T(8,128)} %bins_hbm.1) | copy-start | bytes 4718596
  2.5 23.8 %all-to-all-start = ((bf16[32,104,128]{2,1,0:T(8,128)(2,1)}), bf16[32,104,128]{2,1,0:T(8,128)(2,1)S(1)}, u32[]{:S(2)}, u32[]{:S(2)}) async-start(bf16[32,104,128]{2,1,0:T(8,128)(2,1)} %payload.1), calls=%async_computation | async-start | bytes 1703936 | tf_op jit(solution)/shard_map/all_to_all | solution.py:278
  12.8 17.4 %collective-permute-start = (bf16[2,4,4,3072]{3,2,1,0:T(4,128)(2,1)S(1)}, bf16[2,4,4,3072]{3,2,1,0:T(4,128)(2,1)S(1)}, u32[]{:S(2)}, u32[]{:S(2)}) collective-permute-start(bf16[2,4,4,3072]{3,2,1,0:T(4,128)(2,1)S(1)} %get-tuple-element.14), channel_id=1, source_target_pairs={{0,16},{16,0},{1,17},{17,1},{2,18},{18,2},{3,19},{19,3},{4,20},{20... | collective-permute-start | bytes 589832 | tf_op jit(solution)/shard_map/ppermute | solution.py:280
  14.2 16.1 %collective-permute-start.1 = (bf16[2,4,4,3072]{3,2,1,0:T(4,128)(2,1)S(1)}, bf16[2,4,4,3072]{3,2,1,0:T(4,128)(2,1)S(1)}, u32[]{:S(2)}, u32[]{:S(2)}) collective-permute-start(bf16[2,4,4,3072]{3,2,1,0:T(4,128)(2,1)S(1)} %get-tuple-element.15), channel_id=1, source_target_pairs={{0,128},{128,0},{1,129},{129,1},{2,130},{130,2},{3,131},{131,3},{4... | collective-permute-start | bytes 589832 | tf_op jit(solution)/shard_map/ppermute | solution.py:281
  16.9 16.0 %collective-permute-start.2 = (bf16[2,4,4,3072]{3,2,1,0:T(4,128)(2,1)S(1)}, bf16[2,4,4,3072]{3,2,1,0:T(4,128)(2,1)S(1)}, u32[]{:S(2)}, u32[]{:S(2)}) collective-permute-start(bf16[2,4,4,3072]{3,2,1,0:T(4,128)(2,1)S(1)} %get-tuple-element.16), channel_id=1, source_target_pairs={{0,144},{16,128},{128,16},{144,0},{1,145},{17,129},{129,17},{145,1... | collective-permute-start | bytes 589832 | tf_op jit(solution)/shard_map/ppermute | solution.py:282
  38.3 7.5 %collective-permute-start.3 = (f32[4,264,256]{2,1,0:T(8,128)S(1)}, f32[4,264,256]{2,1,0:T(8,128)S(1)}, u32[]{:S(2)}, u32[]{:S(2)}) collective-permute-start(f32[4,264,256]{2,1,0:T(8,128)S(1)} %left_sums.7), channel_id=1, source_target_pairs={{0,8},{8,0},{1,9},{9,1},{2,10},{10,2},{3,11},{11,3},{4,12},{12,4},... | collective-permute-start | bytes 3244040 | tf_op jit(solution)/shard_map/ppermute | solution.py:286

commit v7 on v6

--- a/solution.py
+++ b/solution.py
@@ -280,11 +280,13 @@
     pieces[1] = lax.ppermute(pieces[1], "zl", swap)
     pieces[2] = lax.ppermute(pieces[2], "xh", swap)
     pieces[3] = lax.ppermute(pieces[3], ("xh", "zl"), [(0, 3), (1, 2), (2, 1), (3, 0)])
-    near = [local_sums(core, (0,), pay, pieces[:1]) for core in range(2)]
-    near, pieces[1:] = lax.optimization_barrier((near, pieces[1:]))
+    near = [None, local_sums(1, (0,), pay, pieces[:1])]
+    near[1], pieces[1] = lax.optimization_barrier((near[1], pieces[1]))
+    near[0] = local_sums(0, (0, 1), pay, pieces[:2])
+    near, pieces[2:] = lax.optimization_barrier((near, pieces[2:]))
     theirs = local_sums(1, (1, 2, 3), pay, pieces[1:], (near[1],))
     theirs = lax.ppermute(theirs, "c", swap)
-    sums = to_wire(local_sums(0, (1, 2, 3), pay, pieces[1:], (near[0],)), theirs)
+    sums = to_wire(local_sums(0, (2, 3), pay, pieces[2:], (near[0],)), theirs)
     parts = lax.all_to_all(sums, "zh", 0, 0, tiled=True)
     gain, best = final_scores(parts, lax.axis_size(ALL))
     best = lax.all_to_all(best, ALL, 0, 0, tiled=True)

time: 93.2 us -> 91.8 us (0.985)
  waiting for transfers between devices: 11.9 us -> 10.2 us
  starting transfers between devices: 15.6 us -> 16.6 us
    ppermute x1, waiting for transfers between devices: 2.61 us -> 0.9 us  [on_device(): lax.ppermute(pieces[3], ('xh', 'zl'), [(0, 3), (1, 2), (2, 1), (3, 0)])]
    ppermute x1, starting transfers between devices: 2.14 us -> 3.08 us  [on_device(): theirs = lax.ppermute(theirs, 'c', swap)]
where the time goes in v7:
time: 91.8 us; the launch traced here: 91.6 us
  blocking collectives  44.3 us (48%)
  Pallas kernels  19 us (21%)
  starting transfers between devices  16.6 us (18%)
  waiting for transfers between devices  10.2 us (11%)
    all_to_all x1, blocking collectives, on_device(): parts = lax.all_to_all(sums, 'zh', 0, 0, tiled=True)  23.9 us
    all_to_all x1, blocking collectives, on_device(): best = lax.all_to_all(best, ALL, 0, 0, tiled=True)  20.4 us
    pallas_call x4, Pallas kernels, local_sums(): pl.pallas_call(functools.partial(sums_kernel, places), out_shape=jax.Shap...  14.6 us
    all_to_all x1, waiting for transfers between devices, on_device(): pay = lax.all_to_all(pay, NEAR, 0, 0, tiled=True)  9.31 us
    all_to_all x1, starting transfers between devices, on_device(): pay = lax.all_to_all(pay, NEAR, 0, 0, tiled=True)  9.24 us
    ppermute x1, starting transfers between devices, on_device(): theirs = lax.ppermute(theirs, 'c', swap)  3.08 us
    ppermute x1, starting transfers between devices, on_device(): pieces[2] = lax.ppermute(pieces[2], 'xh', swap)  2.73 us
    pallas_call x1, Pallas kernels, payload(): pl.pallas_call(pay_kernel, out_shape=jax.ShapeDtypeStruct((near, pay_rows...  1.89 us
  transfers between devices with their start and end apart: 5, of which 2 were waited for; matrix products, arithmetic and copies ran while one was open for 0% of the time, Pallas kernels for 11%

profile of v7, /device:TPU:1, one launch (start us, length us, event | category | flops | bytes accessed | tf_op | source)
XLA Modules:
  0.0 91.6 jit_solution(579708325821163611)
XLA Ops:
  0.6 0.0 copy-start
  0.6 1.9 %payload.1 = bf16[32,104,128]{2,1,0:T(8,128)(2,1)} custom-call(bf16[32,384]{1,0:T(8,128)(2,1)} %grad_hbm.1, bf16[3,128]{1,0:T(4,128)(2,1)} %bitcast.7, s32[24,128]{1,0:T(8,128)} %bitcast.6), custom_call_target="tpu_custom_call" | custom-call | tf_op jit(solution)/shard_map/payload/pallas_call | solution.py:70
  2.5 9.2 %all-to-all-start = ((bf16[32,104,128]{2,1,0:T(8,128)(2,1)}), bf16[32,104,128]{2,1,0:T(8,128)(2,1)S(1)}, u32[]{:S(2)}, u32[]{:S(2)}) async-start(bf16[32,104,128]{2,1,0:T(8,128)(2,1)} %payload.1), calls=%async_computation | async-start | bytes 1703936 | tf_op jit(solution)/shard_map/all_to_all | solution.py:278
  11.8 0.0 copy-done
  11.8 1.0 %cut_bins.1 = (bf16[2,4,4,3072]{3,2,1,0:T(4,128)(2,1)S(1)}, bf16[2,4,4,3072]{3,2,1,0:T(4,128)(2,1)S(1)}, bf16[2,4,4,3072]{3,2,1,0:T(4,128)(2,1)S(1)}, bf16[2,4,4,3072]{3,2,1,0:T(4,128)(2,1)S(1)}) custom-call(s32[128,3072]{1,0:T(8,128)S(1)} %copy-done), custom_call_target="tpu_custom_call" | custom-call | tf_op jit(solution)/shard_map/cut_bins/pallas_call | solution.py:111
  12.8 1.3 %collective-permute-start = (bf16[2,4,4,3072]{3,2,1,0:T(4,128)(2,1)S(1)}, bf16[2,4,4,3072]{3,2,1,0:T(4,128)(2,1)S(1)}, u32[]{:S(2)}, u32[]{:S(2)}) collective-permute-start(bf16[2,4,4,3072]{3,2,1,0:T(4,128)(2,1)S(1)} %get-tuple-element.15), channel_id=1, source_target_pairs={{0,16},{16,0},{1,17},{17,1},{2,18},{18,2},{3,19},{19,3},{4,20},{20... | collective-permute-start | bytes 589832 | tf_op jit(solution)/shard_map/ppermute | solution.py:280
  14.2 2.7 %collective-permute-start.1 = (bf16[2,4,4,3072]{3,2,1,0:T(4,128)(2,1)S(1)}, bf16[2,4,4,3072]{3,2,1,0:T(4,128)(2,1)S(1)}, u32[]{:S(2)}, u32[]{:S(2)}) collective-permute-start(bf16[2,4,4,3072]{3,2,1,0:T(4,128)(2,1)S(1)} %get-tuple-element.18), channel_id=1, source_target_pairs={{0,128},{128,0},{1,129},{129,1},{2,130},{130,2},{3,131},{131,3},{4... | collective-permute-start | bytes 589832 | tf_op jit(solution)/shard_map/ppermute | solution.py:281
  16.9 0.2 collective-permute-start.2
  17.1 9.3 %all-to-all-done.pay = bf16[32,104,128]{2,1,0:T(8,128)(2,1)S(1)} async-done(((bf16[32,104,128]{2,1,0:T(8,128)(2,1)}), bf16[32,104,128]{2,1,0:T(8,128)(2,1)S(1)}, u32[]{:S(2)}, u32[]{:S(2)}) %all-to-all-start) | async-done | bytes 852000 | tf_op jit(solution)/shard_map/all_to_all | solution.py:278
  26.4 1.9 %left_sums.4.refs_3_ = f32[4,264,256]{2,1,0:T(8,128)S(1)} custom-call(bf16[32,104,128]{2,1,0:T(8,128)(2,1)S(1)} %all-to-all-done.pay, bf16[2,4,4,3072]{3,2,1,0:T(4,128)(2,1)S(1)} %get-tuple-element.14.refs_0_), custom_call_target="tpu_custom_call" | custom-call | flops 1660944384 | bytes 2097152 | tf_op jit(solution)/shard_map/left_sums/pallas_call | solution.py:187
  28.3 0.0 collective-permute-done.refs_1_.refs_0_
  28.3 3.6 %left_sums.5.refs_2_ = f32[4,264,256]{2,1,0:T(8,128)S(1)} custom-call(bf16[32,104,128]{2,1,0:T(8,128)(2,1)S(1)} %all-to-all-done.pay, bf16[2,4,4,3072]{3,2,1,0:T(4,128)(2,1)S(1)} %get-tuple-element.14.refs_0_, bf16[2,4,4,3072]{3,2,1,0:T(4,128)(2,1)S(1)} %collective-permute-done.refs_1_.refs_0_), custom_call_target="tpu_custom_call" | custom-call | flops 3321888768 | bytes 2097152 | tf_op jit(solution)/shard_map/left_sums/pallas_call | solution.py:187
  32.0 0.0 collective-permute-done.1.refs_0_.refs_1_
  32.0 0.9 collective-permute-done.2.refs_1_.refs_2_
  32.9 5.4 %left_sums.7 = f32[4,264,256]{2,1,0:T(8,128)S(1)} custom-call(bf16[32,104,128]{2,1,0:T(8,128)(2,1)S(1)} %all-to-all-done.pay, bf16[2,4,4,3072]{3,2,1,0:T(4,128)(2,1)S(1)} %collective-permute-done.refs_1_.refs_0_, bf16[2,4,4,3072]{3,2,1,0:T(4,128)(2,1)S(1)} %collective-permute-done.1.refs_0_.refs_1_, ...), custom_call_target="tpu_custom_call" | custom-call | flops 4982833152 | bytes 2097152 | tf_op jit(solution)/shard_map/left_sums/pallas_call | solution.py:187
  38.3 3.1 %collective-permute-start.3 = (f32[4,264,256]{2,1,0:T(8,128)S(1)}, f32[4,264,256]{2,1,0:T(8,128)S(1)}, u32[]{:S(2)}, u32[]{:S(2)}) collective-permute-start(f32[4,264,256]{2,1,0:T(8,128)S(1)} %left_sums.7), channel_id=1, source_target_pairs={{0,8},{8,0},{1,9},{9,1},{2,10},{10,2},{3,11},{11,3},{4,12},{12,4},... | collective-permute-start | bytes 3244040 | tf_op jit(solution)/shard_map/ppermute | solution.py:288
  41.3 3.6 %left_sums.6.mine = f32[4,264,256]{2,1,0:T(8,128)S(1)} custom-call(bf16[32,104,128]{2,1,0:T(8,128)(2,1)S(1)} %all-to-all-done.pay, bf16[2,4,4,3072]{3,2,1,0:T(4,128)(2,1)S(1)} %collective-permute-done.1.refs_0_.refs_1_, bf16[2,4,4,3072]{3,2,1,0:T(4,128)(2,1)S(1)} %collective-permute-done.2.refs_1_.refs_2_, f32[4,264,256]{2,1,0:T(8,128)S(1)} %left_sums.5.refs_2_), custom_call_target="tpu_custom_call" | custom-call | flops 3321888768 | bytes 2097152 | tf_op jit(solution)/shard_map/left_sums/pallas_call | solution.py:187
  45.0 0.0 collective-permute-done.3.theirs
  45.0 0.5 to_wire.1
  45.5 23.9 %all_to_all.19.refs_0_ = s16[4,288,256]{2,1,0:T(8,128)(2,1)S(1)} all-to-all(s16[4,288,256]{2,1,0:T(8,128)(2,1)S(1)} %to_wire.1), channel_id=1, replica_groups=mesh['xh'=2,'zh'=4,'zl'=2,'c'=2,'y'=4,'xl'=2] {'zh'}, dimensions={0} | all-to-all | bytes 1179648 | tf_op jit(solution)/shard_map/all_to_all | solution.py:290
  69.5 0.9 %split_scores.1 = (f32[4,512]{1,0:T(4,128)}, f32[256,8]{1,0:T(8,128)S(1)}) custom-call(s16[4,288,256]{2,1,0:T(8,128)(2,1)S(1)} %all_to_all.19.refs_0_), custom_call_target="tpu_custom_call" | custom-call | tf_op jit(solution)/shard_map/split_scores/pallas_call | solution.py:264
  70.4 20.4 %all_to_all.20 = f32[256,1,8]{2,1,0:T(1,128)S(1)} all-to-all(f32[256,1,8]{2,1,0:T(1,128)S(1)} %bitcast.5), channel_id=1, replica_groups=mesh['xh'=2,'zh'=4,'zl'=2,'c'=2,'y'=4,'xl'=2] {'xh','zh','zl','c','y','xl'}, dimensions={0} | all-to-all | bytes 16384 | tf_op jit(solution)/shard_map/all_to_all | solution.py:292
  90.8 0.8 reduce_max.9
Async XLA Ops:
  0.6 11.2 %copy-start = (s32[128,3072]{1,0:T(8,128)S(1)}, s32[128,3072]{1,0:T(8,128)}, u32[]{:S(2)}) copy-start(s32[128,3072]{1,0:T(8,128)} %bins_hbm.1) | copy-start | bytes 4718596
  2.5 23.8 %all-to-all-start = ((bf16[32,104,128]{2,1,0:T(8,128)(2,1)}), bf16[32,104,128]{2,1,0:T(8,128)(2,1)S(1)}, u32[]{:S(2)}, u32[]{:S(2)}) async-start(bf16[32,104,128]{2,1,0:T(8,128)(2,1)} %payload.1), calls=%async_computation | async-start | bytes 1703936 | tf_op jit(solution)/shard_map/all_to_all | solution.py:278
  12.8 15.5 %collective-permute-start = (bf16[2,4,4,3072]{3,2,1,0:T(4,128)(2,1)S(1)}, bf16[2,4,4,3072]{3,2,1,0:T(4,128)(2,1)S(1)}, u32[]{:S(2)}, u32[]{:S(2)}) collective-permute-start(bf16[2,4,4,3072]{3,2,1,0:T(4,128)(2,1)S(1)} %get-tuple-element.15), channel_id=1, source_target_pairs={{0,16},{16,0},{1,17},{17,1},{2,18},{18,2},{3,19},{19,3},{4,20},{20... | collective-permute-start | bytes 589832 | tf_op jit(solution)/shard_map/ppermute | solution.py:280
  14.2 17.8 %collective-permute-start.1 = (bf16[2,4,4,3072]{3,2,1,0:T(4,128)(2,1)S(1)}, bf16[2,4,4,3072]{3,2,1,0:T(4,128)(2,1)S(1)}, u32[]{:S(2)}, u32[]{:S(2)}) collective-permute-start(bf16[2,4,4,3072]{3,2,1,0:T(4,128)(2,1)S(1)} %get-tuple-element.18), channel_id=1, source_target_pairs={{0,128},{128,0},{1,129},{129,1},{2,130},{130,2},{3,131},{131,3},{4... | collective-permute-start | bytes 589832 | tf_op jit(solution)/shard_map/ppermute | solution.py:281
  16.9 16.0 %collective-permute-start.2 = (bf16[2,4,4,3072]{3,2,1,0:T(4,128)(2,1)S(1)}, bf16[2,4,4,3072]{3,2,1,0:T(4,128)(2,1)S(1)}, u32[]{:S(2)}, u32[]{:S(2)}) collective-permute-start(bf16[2,4,4,3072]{3,2,1,0:T(4,128)(2,1)S(1)} %get-tuple-element.19), channel_id=1, source_target_pairs={{0,144},{16,128},{128,16},{144,0},{1,145},{17,129},{129,17},{145,1... | collective-permute-start | bytes 589832 | tf_op jit(solution)/shard_map/ppermute | solution.py:282
  38.3 6.7 %collective-permute-start.3 = (f32[4,264,256]{2,1,0:T(8,128)S(1)}, f32[4,264,256]{2,1,0:T(8,128)S(1)}, u32[]{:S(2)}, u32[]{:S(2)}) collective-permute-start(f32[4,264,256]{2,1,0:T(8,128)S(1)} %left_sums.7), channel_id=1, source_target_pairs={{0,8},{8,0},{1,9},{9,1},{2,10},{10,2},{3,11},{11,3},{4,12},{12,4},... | collective-permute-start | bytes 3244040 | tf_op jit(solution)/shard_map/ppermute | solution.py:288

commit v8 on v7

--- a/solution.py
+++ b/solution.py
@@ -198,41 +198,40 @@
     )(pay, *pieces, *before)
 
 
-def wire_kernel(mine, theirs, out):
-    sums = mine[0] + theirs[0]
-    grads = sums[0:GRAD_ROWS].reshape(NODES, OUTPUTS, LANES)
-    largest = jnp.max(jnp.abs(grads), axis=1)
-    octave = jnp.ceil(jnp.log2(jnp.maximum(largest, 1e-30)) * STEPS + 0.01)
-    factor = TOP * jnp.exp2(octave * (-1.0 / STEPS))
-    scaled = jnp.floor(grads * factor[:, None, :] + 0.5).reshape(GRAD_ROWS, LANES)
-    out[0, 0:GRAD_ROWS, :] = scaled.astype(jnp.int32).astype(jnp.int16)
-    units = sums[GRAD_ROWS:SUM_ROWS] * HESS_UNIT
-    high = jnp.floor(units * (1.0 / HESS_SPLIT))
-    low = units - high * HESS_SPLIT
-    rest = jnp.concatenate([octave, high, low, jnp.zeros_like(low)], axis=0)
-    out[0, GRAD_ROWS:WIRE_ROWS, :] = rest.astype(jnp.int32).astype(jnp.int16)
-
-
-def to_wire(mine, theirs):
-    blocks = mine.shape[0]
-    sums_spec = pl.BlockSpec((1, SUM_ROWS, LANES), lambda j: (j, 0, 0))
-    return pl.pallas_call(
-        wire_kernel,
-        out_shape=jax.ShapeDtypeStruct((blocks, WIRE_ROWS, LANES), jnp.int16),
-        grid=(blocks,),
-        in_specs=[sums_spec] * 2,
-        out_specs=pl.BlockSpec((1, WIRE_ROWS, LANES), lambda j: (j, 0, 0)),
+def wire_kernel(order, mine, theirs, *outs):
+    zh, depth = lax.axis_index("zh"), mine.shape[0]
+    for d, out in zip(order, outs):
+        keeper = (zh + d) % depth
+        sums = mine[keeper] + theirs[keeper]
+        grads = sums[0:GRAD_ROWS].reshape(NODES, OUTPUTS, LANES)
+        largest = jnp.max(jnp.abs(grads), axis=1)
+        octave = jnp.ceil(jnp.log2(jnp.maximum(largest, 1e-30)) * STEPS + 0.01)
+        factor = TOP * jnp.exp2(octave * (-1.0 / STEPS))
+        scaled = jnp.floor(grads * factor[:, None, :] + 0.5).reshape(GRAD_ROWS, LANES)
+        out[0:GRAD_ROWS, :] = scaled.astype(jnp.int32).astype(jnp.int16)
+        units = sums[GRAD_ROWS:SUM_ROWS] * HESS_UNIT
+        high = jnp.floor(units * (1.0 / HESS_SPLIT))
+        low = units - high * HESS_SPLIT
+        rest = jnp.concatenate([octave, high, low, jnp.zeros_like(low)], axis=0)
+        out[GRAD_ROWS:WIRE_ROWS, :] = rest.astype(jnp.int32).astype(jnp.int16)
+
+
+def to_wire(order, mine, theirs):
+    return pl.pallas_call(
+        functools.partial(wire_kernel, order),
+        out_shape=(jax.ShapeDtypeStruct((WIRE_ROWS, LANES), jnp.int16),) * len(order),
         compiler_params=pltpu.CompilerParams(vmem_limit_bytes=24 << 20),
         name="to_wire",
     )(mine, theirs)
 
 
-def score_kernel(devices, parts, gain_out, best_out):
+def score_kernel(devices, *refs):
+    parts, (gain_out, best_out) = refs[:-2], refs[-2:]
     left = jnp.zeros((NODES, OUTPUTS, LANES), f32)
     left_hess = jnp.zeros((NODES, LANES), f32)
-    for s in range(parts.shape[0]):
-        scaled = parts[s, 0:GRAD_ROWS, :].astype(jnp.int32).astype(f32)
-        rest = parts[s, GRAD_ROWS:WIRE_ROWS, :].astype(jnp.int32).astype(f32)
+    for part in parts:
+        scaled = part[0:GRAD_ROWS, :].astype(jnp.int32).astype(f32)
+        rest = part[GRAD_ROWS:WIRE_ROWS, :].astype(jnp.int32).astype(f32)
         unit = jnp.exp2(rest[0:NODES] * (1.0 / STEPS)) * (1.0 / TOP)
         left = left + scaled.reshape(NODES, OUTPUTS, LANES) * unit[:, None, :]
         left_hess = left_hess + (
@@ -262,14 +261,14 @@
 
 def final_scores(parts, devices):
     return pl.pallas_call(
-        lambda *refs: score_kernel(devices, *refs),
+        functools.partial(score_kernel, devices),
         out_shape=(
             jax.ShapeDtypeStruct((OWNED, NODES * BINS), f32),
             jax.ShapeDtypeStruct((devices, NODES), f32),
         ),
         compiler_params=pltpu.CompilerParams(vmem_limit_bytes=48 << 20),
         name="split_scores",
-    )(parts)
+    )(*parts)
 
 
 def on_device(bin_index, gradient, hessian, row_node):
@@ -286,8 +285,13 @@
     near, pieces[2:] = lax.optimization_barrier((near, pieces[2:]))
     theirs = local_sums(1, (1, 2, 3), pay, pieces[1:], (near[1],))
     theirs = lax.ppermute(theirs, "c", swap)
-    sums = to_wire(local_sums(0, (2, 3), pay, pieces[2:], (near[0],)), theirs)
-    parts = lax.all_to_all(sums, "zh", 0, 0, tiled=True)
+    mine = local_sums(0, (2, 3), pay, pieces[2:], (near[0],))
+    depth = lax.axis_size("zh")
+    order = (2, 1, 3, 0)
+    parts = [
+        lax.ppermute(part, "zh", [(i, (i + d) % depth) for i in range(depth)]) if d else part
+        for d, part in zip(order, to_wire(order, mine, theirs))
+    ]
     gain, best = final_scores(parts, lax.axis_size(ALL))
     best = lax.all_to_all(best, ALL, 0, 0, tiled=True)
     return gain, jnp.max(best, axis=0)

time: 91.8 us -> 88.5 us (0.964)
  blocking collectives: 44.3 us -> 21.1 us
  waiting for transfers between devices: 10.2 us -> 20.5 us
  starting transfers between devices: 16.6 us -> 26.2 us
    all_to_all x1 -> x0, blocking collectives: 23.9 us -> none  [on_device(): parts = lax.all_to_all(sums, 'zh', 0, 0, tiled=True)]
    ppermute x0 -> x3, waiting for transfers between devices: none -> 10.3 us  [on_device(): lax.ppermute(part, 'zh', [(i, (i + d) % depth) for i in range(depth)])]
    ppermute x0 -> x3, starting transfers between devices: none -> 9.68 us  [on_device(): lax.ppermute(part, 'zh', [(i, (i + d) % depth) for i in range(depth)])]
  transfers between devices with their start and end apart: 5 -> 8, of which waited for: 2 -> 4; matrix products, arithmetic and copies ran while one was open for 0% -> 0% of each run, Pallas kernels for 11% -> 12%
where the time goes in v8:
time: 88.5 us; the launch traced here: 88.3 us
  starting transfers between devices  26.2 us (30%)
  blocking collectives  21.1 us (24%)
  waiting for transfers between devices  20.5 us (23%)
  Pallas kernels  18.9 us (21%)
    all_to_all x1, blocking collectives, on_device(): best = lax.all_to_all(best, ALL, 0, 0, tiled=True)  21.1 us
    pallas_call x4, Pallas kernels, local_sums(): pl.pallas_call(functools.partial(sums_kernel, places), out_shape=jax.Shap...  14.6 us
    ppermute x3, waiting for transfers between devices, on_device(): lax.ppermute(part, 'zh', [(i, (i + d) % depth) for i in range(depth)])  10.3 us
    ppermute x3, starting transfers between devices, on_device(): lax.ppermute(part, 'zh', [(i, (i + d) % depth) for i in range(depth)])  9.68 us
    all_to_all x1, waiting for transfers between devices, on_device(): pay = lax.all_to_all(pay, NEAR, 0, 0, tiled=True)  9.31 us
    all_to_all x1, starting transfers between devices, on_device(): pay = lax.all_to_all(pay, NEAR, 0, 0, tiled=True)  9.24 us
    ppermute x1, starting transfers between devices, on_device(): theirs = lax.ppermute(theirs, 'c', swap)  3.07 us
    ppermute x1, starting transfers between devices, on_device(): pieces[2] = lax.ppermute(pieces[2], 'xh', swap)  2.73 us
  transfers between devices with their start and end apart: 8, of which 4 were waited for; matrix products, arithmetic and copies ran while one was open for 0% of the time, Pallas kernels for 12%

profile of v8, /device:TPU:1, one launch (start us, length us, event | category | flops | bytes accessed | tf_op | source)
XLA Modules:
  0.0 88.3 jit_solution(11750911190078061344)
XLA Ops:
  0.6 0.0 copy-start
  0.6 1.9 %payload.1 = bf16[32,104,128]{2,1,0:T(8,128)(2,1)} custom-call(bf16[32,384]{1,0:T(8,128)(2,1)} %grad_hbm.1, bf16[3,128]{1,0:T(4,128)(2,1)} %bitcast.7, s32[24,128]{1,0:T(8,128)} %bitcast.6), custom_call_target="tpu_custom_call" | custom-call | tf_op jit(solution)/shard_map/payload/pallas_call | solution.py:70
  2.6 9.2 %all-to-all-start = ((bf16[32,104,128]{2,1,0:T(8,128)(2,1)}), bf16[32,104,128]{2,1,0:T(8,128)(2,1)S(1)}, u32[]{:S(2)}, u32[]{:S(2)}) async-start(bf16[32,104,128]{2,1,0:T(8,128)(2,1)} %payload.1), calls=%async_computation | async-start | bytes 1703936 | tf_op jit(solution)/shard_map/all_to_all | solution.py:277
  11.8 0.0 copy-done
  11.8 1.0 %cut_bins.1 = (bf16[2,4,4,3072]{3,2,1,0:T(4,128)(2,1)S(1)}, bf16[2,4,4,3072]{3,2,1,0:T(4,128)(2,1)S(1)}, bf16[2,4,4,3072]{3,2,1,0:T(4,128)(2,1)S(1)}, bf16[2,4,4,3072]{3,2,1,0:T(4,128)(2,1)S(1)}) custom-call(s32[128,3072]{1,0:T(8,128)S(1)} %copy-done), custom_call_target="tpu_custom_call" | custom-call | tf_op jit(solution)/shard_map/cut_bins/pallas_call | solution.py:111
  12.9 1.3 %collective-permute-start = (bf16[2,4,4,3072]{3,2,1,0:T(4,128)(2,1)S(1)}, bf16[2,4,4,3072]{3,2,1,0:T(4,128)(2,1)S(1)}, u32[]{:S(2)}, u32[]{:S(2)}) collective-permute-start(bf16[2,4,4,3072]{3,2,1,0:T(4,128)(2,1)S(1)} %get-tuple-element.19), channel_id=1, source_target_pairs={{0,16},{16,0},{1,17},{17,1},{2,18},{18,2},{3,19},{19,3},{4,20},{20... | collective-permute-start | bytes 589832 | tf_op jit(solution)/shard_map/ppermute | solution.py:279
  14.2 2.7 %collective-permute-start.1 = (bf16[2,4,4,3072]{3,2,1,0:T(4,128)(2,1)S(1)}, bf16[2,4,4,3072]{3,2,1,0:T(4,128)(2,1)S(1)}, u32[]{:S(2)}, u32[]{:S(2)}) collective-permute-start(bf16[2,4,4,3072]{3,2,1,0:T(4,128)(2,1)S(1)} %get-tuple-element.22), channel_id=1, source_target_pairs={{0,128},{128,0},{1,129},{129,1},{2,130},{130,2},{3,131},{131,3},{4... | collective-permute-start | bytes 589832 | tf_op jit(solution)/shard_map/ppermute | solution.py:280
  16.9 0.2 collective-permute-start.2
  17.1 9.3 %all-to-all-done.pay = bf16[32,104,128]{2,1,0:T(8,128)(2,1)S(1)} async-done(((bf16[32,104,128]{2,1,0:T(8,128)(2,1)}), bf16[32,104,128]{2,1,0:T(8,128)(2,1)S(1)}, u32[]{:S(2)}, u32[]{:S(2)}) %all-to-all-start) | async-done | bytes 852000 | tf_op jit(solution)/shard_map/all_to_all | solution.py:277
  26.4 1.9 %left_sums.4.refs_3_ = f32[4,264,256]{2,1,0:T(8,128)S(1)} custom-call(bf16[32,104,128]{2,1,0:T(8,128)(2,1)S(1)} %all-to-all-done.pay, bf16[2,4,4,3072]{3,2,1,0:T(4,128)(2,1)S(1)} %get-tuple-element.18.refs_0_), custom_call_target="tpu_custom_call" | custom-call | flops 1660944384 | bytes 2097152 | tf_op jit(solution)/shard_map/left_sums/pallas_call | solution.py:187
  28.4 0.0 collective-permute-done.refs_1_.refs_0_
  28.4 3.7 %left_sums.5.refs_2_ = f32[4,264,256]{2,1,0:T(8,128)S(1)} custom-call(bf16[32,104,128]{2,1,0:T(8,128)(2,1)S(1)} %all-to-all-done.pay, bf16[2,4,4,3072]{3,2,1,0:T(4,128)(2,1)S(1)} %get-tuple-element.18.refs_0_, bf16[2,4,4,3072]{3,2,1,0:T(4,128)(2,1)S(1)} %collective-permute-done.refs_1_.refs_0_), custom_call_target="tpu_custom_call" | custom-call | flops 3321888768 | bytes 2097152 | tf_op jit(solution)/shard_map/left_sums/pallas_call | solution.py:187
  32.0 0.0 collective-permute-done.1.refs_0_.refs_1_
  32.0 0.9 %collective-permute-done.2.refs_1_.refs_2_ = bf16[2,4,4,3072]{3,2,1,0:T(4,128)(2,1)S(1)} collective-permute-done((bf16[2,4,4,3072]{3,2,1,0:T(4,128)(2,1)S(1)}, bf16[2,4,4,3072]{3,2,1,0:T(4,128)(2,1)S(1)}, u32[]{:S(2)}, u32[]{:S(2)}) %collective-permute-start.2) | collective-permute-done | bytes 196640 | tf_op jit(solution)/shard_map/ppermute | solution.py:281
  32.9 5.4 %left_sums.7 = f32[4,264,256]{2,1,0:T(8,128)S(1)} custom-call(bf16[32,104,128]{2,1,0:T(8,128)(2,1)S(1)} %all-to-all-done.pay, bf16[2,4,4,3072]{3,2,1,0:T(4,128)(2,1)S(1)} %collective-permute-done.refs_1_.refs_0_, bf16[2,4,4,3072]{3,2,1,0:T(4,128)(2,1)S(1)} %collective-permute-done.1.refs_0_.refs_1_, ...), custom_call_target="tpu_custom_call" | custom-call | flops 4982833152 | bytes 2097152 | tf_op jit(solution)/shard_map/left_sums/pallas_call | solution.py:187
  38.3 3.1 %collective-permute-start.3 = (f32[4,264,256]{2,1,0:T(8,128)S(1)}, f32[4,264,256]{2,1,0:T(8,128)S(1)}, u32[]{:S(2)}, u32[]{:S(2)}) collective-permute-start(f32[4,264,256]{2,1,0:T(8,128)S(1)} %left_sums.7), channel_id=1, source_target_pairs={{0,8},{8,0},{1,9},{9,1},{2,10},{10,2},{3,11},{11,3},{4,12},{12,4},... | collective-permute-start | bytes 3244040 | tf_op jit(solution)/shard_map/ppermute | solution.py:287
  41.4 3.6 %left_sums.6.mine = f32[4,264,256]{2,1,0:T(8,128)S(1)} custom-call(bf16[32,104,128]{2,1,0:T(8,128)(2,1)S(1)} %all-to-all-done.pay, bf16[2,4,4,3072]{3,2,1,0:T(4,128)(2,1)S(1)} %collective-permute-done.1.refs_0_.refs_1_, bf16[2,4,4,3072]{3,2,1,0:T(4,128)(2,1)S(1)} %collective-permute-done.2.refs_1_.refs_2_, f32[4,264,256]{2,1,0:T(8,128)S(1)} %left_sums.5.refs_2_), custom_call_target="tpu_custom_call" | custom-call | flops 3321888768 | bytes 2097152 | tf_op jit(solution)/shard_map/left_sums/pallas_call | solution.py:187
  45.0 0.0 collective-permute-done.3.theirs
  45.0 0.4 to_wire.1
  45.5 6.1 %collective-permute-start.4 = (s16[288,256]{1,0:T(8,128)(2,1)S(1)}, s16[288,256]{1,0:T(8,128)(2,1)S(1)}, u32[]{:S(2)}, u32[]{:S(2)}) collective-permute-start(s16[288,256]{1,0:T(8,128)(2,1)S(1)} %get-tuple-element.28), channel_id=1, source_target_pairs={{0,64},{32,96},{64,0},{96,32},{1,65},{33,97},{65,1},{97,33},{2,66}... | collective-permute-start | bytes 442376 | tf_op jit(solution)/shard_map/ppermute | solution.py:292
  51.6 1.2 %collective-permute-start.5 = (s16[288,256]{1,0:T(8,128)(2,1)S(1)}, s16[288,256]{1,0:T(8,128)(2,1)S(1)}, u32[]{:S(2)}, u32[]{:S(2)}) collective-permute-start(s16[288,256]{1,0:T(8,128)(2,1)S(1)} %get-tuple-element.29), channel_id=1, source_target_pairs={{0,32},{32,64},{64,96},{96,0},{1,33},{33,65},{65,97},{97,1},{2,34}... | collective-permute-start | bytes 442376 | tf_op jit(solution)/shard_map/ppermute | solution.py:292
  52.7 2.4 %collective-permute-start.6 = (s16[288,256]{1,0:T(8,128)(2,1)S(1)}, s16[288,256]{1,0:T(8,128)(2,1)S(1)}, u32[]{:S(2)}, u32[]{:S(2)}) collective-permute-start(s16[288,256]{1,0:T(8,128)(2,1)S(1)} %get-tuple-element.30), channel_id=1, source_target_pairs={{0,96},{32,0},{64,32},{96,64},{1,97},{33,1},{65,33},{97,65},{2,98}... | collective-permute-start | bytes 442376 | tf_op jit(solution)/shard_map/ppermute | solution.py:292
  55.1 3.6 %collective-permute-done.4.refs_0_ = s16[288,256]{1,0:T(8,128)(2,1)S(1)} collective-permute-done((s16[288,256]{1,0:T(8,128)(2,1)S(1)}, s16[288,256]{1,0:T(8,128)(2,1)S(1)}, u32[]{:S(2)}, u32[]{:S(2)}) %collective-permute-start.4) | collective-permute-done | bytes 147488 | tf_op jit(solution)/shard_map/ppermute | solution.py:292
  58.8 6.7 %collective-permute-done.5.refs_1_ = s16[288,256]{1,0:T(8,128)(2,1)S(1)} collective-permute-done((s16[288,256]{1,0:T(8,128)(2,1)S(1)}, s16[288,256]{1,0:T(8,128)(2,1)S(1)}, u32[]{:S(2)}, u32[]{:S(2)}) %collective-permute-start.5) | collective-permute-done | bytes 147488 | tf_op jit(solution)/shard_map/ppermute | solution.py:292
  65.4 0.0 collective-permute-done.6.refs_2_
  65.4 0.9 %split_scores.1 = (f32[4,512]{1,0:T(4,128)}, f32[256,8]{1,0:T(8,128)S(1)}) custom-call(s16[288,256]{1,0:T(8,128)(2,1)S(1)} %collective-permute-done.4.refs_0_, s16[288,256]{1,0:T(8,128)(2,1)S(1)} %collective-permute-done.5.refs_1_, s16[288,256]{1,0:T(8,128)(2,1)S(1)} %collective-permute-done.6.refs_2_, s16[288,256]{1,0:T(8,128)(2,1)S(1)} %get-tuple-element.31.refs_3_), custom_call_target="tpu_custom_call" | custom-call | tf_op jit(solution)/shard_map/split_scores/pallas_call | solution.py:263
  66.4 21.1 %all_to_all.14 = f32[256,1,8]{2,1,0:T(1,128)S(1)} all-to-all(f32[256,1,8]{2,1,0:T(1,128)S(1)} %bitcast.5), channel_id=1, replica_groups=mesh['xh'=2,'zh'=4,'zl'=2,'c'=2,'y'=4,'xl'=2] {'xh','zh','zl','c','y','xl'}, dimensions={0} | all-to-all | bytes 16384 | tf_op jit(solution)/shard_map/all_to_all | solution.py:296
  87.5 0.8 reduce_max.9
Async XLA Ops:
  0.6 11.2 %copy-start = (s32[128,3072]{1,0:T(8,128)S(1)}, s32[128,3072]{1,0:T(8,128)}, u32[]{:S(2)}) copy-start(s32[128,3072]{1,0:T(8,128)} %bins_hbm.1) | copy-start | bytes 4718596
  2.6 23.8 %all-to-all-start = ((bf16[32,104,128]{2,1,0:T(8,128)(2,1)}), bf16[32,104,128]{2,1,0:T(8,128)(2,1)S(1)}, u32[]{:S(2)}, u32[]{:S(2)}) async-start(bf16[32,104,128]{2,1,0:T(8,128)(2,1)} %payload.1), calls=%async_computation | async-start | bytes 1703936 | tf_op jit(solution)/shard_map/all_to_all | solution.py:277
  12.9 15.5 %collective-permute-start = (bf16[2,4,4,3072]{3,2,1,0:T(4,128)(2,1)S(1)}, bf16[2,4,4,3072]{3,2,1,0:T(4,128)(2,1)S(1)}, u32[]{:S(2)}, u32[]{:S(2)}) collective-permute-start(bf16[2,4,4,3072]{3,2,1,0:T(4,128)(2,1)S(1)} %get-tuple-element.19), channel_id=1, source_target_pairs={{0,16},{16,0},{1,17},{17,1},{2,18},{18,2},{3,19},{19,3},{4,20},{20... | collective-permute-start | bytes 589832 | tf_op jit(solution)/shard_map/ppermute | solution.py:279
  14.2 17.8 %collective-permute-start.1 = (bf16[2,4,4,3072]{3,2,1,0:T(4,128)(2,1)S(1)}, bf16[2,4,4,3072]{3,2,1,0:T(4,128)(2,1)S(1)}, u32[]{:S(2)}, u32[]{:S(2)}) collective-permute-start(bf16[2,4,4,3072]{3,2,1,0:T(4,128)(2,1)S(1)} %get-tuple-element.22), channel_id=1, source_target_pairs={{0,128},{128,0},{1,129},{129,1},{2,130},{130,2},{3,131},{131,3},{4... | collective-permute-start | bytes 589832 | tf_op jit(solution)/shard_map/ppermute | solution.py:280
  16.9 16.0 %collective-permute-start.2 = (bf16[2,4,4,3072]{3,2,1,0:T(4,128)(2,1)S(1)}, bf16[2,4,4,3072]{3,2,1,0:T(4,128)(2,1)S(1)}, u32[]{:S(2)}, u32[]{:S(2)}) collective-permute-start(bf16[2,4,4,3072]{3,2,1,0:T(4,128)(2,1)S(1)} %get-tuple-element.23), channel_id=1, source_target_pairs={{0,144},{16,128},{128,16},{144,0},{1,145},{17,129},{129,17},{145,1... | collective-permute-start | bytes 589832 | tf_op jit(solution)/shard_map/ppermute | solution.py:281
  38.3 6.7 %collective-permute-start.3 = (f32[4,264,256]{2,1,0:T(8,128)S(1)}, f32[4,264,256]{2,1,0:T(8,128)S(1)}, u32[]{:S(2)}, u32[]{:S(2)}) collective-permute-start(f32[4,264,256]{2,1,0:T(8,128)S(1)} %left_sums.7), channel_id=1, source_target_pairs={{0,8},{8,0},{1,9},{9,1},{2,10},{10,2},{3,11},{11,3},{4,12},{12,4},... | collective-permute-start | bytes 3244040 | tf_op jit(solution)/shard_map/ppermute | solution.py:287
  45.5 13.3 %collective-permute-start.4 = (s16[288,256]{1,0:T(8,128)(2,1)S(1)}, s16[288,256]{1,0:T(8,128)(2,1)S(1)}, u32[]{:S(2)}, u32[]{:S(2)}) collective-permute-start(s16[288,256]{1,0:T(8,128)(2,1)S(1)} %get-tuple-element.28), channel_id=1, source_target_pairs={{0,64},{32,96},{64,0},{96,32},{1,65},{33,97},{65,1},{97,33},{2,66}... | collective-permute-start | bytes 442376 | tf_op jit(solution)/shard_map/ppermute | solution.py:292
  51.6 13.8 %collective-permute-start.5 = (s16[288,256]{1,0:T(8,128)(2,1)S(1)}, s16[288,256]{1,0:T(8,128)(2,1)S(1)}, u32[]{:S(2)}, u32[]{:S(2)}) collective-permute-start(s16[288,256]{1,0:T(8,128)(2,1)S(1)} %get-tuple-element.29), channel_id=1, source_target_pairs={{0,32},{32,64},{64,96},{96,0},{1,33},{33,65},{65,97},{97,1},{2,34}... | collective-permute-start | bytes 442376 | tf_op jit(solution)/shard_map/ppermute | solution.py:292
  52.7 12.7 %collective-permute-start.6 = (s16[288,256]{1,0:T(8,128)(2,1)S(1)}, s16[288,256]{1,0:T(8,128)(2,1)S(1)}, u32[]{:S(2)}, u32[]{:S(2)}) collective-permute-start(s16[288,256]{1,0:T(8,128)(2,1)S(1)} %get-tuple-element.30), channel_id=1, source_target_pairs={{0,96},{32,0},{64,32},{96,64},{1,97},{33,1},{65,33},{97,65},{2,98}... | collective-permute-start | bytes 442376 | tf_op jit(solution)/shard_map/ppermute | solution.py:292

commit v9 on v8

--- a/solution.py
+++ b/solution.py
@@ -121,9 +121,10 @@
     )(bin_index)
 
 
-def sums_kernel(places, pay, *refs):
+def sums_kernel(places, order, pay, *refs):
     pieces, before, out = refs[: len(places)], refs[len(places) : -1], refs[-1]
-    blocks = out.shape[0]
+    pairs = len(order) // 2
+    zh, depth = lax.axis_index("zh"), pieces[0].shape[1]
     columns = pay.shape[0] // 4
     layers = pay.shape[1] // OUTPUTS
     tiles = pieces[0].shape[-1] // DEPTH
@@ -163,29 +164,39 @@
                 values = jnp.concatenate(
                     [by_node(group, t * (DEPTH // 128) + k) for k in range(DEPTH // 128)], axis=1
                 )
-                for j in range(0, blocks, 2):
-                    slot = j // 2 % 2
+                def push(block, slot, m, piece=piece, t=t):
+                    bins = piece[0, (zh + order[block]) % depth, :, t * DEPTH : (t + 1) * DEPTH]
+                    pltpu.matmul_push_rhs(upto(bins), slot, m, transpose=True)
+
+                for pair in range(pairs):
                     for m in range(2):
-                        bins = piece[0, j + m, :, t * DEPTH : (t + 1) * DEPTH]
-                        pltpu.matmul_push_rhs(upto(bins), slot, m, transpose=True)
+                        push(2 * pair + m, pair % 2, m)
                     for m in range(2):
-                        pltpu.matmul_acc_lhs(sums[j + m], values, load_staged_rhs=slot)
-        for j in range(blocks):
-            total = pltpu.matmul_pop(sums[j])[0:SUM_ROWS]
+                        pltpu.matmul_acc_lhs(sums[2 * pair + m], values, load_staged_rhs=pair % 2)
+                if len(order) % 2:
+                    slot = 1 if pairs else t // 2 % 2
+                    push(2 * pairs, slot, t % 2)
+                    pltpu.matmul_acc_lhs(sums[2 * pairs + t % 2], values, load_staged_rhs=slot)
+        totals = [pltpu.matmul_pop(ref)[0:SUM_ROWS] for ref in sums]
+        if len(order) % 2:
+            totals[-2:] = [totals[-2] + totals[-1]]
+        for j, total in enumerate(totals):
             for term in before:
                 total = total + term[j]
             out[j] = total
 
-    pl.run_scoped(body, *[pltpu.ACC(j % 2)((GRAD_ROWS + 16, LANES), f32) for j in range(blocks)])
-
-
-def local_sums(core, places, pay, pieces, before=()):
-    halves, blocks, owned, shard_rows = pieces[0].shape
-    bins_spec = pl.BlockSpec((1, blocks, owned, shard_rows), lambda j: (core, 0, 0, 0))
+    count = len(order) + len(order) % 2
+    pl.run_scoped(body, *[pltpu.ACC(j % 2)((GRAD_ROWS + 16, LANES), f32) for j in range(count)])
+
+
+def local_sums(core, places, order, pay, pieces, before=()):
+    halves, depth, owned, shard_rows = pieces[0].shape
+    blocks = len(order)
+    bins_spec = pl.BlockSpec((1, depth, owned, shard_rows), lambda j: (core, 0, 0, 0))
     pay_spec = pl.BlockSpec(pay.shape, lambda j: (0, 0, 0))
     flops = 2 * SUM_ROWS * len(places) * shard_rows * LANES * blocks
     return pl.pallas_call(
-        functools.partial(sums_kernel, places),
+        functools.partial(sums_kernel, places, order),
         out_shape=jax.ShapeDtypeStruct((blocks, SUM_ROWS, LANES), f32),
         grid=(1,),
         in_specs=[pay_spec]
@@ -198,11 +209,9 @@
     )(pay, *pieces, *before)
 
 
-def wire_kernel(order, mine, theirs, *outs):
-    zh, depth = lax.axis_index("zh"), mine.shape[0]
-    for d, out in zip(order, outs):
-        keeper = (zh + d) % depth
-        sums = mine[keeper] + theirs[keeper]
+def wire_kernel(mine, theirs, *outs):
+    for j, out in enumerate(outs):
+        sums = mine[j] + theirs[j]
         grads = sums[0:GRAD_ROWS].reshape(NODES, OUTPUTS, LANES)
         largest = jnp.max(jnp.abs(grads), axis=1)
         octave = jnp.ceil(jnp.log2(jnp.maximum(largest, 1e-30)) * STEPS + 0.01)
@@ -216,19 +225,20 @@
         out[GRAD_ROWS:WIRE_ROWS, :] = rest.astype(jnp.int32).astype(jnp.int16)
 
 
-def to_wire(order, mine, theirs):
-    return pl.pallas_call(
-        functools.partial(wire_kernel, order),
-        out_shape=(jax.ShapeDtypeStruct((WIRE_ROWS, LANES), jnp.int16),) * len(order),
+def to_wire(mine, theirs):
+    return pl.pallas_call(
+        wire_kernel,
+        out_shape=(jax.ShapeDtypeStruct((WIRE_ROWS, LANES), jnp.int16),) * mine.shape[0],
         compiler_params=pltpu.CompilerParams(vmem_limit_bytes=24 << 20),
         name="to_wire",
     )(mine, theirs)
 
 
 def score_kernel(devices, *refs):
-    parts, (gain_out, best_out) = refs[:-2], refs[-2:]
-    left = jnp.zeros((NODES, OUTPUTS, LANES), f32)
-    left_hess = jnp.zeros((NODES, LANES), f32)
+    (mine, theirs), parts, (gain_out, best_out) = refs[:2], refs[2:-2], refs[-2:]
+    kept = mine[0] + theirs[theirs.shape[0] - 1]
+    left = kept[0:GRAD_ROWS].reshape(NODES, OUTPUTS, LANES)
+    left_hess = kept[GRAD_ROWS:SUM_ROWS]
     for part in parts:
         scaled = part[0:GRAD_ROWS, :].astype(jnp.int32).astype(f32)
         rest = part[GRAD_ROWS:WIRE_ROWS, :].astype(jnp.int32).astype(f32)
@@ -279,19 +289,22 @@
     pieces[1] = lax.ppermute(pieces[1], "zl", swap)
     pieces[2] = lax.ppermute(pieces[2], "xh", swap)
     pieces[3] = lax.ppermute(pieces[3], ("xh", "zl"), [(0, 3), (1, 2), (2, 1), (3, 0)])
-    near = [None, local_sums(1, (0,), pay, pieces[:1])]
+    leaving, kept = (2, 1, 3), (0,)
+    near = [None, local_sums(1, (0,), leaving + kept, pay, pieces[:1])]
     near[1], pieces[1] = lax.optimization_barrier((near[1], pieces[1]))
-    near[0] = local_sums(0, (0, 1), pay, pieces[:2])
+    near[0] = local_sums(0, (0, 1), leaving, pay, pieces[:2])
     near, pieces[2:] = lax.optimization_barrier((near, pieces[2:]))
-    theirs = local_sums(1, (1, 2, 3), pay, pieces[1:], (near[1],))
+    theirs = local_sums(1, (1, 2, 3), leaving + kept, pay, pieces[1:], (near[1],))
     theirs = lax.ppermute(theirs, "c", swap)
-    mine = local_sums(0, (2, 3), pay, pieces[2:], (near[0],))
+    mine = local_sums(0, (2, 3), leaving, pay, pieces[2:], (near[0],))
     depth = lax.axis_size("zh")
-    order = (2, 1, 3, 0)
+    wires = to_wire(mine, theirs)
+    wires, pay = lax.optimization_barrier((wires, pay))
     parts = [
-        lax.ppermute(part, "zh", [(i, (i + d) % depth) for i in range(depth)]) if d else part
-        for d, part in zip(order, to_wire(order, mine, theirs))
+        lax.ppermute(part, "zh", [(i, (i + d) % depth) for i in range(depth)])
+        for d, part in zip(leaving, wires)
     ]
+    parts = [local_sums(0, (0, 1, 2, 3), kept, pay, pieces), theirs] + parts
     gain, best = final_scores(parts, lax.axis_size(ALL))
     best = lax.all_to_all(best, ALL, 0, 0, tiled=True)
     return gain, jnp.max(best, axis=0)

time: 88.5 us -> 87.2 us (0.985)
  waiting for transfers between devices: 20.5 us -> 19.2 us
    ppermute x3, waiting for transfers between devices: 10.3 us -> 8.2 us  [on_device(): lax.ppermute(part, 'zh', [(i, (i + d) % depth) for i in range(depth)])]
    pallas_call x5 -> x6, Pallas kernels: 15 us -> 15.2 us  [the longest x5 14.9 us: local_sums(): pl.pallas_call(functools.partial(sums_kernel, places, order), out_shape=j...]
where the time goes in v9:
time: 87.2 us; the launch traced here: 87 us
  starting transfers between devices  25.4 us (29%)
  blocking collectives  21.7 us (25%)
  waiting for transfers between devices  19.2 us (22%)
  Pallas kernels  19.1 us (22%)
    all_to_all x1, blocking collectives, on_device(): best = lax.all_to_all(best, ALL, 0, 0, tiled=True)  21.7 us
    pallas_call x5, Pallas kernels, local_sums(): pl.pallas_call(functools.partial(sums_kernel, places, order), out_shape=j...  14.9 us
    ppermute x3, starting transfers between devices, on_device(): lax.ppermute(part, 'zh', [(i, (i + d) % depth) for i in range(depth)])  9.67 us
    all_to_all x1, waiting for transfers between devices, on_device(): pay = lax.all_to_all(pay, NEAR, 0, 0, tiled=True)  9.31 us
    all_to_all x1, starting transfers between devices, on_device(): pay = lax.all_to_all(pay, NEAR, 0, 0, tiled=True)  9.24 us
    ppermute x3, waiting for transfers between devices, on_device(): lax.ppermute(part, 'zh', [(i, (i + d) % depth) for i in range(depth)])  8.2 us
    ppermute x1, starting transfers between devices, on_device(): pieces[2] = lax.ppermute(pieces[2], 'xh', swap)  2.73 us
    ppermute x1, starting transfers between devices, on_device(): theirs = lax.ppermute(theirs, 'c', swap)  2.29 us
  transfers between devices with their start and end apart: 8, of which 4 were waited for; matrix products, arithmetic and copies ran while one was open for 0% of the time, Pallas kernels for 12%

profile of v9, /device:TPU:1, one launch (start us, length us, event | category | flops | bytes accessed | tf_op | source)
XLA Modules:
  0.0 87.0 jit_solution(1999059715919011246)
XLA Ops:
  0.6 0.0 copy-start
  0.6 1.9 %payload.1 = bf16[32,104,128]{2,1,0:T(8,128)(2,1)} custom-call(bf16[32,384]{1,0:T(8,128)(2,1)} %grad_hbm.1, bf16[3,128]{1,0:T(4,128)(2,1)} %bitcast.7, s32[24,128]{1,0:T(8,128)} %bitcast.6), custom_call_target="tpu_custom_call" | custom-call | tf_op jit(solution)/shard_map/payload/pallas_call | solution.py:70
  2.6 9.2 %all-to-all-start = ((bf16[32,104,128]{2,1,0:T(8,128)(2,1)}), bf16[32,104,128]{2,1,0:T(8,128)(2,1)S(1)}, u32[]{:S(2)}, u32[]{:S(2)}) async-start(bf16[32,104,128]{2,1,0:T(8,128)(2,1)} %payload.1), calls=%async_computation | async-start | bytes 1703936 | tf_op jit(solution)/shard_map/all_to_all | solution.py:287
  11.8 0.0 copy-done
  11.8 1.0 %cut_bins.1 = (bf16[2,4,4,3072]{3,2,1,0:T(4,128)(2,1)S(1)}, bf16[2,4,4,3072]{3,2,1,0:T(4,128)(2,1)S(1)}, bf16[2,4,4,3072]{3,2,1,0:T(4,128)(2,1)S(1)}, bf16[2,4,4,3072]{3,2,1,0:T(4,128)(2,1)S(1)}) custom-call(s32[128,3072]{1,0:T(8,128)S(1)} %copy-done), custom_call_target="tpu_custom_call" | custom-call | tf_op jit(solution)/shard_map/cut_bins/pallas_call | solution.py:111
  12.9 1.3 %collective-permute-start = (bf16[2,4,4,3072]{3,2,1,0:T(4,128)(2,1)S(1)}, bf16[2,4,4,3072]{3,2,1,0:T(4,128)(2,1)S(1)}, u32[]{:S(2)}, u32[]{:S(2)}) collective-permute-start(bf16[2,4,4,3072]{3,2,1,0:T(4,128)(2,1)S(1)} %get-tuple-element.22), channel_id=1, source_target_pairs={{0,16},{16,0},{1,17},{17,1},{2,18},{18,2},{3,19},{19,3},{4,20},{20... | collective-permute-start | bytes 589832 | tf_op jit(solution)/shard_map/ppermute | solution.py:289
  14.2 2.7 %collective-permute-start.1 = (bf16[2,4,4,3072]{3,2,1,0:T(4,128)(2,1)S(1)}, bf16[2,4,4,3072]{3,2,1,0:T(4,128)(2,1)S(1)}, u32[]{:S(2)}, u32[]{:S(2)}) collective-permute-start(bf16[2,4,4,3072]{3,2,1,0:T(4,128)(2,1)S(1)} %get-tuple-element.25), channel_id=1, source_target_pairs={{0,128},{128,0},{1,129},{129,1},{2,130},{130,2},{3,131},{131,3},{4... | collective-permute-start | bytes 589832 | tf_op jit(solution)/shard_map/ppermute | solution.py:290
  16.9 0.2 collective-permute-start.2
  17.1 9.3 %all-to-all-done.pay = bf16[32,104,128]{2,1,0:T(8,128)(2,1)S(1)} async-done(((bf16[32,104,128]{2,1,0:T(8,128)(2,1)}), bf16[32,104,128]{2,1,0:T(8,128)(2,1)S(1)}, u32[]{:S(2)}, u32[]{:S(2)}) %all-to-all-start) | async-done | bytes 852000 | tf_op jit(solution)/shard_map/all_to_all | solution.py:287
  26.4 1.9 %left_sums.5.refs_3_ = f32[4,264,256]{2,1,0:T(8,128)S(1)} custom-call(bf16[32,104,128]{2,1,0:T(8,128)(2,1)S(1)} %all-to-all-done.pay, bf16[2,4,4,3072]{3,2,1,0:T(4,128)(2,1)S(1)} %get-tuple-element.21.refs_0_), custom_call_target="tpu_custom_call" | custom-call | flops 1660944384 | bytes 2097152 | tf_op jit(solution)/shard_map/left_sums/pallas_call | solution.py:198
  28.4 0.0 collective-permute-done.refs_1_.refs_0_
  28.4 2.8 %left_sums.6.refs_2_ = f32[3,264,256]{2,1,0:T(8,128)S(1)} custom-call(bf16[32,104,128]{2,1,0:T(8,128)(2,1)S(1)} %all-to-all-done.pay, bf16[2,4,4,3072]{3,2,1,0:T(4,128)(2,1)S(1)} %get-tuple-element.21.refs_0_, bf16[2,4,4,3072]{3,2,1,0:T(4,128)(2,1)S(1)} %collective-permute-done.refs_1_.refs_0_), custom_call_target="tpu_custom_call" | custom-call | flops 2491416576 | bytes 2097152 | tf_op jit(solution)/shard_map/left_sums/pallas_call | solution.py:198
  31.2 0.0 collective-permute-done.1.refs_0_.refs_1_.refs_2_
  31.2 1.7 %collective-permute-done.2.refs_1_.refs_2_.refs_3_ = bf16[2,4,4,3072]{3,2,1,0:T(4,128)(2,1)S(1)} collective-permute-done((bf16[2,4,4,3072]{3,2,1,0:T(4,128)(2,1)S(1)}, bf16[2,4,4,3072]{3,2,1,0:T(4,128)(2,1)S(1)}, u32[]{:S(2)}, u32[]{:S(2)}) %collective-permute-start.2) | collective-permute-done | bytes 196640 | tf_op jit(solution)/shard_map/ppermute | solution.py:291
  32.9 5.4 %left_sums.8 = f32[4,264,256]{2,1,0:T(8,128)S(1)} custom-call(bf16[32,104,128]{2,1,0:T(8,128)(2,1)S(1)} %all-to-all-done.pay, bf16[2,4,4,3072]{3,2,1,0:T(4,128)(2,1)S(1)} %collective-permute-done.refs_1_.refs_0_, bf16[2,4,4,3072]{3,2,1,0:T(4,128)(2,1)S(1)} %collective-permute-done.1.refs_0_.refs_1_.refs_2_, ...), custom_call_target="tpu_custom_call" | custom-call | flops 4982833152 | bytes 2097152 | tf_op jit(solution)/shard_map/left_sums/pallas_call | solution.py:198
  38.3 2.3 %collective-permute-start.3 = (f32[4,264,256]{2,1,0:T(8,128)S(1)}, f32[4,264,256]{2,1,0:T(8,128)S(1)}, u32[]{:S(2)}, u32[]{:S(2)}) collective-permute-start(f32[4,264,256]{2,1,0:T(8,128)S(1)} %left_sums.8), channel_id=1, source_target_pairs={{0,8},{8,0},{1,9},{9,1},{2,10},{10,2},{3,11},{11,3},{4,12},{12,4},... | collective-permute-start | bytes 3244040 | tf_op jit(solution)/shard_map/ppermute | solution.py:298
  40.6 2.8 %left_sums.7.mine = f32[3,264,256]{2,1,0:T(8,128)S(1)} custom-call(bf16[32,104,128]{2,1,0:T(8,128)(2,1)S(1)} %all-to-all-done.pay, bf16[2,4,4,3072]{3,2,1,0:T(4,128)(2,1)S(1)} %collective-permute-done.1.refs_0_.refs_1_.refs_2_, bf16[2,4,4,3072]{3,2,1,0:T(4,128)(2,1)S(1)} %collective-permute-done.2.refs_1_.refs_2_.refs_3_, f32[3,264,256]{2,1,0:T(8,128)S(1)} %left_sums.6.refs_2_), custom_call_target="tpu_custom_call" | custom-call | flops 2491416576 | bytes 2097152 | tf_op jit(solution)/shard_map/left_sums/pallas_call | solution.py:198
  43.4 0.0 collective-permute-done.3.theirs.refs_1_
  43.4 0.3 to_wire.1
  43.8 6.1 %collective-permute-start.4 = (s16[288,256]{1,0:T(8,128)(2,1)S(1)}, s16[288,256]{1,0:T(8,128)(2,1)S(1)}, u32[]{:S(2)}, u32[]{:S(2)}) collective-permute-start(s16[288,256]{1,0:T(8,128)(2,1)S(1)} %get-tuple-element.35), channel_id=1, source_target_pairs={{0,64},{32,96},{64,0},{96,32},{1,65},{33,97},{65,1},{97,33},{2,66}... | collective-permute-start | bytes 442376 | tf_op jit(solution)/shard_map/ppermute | solution.py:304
  49.9 1.2 %collective-permute-start.5 = (s16[288,256]{1,0:T(8,128)(2,1)S(1)}, s16[288,256]{1,0:T(8,128)(2,1)S(1)}, u32[]{:S(2)}, u32[]{:S(2)}) collective-permute-start(s16[288,256]{1,0:T(8,128)(2,1)S(1)} %get-tuple-element.36), channel_id=1, source_target_pairs={{0,32},{32,64},{64,96},{96,0},{1,33},{33,65},{65,97},{97,1},{2,34}... | collective-permute-start | bytes 442376 | tf_op jit(solution)/shard_map/ppermute | solution.py:304
  51.1 2.4 %collective-permute-start.6 = (s16[288,256]{1,0:T(8,128)(2,1)S(1)}, s16[288,256]{1,0:T(8,128)(2,1)S(1)}, u32[]{:S(2)}, u32[]{:S(2)}) collective-permute-start(s16[288,256]{1,0:T(8,128)(2,1)S(1)} %get-tuple-element.37), channel_id=1, source_target_pairs={{0,96},{32,0},{64,32},{96,64},{1,97},{33,1},{65,33},{97,65},{2,98}... | collective-permute-start | bytes 442376 | tf_op jit(solution)/shard_map/ppermute | solution.py:304
  53.4 1.9 %left_sums.9.refs_0_ = f32[1,264,256]{2,1,0:T(8,128)S(1)} custom-call(bf16[32,104,128]{2,1,0:T(8,128)(2,1)S(1)} %all-to-all-done.pay, bf16[2,4,4,3072]{3,2,1,0:T(4,128)(2,1)S(1)} %get-tuple-element.21.refs_0_, bf16[2,4,4,3072]{3,2,1,0:T(4,128)(2,1)S(1)} %collective-permute-done.refs_1_.refs_0_, ...), custom_call_target="tpu_custom_call" | custom-call | flops 1660944384 | bytes 2097152 | tf_op jit(solution)/shard_map/left_sums/pallas_call | solution.py:198
  55.4 0.0 collective-permute-done.4.refs_2_
  55.4 7.4 %collective-permute-done.5.refs_3_ = s16[288,256]{1,0:T(8,128)(2,1)S(1)} collective-permute-done((s16[288,256]{1,0:T(8,128)(2,1)S(1)}, s16[288,256]{1,0:T(8,128)(2,1)S(1)}, u32[]{:S(2)}, u32[]{:S(2)}) %collective-permute-start.5) | collective-permute-done | bytes 147488 | tf_op jit(solution)/shard_map/ppermute | solution.py:304
  62.8 0.8 collective-permute-done.6.refs_4_
  63.6 0.9 %split_scores.1 = (f32[4,512]{1,0:T(4,128)}, f32[256,8]{1,0:T(8,128)S(1)}) custom-call(f32[1,264,256]{2,1,0:T(8,128)S(1)} %left_sums.9.refs_0_, f32[4,264,256]{2,1,0:T(8,128)S(1)} %collective-permute-done.3.theirs.refs_1_, s16[288,256]{1,0:T(8,128)(2,1)S(1)} %collective-permute-done.4.refs_2_, s16[288,256]{1,0:T(8,128)(2,1)S(1)} %collective-permute-done.5.refs_3_, ...), custom_call_target="tpu_custom_call" | custom-call | tf_op jit(solution)/shard_map/split_scores/pallas_call | solution.py:273
  64.5 21.7 %all_to_all.14 = f32[256,1,8]{2,1,0:T(1,128)S(1)} all-to-all(f32[256,1,8]{2,1,0:T(1,128)S(1)} %bitcast.5), channel_id=1, replica_groups=mesh['xh'=2,'zh'=4,'zl'=2,'c'=2,'y'=4,'xl'=2] {'xh','zh','zl','c','y','xl'}, dimensions={0} | all-to-all | bytes 16384 | tf_op jit(solution)/shard_map/all_to_all | solution.py:309
  86.2 0.8 reduce_max.9
Async XLA Ops:
  0.6 11.2 %copy-start = (s32[128,3072]{1,0:T(8,128)S(1)}, s32[128,3072]{1,0:T(8,128)}, u32[]{:S(2)}) copy-start(s32[128,3072]{1,0:T(8,128)} %bins_hbm.1) | copy-start | bytes 4718596
  2.6 23.8 %all-to-all-start = ((bf16[32,104,128]{2,1,0:T(8,128)(2,1)}), bf16[32,104,128]{2,1,0:T(8,128)(2,1)S(1)}, u32[]{:S(2)}, u32[]{:S(2)}) async-start(bf16[32,104,128]{2,1,0:T(8,128)(2,1)} %payload.1), calls=%async_computation | async-start | bytes 1703936 | tf_op jit(solution)/shard_map/all_to_all | solution.py:287
  12.9 15.5 %collective-permute-start = (bf16[2,4,4,3072]{3,2,1,0:T(4,128)(2,1)S(1)}, bf16[2,4,4,3072]{3,2,1,0:T(4,128)(2,1)S(1)}, u32[]{:S(2)}, u32[]{:S(2)}) collective-permute-start(bf16[2,4,4,3072]{3,2,1,0:T(4,128)(2,1)S(1)} %get-tuple-element.22), channel_id=1, source_target_pairs={{0,16},{16,0},{1,17},{17,1},{2,18},{18,2},{3,19},{19,3},{4,20},{20... | collective-permute-start | bytes 589832 | tf_op jit(solution)/shard_map/ppermute | solution.py:289
  14.2 17.0 %collective-permute-start.1 = (bf16[2,4,4,3072]{3,2,1,0:T(4,128)(2,1)S(1)}, bf16[2,4,4,3072]{3,2,1,0:T(4,128)(2,1)S(1)}, u32[]{:S(2)}, u32[]{:S(2)}) collective-permute-start(bf16[2,4,4,3072]{3,2,1,0:T(4,128)(2,1)S(1)} %get-tuple-element.25), channel_id=1, source_target_pairs={{0,128},{128,0},{1,129},{129,1},{2,130},{130,2},{3,131},{131,3},{4... | collective-permute-start | bytes 589832 | tf_op jit(solution)/shard_map/ppermute | solution.py:290
  16.9 16.0 %collective-permute-start.2 = (bf16[2,4,4,3072]{3,2,1,0:T(4,128)(2,1)S(1)}, bf16[2,4,4,3072]{3,2,1,0:T(4,128)(2,1)S(1)}, u32[]{:S(2)}, u32[]{:S(2)}) collective-permute-start(bf16[2,4,4,3072]{3,2,1,0:T(4,128)(2,1)S(1)} %get-tuple-element.26), channel_id=1, source_target_pairs={{0,144},{16,128},{128,16},{144,0},{1,145},{17,129},{129,17},{145,1... | collective-permute-start | bytes 589832 | tf_op jit(solution)/shard_map/ppermute | solution.py:291
  38.3 5.1 %collective-permute-start.3 = (f32[4,264,256]{2,1,0:T(8,128)S(1)}, f32[4,264,256]{2,1,0:T(8,128)S(1)}, u32[]{:S(2)}, u32[]{:S(2)}) collective-permute-start(f32[4,264,256]{2,1,0:T(8,128)S(1)} %left_sums.8), channel_id=1, source_target_pairs={{0,8},{8,0},{1,9},{9,1},{2,10},{10,2},{3,11},{11,3},{4,12},{12,4},... | collective-permute-start | bytes 3244040 | tf_op jit(solution)/shard_map/ppermute | solution.py:298
  43.8 11.6 %collective-permute-start.4 = (s16[288,256]{1,0:T(8,128)(2,1)S(1)}, s16[288,256]{1,0:T(8,128)(2,1)S(1)}, u32[]{:S(2)}, u32[]{:S(2)}) collective-permute-start(s16[288,256]{1,0:T(8,128)(2,1)S(1)} %get-tuple-element.35), channel_id=1, source_target_pairs={{0,64},{32,96},{64,0},{96,32},{1,65},{33,97},{65,1},{97,33},{2,66}... | collective-permute-start | bytes 442376 | tf_op jit(solution)/shard_map/ppermute | solution.py:304
  49.9 13.0 %collective-permute-start.5 = (s16[288,256]{1,0:T(8,128)(2,1)S(1)}, s16[288,256]{1,0:T(8,128)(2,1)S(1)}, u32[]{:S(2)}, u32[]{:S(2)}) collective-permute-start(s16[288,256]{1,0:T(8,128)(2,1)S(1)} %get-tuple-element.36), channel_id=1, source_target_pairs={{0,32},{32,64},{64,96},{96,0},{1,33},{33,65},{65,97},{97,1},{2,34}... | collective-permute-start | bytes 442376 | tf_op jit(solution)/shard_map/ppermute | solution.py:304
  51.1 12.5 %collective-permute-start.6 = (s16[288,256]{1,0:T(8,128)(2,1)S(1)}, s16[288,256]{1,0:T(8,128)(2,1)S(1)}, u32[]{:S(2)}, u32[]{:S(2)}) collective-permute-start(s16[288,256]{1,0:T(8,128)(2,1)S(1)} %get-tuple-element.37), channel_id=1, source_target_pairs={{0,96},{32,0},{64,32},{96,64},{1,97},{33,1},{65,33},{97,65},{2,98}... | collective-permute-start | bytes 442376 | tf_op jit(solution)/shard_map/ppermute | solution.py:304

commit v10 on v9

--- a/solution.py
+++ b/solution.py
@@ -293,8 +293,9 @@
     near = [None, local_sums(1, (0,), leaving + kept, pay, pieces[:1])]
     near[1], pieces[1] = lax.optimization_barrier((near[1], pieces[1]))
     near[0] = local_sums(0, (0, 1), leaving, pay, pieces[:2])
+    near[1] = local_sums(1, (1,), leaving + kept, pay, pieces[1:2], (near[1],))
     near, pieces[2:] = lax.optimization_barrier((near, pieces[2:]))
-    theirs = local_sums(1, (1, 2, 3), leaving + kept, pay, pieces[1:], (near[1],))
+    theirs = local_sums(1, (2, 3), leaving + kept, pay, pieces[2:], (near[1],))
     theirs = lax.ppermute(theirs, "c", swap)
     mine = local_sums(0, (2, 3), leaving, pay, pieces[2:], (near[0],))
     depth = lax.axis_size("zh")

time: 87.2 us -> 87 us (level)
  starting transfers between devices: 25.4 us -> 27.1 us
  waiting for transfers between devices: 19.2 us -> 17.7 us
    ppermute x1, waiting for transfers between devices: 1.7 us -> 0.01 us  [on_device(): lax.ppermute(pieces[3], ('xh', 'zl'), [(0, 3), (1, 2), (2, 1), (3, 0)])]
    ppermute x1, starting transfers between devices: 2.29 us -> 3.96 us  [on_device(): theirs = lax.ppermute(theirs, 'c', swap)]
    pallas_call x5 -> x6, Pallas kernels: 14.9 us -> 15.1 us  [local_sums(): pl.pallas_call(functools.partial(sums_kernel, places, order), out_shape=j...]
  transfers between devices with their start and end apart: 8 -> 8, of which waited for: 4 -> 3; matrix products, arithmetic and copies ran while one was open for 0% -> 0% of each run, Pallas kernels for 12% -> 14%
where the time goes in v10:
time: 87 us; the launch traced here: 86.8 us
  starting transfers between devices  27.1 us (31%)
  blocking collectives  21 us (24%)
  Pallas kernels  19.4 us (22%)
  waiting for transfers between devices  17.7 us (20%)
    all_to_all x1, blocking collectives, on_device(): best = lax.all_to_all(best, ALL, 0, 0, tiled=True)  21 us
    pallas_call x6, Pallas kernels, local_sums(): pl.pallas_call(functools.partial(sums_kernel, places, order), out_shape=j...  15.1 us
    ppermute x3, starting transfers between devices, on_device(): lax.ppermute(part, 'zh', [(i, (i + d) % depth) for i in range(depth)])  9.67 us
    all_to_all x1, waiting for transfers between devices, on_device(): pay = lax.all_to_all(pay, NEAR, 0, 0, tiled=True)  9.31 us
    all_to_all x1, starting transfers between devices, on_device(): pay = lax.all_to_all(pay, NEAR, 0, 0, tiled=True)  9.24 us
    ppermute x3, waiting for transfers between devices, on_device(): lax.ppermute(part, 'zh', [(i, (i + d) % depth) for i in range(depth)])  8.41 us
    ppermute x1, starting transfers between devices, on_device(): theirs = lax.ppermute(theirs, 'c', swap)  3.96 us
    ppermute x1, starting transfers between devices, on_device(): pieces[2] = lax.ppermute(pieces[2], 'xh', swap)  2.73 us
  transfers between devices with their start and end apart: 8, of which 3 were waited for; matrix products, arithmetic and copies ran while one was open for 0% of the time, Pallas kernels for 14%

profile of v10, /device:TPU:1, one launch (start us, length us, event | category | flops | bytes accessed | tf_op | source)
XLA Modules:
  0.0 86.8 jit_solution(16780397590661565452)
XLA Ops:
  0.6 0.0 copy-start
  0.6 1.9 %payload.1 = bf16[32,104,128]{2,1,0:T(8,128)(2,1)} custom-call(bf16[32,384]{1,0:T(8,128)(2,1)} %grad_hbm.1, bf16[3,128]{1,0:T(4,128)(2,1)} %bitcast.7, s32[24,128]{1,0:T(8,128)} %bitcast.6), custom_call_target="tpu_custom_call" | custom-call | tf_op jit(solution)/shard_map/payload/pallas_call | solution.py:70
  2.6 9.2 %all-to-all-start = ((bf16[32,104,128]{2,1,0:T(8,128)(2,1)}), bf16[32,104,128]{2,1,0:T(8,128)(2,1)S(1)}, u32[]{:S(2)}, u32[]{:S(2)}) async-start(bf16[32,104,128]{2,1,0:T(8,128)(2,1)} %payload.1), calls=%async_computation | async-start | bytes 1703936 | tf_op jit(solution)/shard_map/all_to_all | solution.py:287
  11.8 0.0 copy-done
  11.8 1.0 %cut_bins.1 = (bf16[2,4,4,3072]{3,2,1,0:T(4,128)(2,1)S(1)}, bf16[2,4,4,3072]{3,2,1,0:T(4,128)(2,1)S(1)}, bf16[2,4,4,3072]{3,2,1,0:T(4,128)(2,1)S(1)}, bf16[2,4,4,3072]{3,2,1,0:T(4,128)(2,1)S(1)}) custom-call(s32[128,3072]{1,0:T(8,128)S(1)} %copy-done), custom_call_target="tpu_custom_call" | custom-call | tf_op jit(solution)/shard_map/cut_bins/pallas_call | solution.py:111
  12.9 1.3 %collective-permute-start = (bf16[2,4,4,3072]{3,2,1,0:T(4,128)(2,1)S(1)}, bf16[2,4,4,3072]{3,2,1,0:T(4,128)(2,1)S(1)}, u32[]{:S(2)}, u32[]{:S(2)}) collective-permute-start(bf16[2,4,4,3072]{3,2,1,0:T(4,128)(2,1)S(1)} %get-tuple-element.22), channel_id=1, source_target_pairs={{0,16},{16,0},{1,17},{17,1},{2,18},{18,2},{3,19},{19,3},{4,20},{20... | collective-permute-start | bytes 589832 | tf_op jit(solution)/shard_map/ppermute | solution.py:289
  14.2 2.7 %collective-permute-start.1 = (bf16[2,4,4,3072]{3,2,1,0:T(4,128)(2,1)S(1)}, bf16[2,4,4,3072]{3,2,1,0:T(4,128)(2,1)S(1)}, u32[]{:S(2)}, u32[]{:S(2)}) collective-permute-start(bf16[2,4,4,3072]{3,2,1,0:T(4,128)(2,1)S(1)} %get-tuple-element.25), channel_id=1, source_target_pairs={{0,128},{128,0},{1,129},{129,1},{2,130},{130,2},{3,131},{131,3},{4... | collective-permute-start | bytes 589832 | tf_op jit(solution)/shard_map/ppermute | solution.py:290
  16.9 0.2 collective-permute-start.2
  17.1 9.3 %all-to-all-done.pay = bf16[32,104,128]{2,1,0:T(8,128)(2,1)S(1)} async-done(((bf16[32,104,128]{2,1,0:T(8,128)(2,1)}), bf16[32,104,128]{2,1,0:T(8,128)(2,1)S(1)}, u32[]{:S(2)}, u32[]{:S(2)}) %all-to-all-start) | async-done | bytes 852000 | tf_op jit(solution)/shard_map/all_to_all | solution.py:287
  26.4 1.9 %left_sums.6.refs_1_ = f32[4,264,256]{2,1,0:T(8,128)S(1)} custom-call(bf16[32,104,128]{2,1,0:T(8,128)(2,1)S(1)} %all-to-all-done.pay, bf16[2,4,4,3072]{3,2,1,0:T(4,128)(2,1)S(1)} %get-tuple-element.21.refs_0_), custom_call_target="tpu_custom_call" | custom-call | flops 1660944384 | bytes 2097152 | tf_op jit(solution)/shard_map/left_sums/pallas_call | solution.py:198
  28.4 0.0 collective-permute-done.refs_1_.refs_0_
  28.4 1.9 %left_sums.8.refs_2_ = f32[4,264,256]{2,1,0:T(8,128)S(1)} custom-call(bf16[32,104,128]{2,1,0:T(8,128)(2,1)S(1)} %all-to-all-done.pay, bf16[2,4,4,3072]{3,2,1,0:T(4,128)(2,1)S(1)} %collective-permute-done.refs_1_.refs_0_, f32[4,264,256]{2,1,0:T(8,128)S(1)} %left_sums.6.refs_1_), custom_call_target="tpu_custom_call" | custom-call | flops 1660944384 | bytes 2097152 | tf_op jit(solution)/shard_map/left_sums/pallas_call | solution.py:198
  30.3 2.8 %left_sums.7.refs_2_ = f32[3,264,256]{2,1,0:T(8,128)S(1)} custom-call(bf16[32,104,128]{2,1,0:T(8,128)(2,1)S(1)} %all-to-all-done.pay, bf16[2,4,4,3072]{3,2,1,0:T(4,128)(2,1)S(1)} %get-tuple-element.21.refs_0_, bf16[2,4,4,3072]{3,2,1,0:T(4,128)(2,1)S(1)} %collective-permute-done.refs_1_.refs_0_), custom_call_target="tpu_custom_call" | custom-call | flops 2491416576 | bytes 2097152 | tf_op jit(solution)/shard_map/left_sums/pallas_call | solution.py:198
  33.2 0.0 collective-permute-done.1.refs_0_.refs_2_
  33.2 0.0 collective-permute-done.2.refs_1_.refs_3_
  33.2 3.7 %left_sums.10 = f32[4,264,256]{2,1,0:T(8,128)S(1)} custom-call(bf16[32,104,128]{2,1,0:T(8,128)(2,1)S(1)} %all-to-all-done.pay, bf16[2,4,4,3072]{3,2,1,0:T(4,128)(2,1)S(1)} %collective-permute-done.1.refs_0_.refs_2_, bf16[2,4,4,3072]{3,2,1,0:T(4,128)(2,1)S(1)} %collective-permute-done.2.refs_1_.refs_3_, f32[4,264,256]{2,1,0:T(8,128)S(1)} %left_sums.8.refs_2_), custom_call_target="tpu_custom_call" | custom-call | flops 3321888768 | bytes 2097152 | tf_op jit(solution)/shard_map/left_sums/pallas_call | solution.py:198
  36.9 4.0 %collective-permute-start.3 = (f32[4,264,256]{2,1,0:T(8,128)S(1)}, f32[4,264,256]{2,1,0:T(8,128)S(1)}, u32[]{:S(2)}, u32[]{:S(2)}) collective-permute-start(f32[4,264,256]{2,1,0:T(8,128)S(1)} %left_sums.10), channel_id=1, source_target_pairs={{0,8},{8,0},{1,9},{9,1},{2,10},{10,2},{3,11},{11,3},{4,12},{12,4},... | collective-permute-start | bytes 3244040 | tf_op jit(solution)/shard_map/ppermute | solution.py:299
  40.8 2.8 %left_sums.9.mine = f32[3,264,256]{2,1,0:T(8,128)S(1)} custom-call(bf16[32,104,128]{2,1,0:T(8,128)(2,1)S(1)} %all-to-all-done.pay, bf16[2,4,4,3072]{3,2,1,0:T(4,128)(2,1)S(1)} %collective-permute-done.1.refs_0_.refs_2_, bf16[2,4,4,3072]{3,2,1,0:T(4,128)(2,1)S(1)} %collective-permute-done.2.refs_1_.refs_3_, f32[3,264,256]{2,1,0:T(8,128)S(1)} %left_sums.7.refs_2_), custom_call_target="tpu_custom_call" | custom-call | flops 2491416576 | bytes 2097152 | tf_op jit(solution)/shard_map/left_sums/pallas_call | solution.py:198
  43.7 0.0 collective-permute-done.3.theirs.refs_1_
  43.7 0.3 to_wire.1
  44.0 6.1 %collective-permute-start.4 = (s16[288,256]{1,0:T(8,128)(2,1)S(1)}, s16[288,256]{1,0:T(8,128)(2,1)S(1)}, u32[]{:S(2)}, u32[]{:S(2)}) collective-permute-start(s16[288,256]{1,0:T(8,128)(2,1)S(1)} %get-tuple-element.35), channel_id=1, source_target_pairs={{0,64},{32,96},{64,0},{96,32},{1,65},{33,97},{65,1},{97,33},{2,66}... | collective-permute-start | bytes 442376 | tf_op jit(solution)/shard_map/ppermute | solution.py:305
  50.1 1.2 %collective-permute-start.5 = (s16[288,256]{1,0:T(8,128)(2,1)S(1)}, s16[288,256]{1,0:T(8,128)(2,1)S(1)}, u32[]{:S(2)}, u32[]{:S(2)}) collective-permute-start(s16[288,256]{1,0:T(8,128)(2,1)S(1)} %get-tuple-element.36), channel_id=1, source_target_pairs={{0,32},{32,64},{64,96},{96,0},{1,33},{33,65},{65,97},{97,1},{2,34}... | collective-permute-start | bytes 442376 | tf_op jit(solution)/shard_map/ppermute | solution.py:305
  51.3 2.4 %collective-permute-start.6 = (s16[288,256]{1,0:T(8,128)(2,1)S(1)}, s16[288,256]{1,0:T(8,128)(2,1)S(1)}, u32[]{:S(2)}, u32[]{:S(2)}) collective-permute-start(s16[288,256]{1,0:T(8,128)(2,1)S(1)} %get-tuple-element.37), channel_id=1, source_target_pairs={{0,96},{32,0},{64,32},{96,64},{1,97},{33,1},{65,33},{97,65},{2,98}... | collective-permute-start | bytes 442376 | tf_op jit(solution)/shard_map/ppermute | solution.py:305
  53.7 1.9 %left_sums.11.refs_0_ = f32[1,264,256]{2,1,0:T(8,128)S(1)} custom-call(bf16[32,104,128]{2,1,0:T(8,128)(2,1)S(1)} %all-to-all-done.pay, bf16[2,4,4,3072]{3,2,1,0:T(4,128)(2,1)S(1)} %get-tuple-element.21.refs_0_, bf16[2,4,4,3072]{3,2,1,0:T(4,128)(2,1)S(1)} %collective-permute-done.refs_1_.refs_0_, ...), custom_call_target="tpu_custom_call" | custom-call | flops 1660944384 | bytes 2097152 | tf_op jit(solution)/shard_map/left_sums/pallas_call | solution.py:198
  55.6 2.0 %collective-permute-done.4.refs_2_ = s16[288,256]{1,0:T(8,128)(2,1)S(1)} collective-permute-done((s16[288,256]{1,0:T(8,128)(2,1)S(1)}, s16[288,256]{1,0:T(8,128)(2,1)S(1)}, u32[]{:S(2)}, u32[]{:S(2)}) %collective-permute-start.4) | collective-permute-done | bytes 147488 | tf_op jit(solution)/shard_map/ppermute | solution.py:305
  57.6 6.4 %collective-permute-done.5.refs_3_ = s16[288,256]{1,0:T(8,128)(2,1)S(1)} collective-permute-done((s16[288,256]{1,0:T(8,128)(2,1)S(1)}, s16[288,256]{1,0:T(8,128)(2,1)S(1)}, u32[]{:S(2)}, u32[]{:S(2)}) %collective-permute-start.5) | collective-permute-done | bytes 147488 | tf_op jit(solution)/shard_map/ppermute | solution.py:305
  64.0 0.0 collective-permute-done.6.refs_4_
  64.0 0.9 %split_scores.1 = (f32[4,512]{1,0:T(4,128)}, f32[256,8]{1,0:T(8,128)S(1)}) custom-call(f32[1,264,256]{2,1,0:T(8,128)S(1)} %left_sums.11.refs_0_, f32[4,264,256]{2,1,0:T(8,128)S(1)} %collective-permute-done.3.theirs.refs_1_, s16[288,256]{1,0:T(8,128)(2,1)S(1)} %collective-permute-done.4.refs_2_, s16[288,256]{1,0:T(8,128)(2,1)S(1)} %collective-permute-done.5.refs_3_, ...), custom_call_target="tpu_custom_call" | custom-call | tf_op jit(solution)/shard_map/split_scores/pallas_call | solution.py:273
  65.0 21.0 %all_to_all.14 = f32[256,1,8]{2,1,0:T(1,128)S(1)} all-to-all(f32[256,1,8]{2,1,0:T(1,128)S(1)} %bitcast.5), channel_id=1, replica_groups=mesh['xh'=2,'zh'=4,'zl'=2,'c'=2,'y'=4,'xl'=2] {'xh','zh','zl','c','y','xl'}, dimensions={0} | all-to-all | bytes 16384 | tf_op jit(solution)/shard_map/all_to_all | solution.py:310
  86.0 0.8 reduce_max.9
Async XLA Ops:
  0.6 11.2 %copy-start = (s32[128,3072]{1,0:T(8,128)S(1)}, s32[128,3072]{1,0:T(8,128)}, u32[]{:S(2)}) copy-start(s32[128,3072]{1,0:T(8,128)} %bins_hbm.1) | copy-start | bytes 4718596
  2.6 23.8 %all-to-all-start = ((bf16[32,104,128]{2,1,0:T(8,128)(2,1)}), bf16[32,104,128]{2,1,0:T(8,128)(2,1)S(1)}, u32[]{:S(2)}, u32[]{:S(2)}) async-start(bf16[32,104,128]{2,1,0:T(8,128)(2,1)} %payload.1), calls=%async_computation | async-start | bytes 1703936 | tf_op jit(solution)/shard_map/all_to_all | solution.py:287
  12.9 15.5 %collective-permute-start = (bf16[2,4,4,3072]{3,2,1,0:T(4,128)(2,1)S(1)}, bf16[2,4,4,3072]{3,2,1,0:T(4,128)(2,1)S(1)}, u32[]{:S(2)}, u32[]{:S(2)}) collective-permute-start(bf16[2,4,4,3072]{3,2,1,0:T(4,128)(2,1)S(1)} %get-tuple-element.22), channel_id=1, source_target_pairs={{0,16},{16,0},{1,17},{17,1},{2,18},{18,2},{3,19},{19,3},{4,20},{20... | collective-permute-start | bytes 589832 | tf_op jit(solution)/shard_map/ppermute | solution.py:289
  14.2 19.0 %collective-permute-start.1 = (bf16[2,4,4,3072]{3,2,1,0:T(4,128)(2,1)S(1)}, bf16[2,4,4,3072]{3,2,1,0:T(4,128)(2,1)S(1)}, u32[]{:S(2)}, u32[]{:S(2)}) collective-permute-start(bf16[2,4,4,3072]{3,2,1,0:T(4,128)(2,1)S(1)} %get-tuple-element.25), channel_id=1, source_target_pairs={{0,128},{128,0},{1,129},{129,1},{2,130},{130,2},{3,131},{131,3},{4... | collective-permute-start | bytes 589832 | tf_op jit(solution)/shard_map/ppermute | solution.py:290
  16.9 16.3 %collective-permute-start.2 = (bf16[2,4,4,3072]{3,2,1,0:T(4,128)(2,1)S(1)}, bf16[2,4,4,3072]{3,2,1,0:T(4,128)(2,1)S(1)}, u32[]{:S(2)}, u32[]{:S(2)}) collective-permute-start(bf16[2,4,4,3072]{3,2,1,0:T(4,128)(2,1)S(1)} %get-tuple-element.26), channel_id=1, source_target_pairs={{0,144},{16,128},{128,16},{144,0},{1,145},{17,129},{129,17},{145,1... | collective-permute-start | bytes 589832 | tf_op jit(solution)/shard_map/ppermute | solution.py:291
  36.9 6.8 %collective-permute-start.3 = (f32[4,264,256]{2,1,0:T(8,128)S(1)}, f32[4,264,256]{2,1,0:T(8,128)S(1)}, u32[]{:S(2)}, u32[]{:S(2)}) collective-permute-start(f32[4,264,256]{2,1,0:T(8,128)S(1)} %left_sums.10), channel_id=1, source_target_pairs={{0,8},{8,0},{1,9},{9,1},{2,10},{10,2},{3,11},{11,3},{4,12},{12,4},... | collective-permute-start | bytes 3244040 | tf_op jit(solution)/shard_map/ppermute | solution.py:299
  44.0 13.6 %collective-permute-start.4 = (s16[288,256]{1,0:T(8,128)(2,1)S(1)}, s16[288,256]{1,0:T(8,128)(2,1)S(1)}, u32[]{:S(2)}, u32[]{:S(2)}) collective-permute-start(s16[288,256]{1,0:T(8,128)(2,1)S(1)} %get-tuple-element.35), channel_id=1, source_target_pairs={{0,64},{32,96},{64,0},{96,32},{1,65},{33,97},{65,1},{97,33},{2,66}... | collective-permute-start | bytes 442376 | tf_op jit(solution)/shard_map/ppermute | solution.py:305
  50.1 13.9 %collective-permute-start.5 = (s16[288,256]{1,0:T(8,128)(2,1)S(1)}, s16[288,256]{1,0:T(8,128)(2,1)S(1)}, u32[]{:S(2)}, u32[]{:S(2)}) collective-permute-start(s16[288,256]{1,0:T(8,128)(2,1)S(1)} %get-tuple-element.36), channel_id=1, source_target_pairs={{0,32},{32,64},{64,96},{96,0},{1,33},{33,65},{65,97},{97,1},{2,34}... | collective-permute-start | bytes 442376 | tf_op jit(solution)/shard_map/ppermute | solution.py:305
  51.3 12.7 %collective-permute-start.6 = (s16[288,256]{1,0:T(8,128)(2,1)S(1)}, s16[288,256]{1,0:T(8,128)(2,1)S(1)}, u32[]{:S(2)}, u32[]{:S(2)}) collective-permute-start(s16[288,256]{1,0:T(8,128)(2,1)S(1)} %get-tuple-element.37), channel_id=1, source_target_pairs={{0,96},{32,0},{64,32},{96,64},{1,97},{33,1},{65,33},{97,65},{2,98}... | collective-permute-start | bytes 442376 | tf_op jit(solution)/shard_map/ppermute | solution.py:305

commit v11 on v10

--- a/solution.py
+++ b/solution.py
@@ -290,10 +290,15 @@
     pieces[2] = lax.ppermute(pieces[2], "xh", swap)
     pieces[3] = lax.ppermute(pieces[3], ("xh", "zl"), [(0, 3), (1, 2), (2, 1), (3, 0)])
     leaving, kept = (2, 1, 3), (0,)
-    near = [None, local_sums(1, (0,), leaving + kept, pay, pieces[:1])]
-    near[1], pieces[1] = lax.optimization_barrier((near[1], pieces[1]))
-    near[0] = local_sums(0, (0, 1), leaving, pay, pieces[:2])
-    near[1] = local_sums(1, (1,), leaving + kept, pay, pieces[1:2], (near[1],))
+    near = [
+        local_sums(0, (0,), leaving, pay, pieces[:1]),
+        local_sums(1, (0,), leaving + kept, pay, pieces[:1]),
+    ]
+    near, pieces[1] = lax.optimization_barrier((near, pieces[1]))
+    near = [
+        local_sums(0, (1,), leaving, pay, pieces[1:2], (near[0],)),
+        local_sums(1, (1,), leaving + kept, pay, pieces[1:2], (near[1],)),
+    ]
     near, pieces[2:] = lax.optimization_barrier((near, pieces[2:]))
     theirs = local_sums(1, (2, 3), leaving + kept, pay, pieces[2:], (near[1],))
     theirs = lax.ppermute(theirs, "c", swap)

time: 87 us -> 85.9 us (0.987)
  blocking collectives: 21 us -> 19.6 us
    all_to_all x1, blocking collectives: 21 us -> 19.6 us  [on_device(): best = lax.all_to_all(best, ALL, 0, 0, tiled=True)]
    pallas_call x6 -> x7, Pallas kernels: 15.1 us -> 15.4 us  [local_sums(): pl.pallas_call(functools.partial(sums_kernel, places, order), out_shape=j...]
  transfers between devices with their start and end apart: 8 -> 8, of which waited for: 3 -> 3; matrix products, arithmetic and copies ran while one was open for 0% -> 0% of each run, Pallas kernels for 14% -> 15%
where the time goes in v11:
time: 85.9 us; the launch traced here: 85.6 us
  starting transfers between devices  27.1 us (32%)
  Pallas kernels  19.6 us (23%)
  blocking collectives  19.6 us (23%)
  waiting for transfers between devices  17.7 us (21%)
    all_to_all x1, blocking collectives, on_device(): best = lax.all_to_all(best, ALL, 0, 0, tiled=True)  19.6 us
    pallas_call x7, Pallas kernels, local_sums(): pl.pallas_call(functools.partial(sums_kernel, places, order), out_shape=j...  15.4 us
    ppermute x3, starting transfers between devices, on_device(): lax.ppermute(part, 'zh', [(i, (i + d) % depth) for i in range(depth)])  9.66 us
    all_to_all x1, waiting for transfers between devices, on_device(): pay = lax.all_to_all(pay, NEAR, 0, 0, tiled=True)  9.31 us
    all_to_all x1, starting transfers between devices, on_device(): pay = lax.all_to_all(pay, NEAR, 0, 0, tiled=True)  9.24 us
    ppermute x3, waiting for transfers between devices, on_device(): lax.ppermute(part, 'zh', [(i, (i + d) % depth) for i in range(depth)])  8.41 us
    ppermute x1, starting transfers between devices, on_device(): theirs = lax.ppermute(theirs, 'c', swap)  3.96 us
    ppermute x1, starting transfers between devices, on_device(): pieces[2] = lax.ppermute(pieces[2], 'xh', swap)  2.73 us
  transfers between devices with their start and end apart: 8, of which 3 were waited for; matrix products, arithmetic and copies ran while one was open for 0% of the time, Pallas kernels for 15%

profile of v11, /device:TPU:1, one launch (start us, length us, event | category | flops | bytes accessed | tf_op | source)
XLA Modules:
  0.0 85.6 jit_solution(10126869239363663837)
XLA Ops:
  0.6 0.0 copy-start
  0.6 1.9 %payload.1 = bf16[32,104,128]{2,1,0:T(8,128)(2,1)} custom-call(bf16[32,384]{1,0:T(8,128)(2,1)} %grad_hbm.1, bf16[3,128]{1,0:T(4,128)(2,1)} %bitcast.7, s32[24,128]{1,0:T(8,128)} %bitcast.6), custom_call_target="tpu_custom_call" | custom-call | tf_op jit(solution)/shard_map/payload/pallas_call | solution.py:70
  2.6 9.2 %all-to-all-start = ((bf16[32,104,128]{2,1,0:T(8,128)(2,1)}), bf16[32,104,128]{2,1,0:T(8,128)(2,1)S(1)}, u32[]{:S(2)}, u32[]{:S(2)}) async-start(bf16[32,104,128]{2,1,0:T(8,128)(2,1)} %payload.1), calls=%async_computation | async-start | bytes 1703936 | tf_op jit(solution)/shard_map/all_to_all | solution.py:287
  11.8 0.0 copy-done
  11.8 1.0 %cut_bins.1 = (bf16[2,4,4,3072]{3,2,1,0:T(4,128)(2,1)S(1)}, bf16[2,4,4,3072]{3,2,1,0:T(4,128)(2,1)S(1)}, bf16[2,4,4,3072]{3,2,1,0:T(4,128)(2,1)S(1)}, bf16[2,4,4,3072]{3,2,1,0:T(4,128)(2,1)S(1)}) custom-call(s32[128,3072]{1,0:T(8,128)S(1)} %copy-done), custom_call_target="tpu_custom_call" | custom-call | tf_op jit(solution)/shard_map/cut_bins/pallas_call | solution.py:111
  12.9 1.3 %collective-permute-start = (bf16[2,4,4,3072]{3,2,1,0:T(4,128)(2,1)S(1)}, bf16[2,4,4,3072]{3,2,1,0:T(4,128)(2,1)S(1)}, u32[]{:S(2)}, u32[]{:S(2)}) collective-permute-start(bf16[2,4,4,3072]{3,2,1,0:T(4,128)(2,1)S(1)} %get-tuple-element.23), channel_id=1, source_target_pairs={{0,16},{16,0},{1,17},{17,1},{2,18},{18,2},{3,19},{19,3},{4,20},{20... | collective-permute-start | bytes 589832 | tf_op jit(solution)/shard_map/ppermute | solution.py:289
  14.2 2.7 %collective-permute-start.1 = (bf16[2,4,4,3072]{3,2,1,0:T(4,128)(2,1)S(1)}, bf16[2,4,4,3072]{3,2,1,0:T(4,128)(2,1)S(1)}, u32[]{:S(2)}, u32[]{:S(2)}) collective-permute-start(bf16[2,4,4,3072]{3,2,1,0:T(4,128)(2,1)S(1)} %get-tuple-element.27), channel_id=1, source_target_pairs={{0,128},{128,0},{1,129},{129,1},{2,130},{130,2},{3,131},{131,3},{4... | collective-permute-start | bytes 589832 | tf_op jit(solution)/shard_map/ppermute | solution.py:290
  16.9 0.2 collective-permute-start.2
  17.1 9.3 %all-to-all-done.pay = bf16[32,104,128]{2,1,0:T(8,128)(2,1)S(1)} async-done(((bf16[32,104,128]{2,1,0:T(8,128)(2,1)}), bf16[32,104,128]{2,1,0:T(8,128)(2,1)S(1)}, u32[]{:S(2)}, u32[]{:S(2)}) %all-to-all-start) | async-done | bytes 852000 | tf_op jit(solution)/shard_map/all_to_all | solution.py:287
  26.4 1.5 %left_sums.7.refs_1_ = f32[3,264,256]{2,1,0:T(8,128)S(1)} custom-call(bf16[32,104,128]{2,1,0:T(8,128)(2,1)S(1)} %all-to-all-done.pay, bf16[2,4,4,3072]{3,2,1,0:T(4,128)(2,1)S(1)} %get-tuple-element.22.refs_0_), custom_call_target="tpu_custom_call" | custom-call | flops 1245708288 | bytes 2097152 | tf_op jit(solution)/shard_map/left_sums/pallas_call | solution.py:198
  28.0 1.9 %left_sums.8.refs_1_ = f32[4,264,256]{2,1,0:T(8,128)S(1)} custom-call(bf16[32,104,128]{2,1,0:T(8,128)(2,1)S(1)} %all-to-all-done.pay, bf16[2,4,4,3072]{3,2,1,0:T(4,128)(2,1)S(1)} %get-tuple-element.22.refs_0_), custom_call_target="tpu_custom_call" | custom-call | flops 1660944384 | bytes 2097152 | tf_op jit(solution)/shard_map/left_sums/pallas_call | solution.py:198
  29.9 0.0 collective-permute-done.refs_0_.refs_1_
  29.9 1.6 %left_sums.9.refs_2_ = f32[3,264,256]{2,1,0:T(8,128)S(1)} custom-call(bf16[32,104,128]{2,1,0:T(8,128)(2,1)S(1)} %all-to-all-done.pay, bf16[2,4,4,3072]{3,2,1,0:T(4,128)(2,1)S(1)} %collective-permute-done.refs_0_.refs_1_, f32[3,264,256]{2,1,0:T(8,128)S(1)} %left_sums.7.refs_1_), custom_call_target="tpu_custom_call" | custom-call | flops 1245708288 | bytes 2097152 | tf_op jit(solution)/shard_map/left_sums/pallas_call | solution.py:198
  31.5 1.9 %left_sums.10.refs_2_ = f32[4,264,256]{2,1,0:T(8,128)S(1)} custom-call(bf16[32,104,128]{2,1,0:T(8,128)(2,1)S(1)} %all-to-all-done.pay, bf16[2,4,4,3072]{3,2,1,0:T(4,128)(2,1)S(1)} %collective-permute-done.refs_0_.refs_1_, f32[4,264,256]{2,1,0:T(8,128)S(1)} %left_sums.8.refs_1_), custom_call_target="tpu_custom_call" | custom-call | flops 1660944384 | bytes 2097152 | tf_op jit(solution)/shard_map/left_sums/pallas_call | solution.py:198
  33.4 0.0 collective-permute-done.1.refs_0_.refs_2_
  33.4 0.0 collective-permute-done.2.refs_1_.refs_3_
  33.5 3.7 %left_sums.12 = f32[4,264,256]{2,1,0:T(8,128)S(1)} custom-call(bf16[32,104,128]{2,1,0:T(8,128)(2,1)S(1)} %all-to-all-done.pay, bf16[2,4,4,3072]{3,2,1,0:T(4,128)(2,1)S(1)} %collective-permute-done.1.refs_0_.refs_2_, bf16[2,4,4,3072]{3,2,1,0:T(4,128)(2,1)S(1)} %collective-permute-done.2.refs_1_.refs_3_, f32[4,264,256]{2,1,0:T(8,128)S(1)} %left_sums.10.refs_2_), custom_call_target="tpu_custom_call" | custom-call | flops 3321888768 | bytes 2097152 | tf_op jit(solution)/shard_map/left_sums/pallas_call | solution.py:198
  37.1 4.0 %collective-permute-start.3 = (f32[4,264,256]{2,1,0:T(8,128)S(1)}, f32[4,264,256]{2,1,0:T(8,128)S(1)}, u32[]{:S(2)}, u32[]{:S(2)}) collective-permute-start(f32[4,264,256]{2,1,0:T(8,128)S(1)} %left_sums.12), channel_id=1, source_target_pairs={{0,8},{8,0},{1,9},{9,1},{2,10},{10,2},{3,11},{11,3},{4,12},{12,4},... | collective-permute-start | bytes 3244040 | tf_op jit(solution)/shard_map/ppermute | solution.py:304
  41.1 2.8 %left_sums.11.mine = f32[3,264,256]{2,1,0:T(8,128)S(1)} custom-call(bf16[32,104,128]{2,1,0:T(8,128)(2,1)S(1)} %all-to-all-done.pay, bf16[2,4,4,3072]{3,2,1,0:T(4,128)(2,1)S(1)} %collective-permute-done.1.refs_0_.refs_2_, bf16[2,4,4,3072]{3,2,1,0:T(4,128)(2,1)S(1)} %collective-permute-done.2.refs_1_.refs_3_, f32[3,264,256]{2,1,0:T(8,128)S(1)} %left_sums.9.refs_2_), custom_call_target="tpu_custom_call" | custom-call | flops 2491416576 | bytes 2097152 | tf_op jit(solution)/shard_map/left_sums/pallas_call | solution.py:198
  43.9 0.0 collective-permute-done.3.theirs.refs_1_
  43.9 0.3 to_wire.1
  44.3 6.1 %collective-permute-start.4 = (s16[288,256]{1,0:T(8,128)(2,1)S(1)}, s16[288,256]{1,0:T(8,128)(2,1)S(1)}, u32[]{:S(2)}, u32[]{:S(2)}) collective-permute-start(s16[288,256]{1,0:T(8,128)(2,1)S(1)} %get-tuple-element.37), channel_id=1, source_target_pairs={{0,64},{32,96},{64,0},{96,32},{1,65},{33,97},{65,1},{97,33},{2,66}... | collective-permute-start | bytes 442376 | tf_op jit(solution)/shard_map/ppermute | solution.py:310
  50.4 1.2 %collective-permute-start.5 = (s16[288,256]{1,0:T(8,128)(2,1)S(1)}, s16[288,256]{1,0:T(8,128)(2,1)S(1)}, u32[]{:S(2)}, u32[]{:S(2)}) collective-permute-start(s16[288,256]{1,0:T(8,128)(2,1)S(1)} %get-tuple-element.38), channel_id=1, source_target_pairs={{0,32},{32,64},{64,96},{96,0},{1,33},{33,65},{65,97},{97,1},{2,34}... | collective-permute-start | bytes 442376 | tf_op jit(solution)/shard_map/ppermute | solution.py:310
  51.6 2.4 %collective-permute-start.6 = (s16[288,256]{1,0:T(8,128)(2,1)S(1)}, s16[288,256]{1,0:T(8,128)(2,1)S(1)}, u32[]{:S(2)}, u32[]{:S(2)}) collective-permute-start(s16[288,256]{1,0:T(8,128)(2,1)S(1)} %get-tuple-element.39), channel_id=1, source_target_pairs={{0,96},{32,0},{64,32},{96,64},{1,97},{33,1},{65,33},{97,65},{2,98}... | collective-permute-start | bytes 442376 | tf_op jit(solution)/shard_map/ppermute | solution.py:310
  53.9 1.9 %left_sums.13.refs_0_ = f32[1,264,256]{2,1,0:T(8,128)S(1)} custom-call(bf16[32,104,128]{2,1,0:T(8,128)(2,1)S(1)} %all-to-all-done.pay, bf16[2,4,4,3072]{3,2,1,0:T(4,128)(2,1)S(1)} %get-tuple-element.22.refs_0_, bf16[2,4,4,3072]{3,2,1,0:T(4,128)(2,1)S(1)} %collective-permute-done.refs_0_.refs_1_, ...), custom_call_target="tpu_custom_call" | custom-call | flops 1660944384 | bytes 2097152 | tf_op jit(solution)/shard_map/left_sums/pallas_call | solution.py:198
  55.9 2.0 %collective-permute-done.4.refs_2_ = s16[288,256]{1,0:T(8,128)(2,1)S(1)} collective-permute-done((s16[288,256]{1,0:T(8,128)(2,1)S(1)}, s16[288,256]{1,0:T(8,128)(2,1)S(1)}, u32[]{:S(2)}, u32[]{:S(2)}) %collective-permute-start.4) | collective-permute-done | bytes 147488 | tf_op jit(solution)/shard_map/ppermute | solution.py:310
  57.8 6.4 %collective-permute-done.5.refs_3_ = s16[288,256]{1,0:T(8,128)(2,1)S(1)} collective-permute-done((s16[288,256]{1,0:T(8,128)(2,1)S(1)}, s16[288,256]{1,0:T(8,128)(2,1)S(1)}, u32[]{:S(2)}, u32[]{:S(2)}) %collective-permute-start.5) | collective-permute-done | bytes 147488 | tf_op jit(solution)/shard_map/ppermute | solution.py:310
  64.3 0.0 collective-permute-done.6.refs_4_
  64.3 0.9 %split_scores.1 = (f32[4,512]{1,0:T(4,128)}, f32[256,8]{1,0:T(8,128)S(1)}) custom-call(f32[1,264,256]{2,1,0:T(8,128)S(1)} %left_sums.13.refs_0_, f32[4,264,256]{2,1,0:T(8,128)S(1)} %collective-permute-done.3.theirs.refs_1_, s16[288,256]{1,0:T(8,128)(2,1)S(1)} %collective-permute-done.4.refs_2_, s16[288,256]{1,0:T(8,128)(2,1)S(1)} %collective-permute-done.5.refs_3_, ...), custom_call_target="tpu_custom_call" | custom-call | tf_op jit(solution)/shard_map/split_scores/pallas_call | solution.py:273
  65.2 19.6 %all_to_all.14 = f32[256,1,8]{2,1,0:T(1,128)S(1)} all-to-all(f32[256,1,8]{2,1,0:T(1,128)S(1)} %bitcast.5), channel_id=1, replica_groups=mesh['xh'=2,'zh'=4,'zl'=2,'c'=2,'y'=4,'xl'=2] {'xh','zh','zl','c','y','xl'}, dimensions={0} | all-to-all | bytes 16384 | tf_op jit(solution)/shard_map/all_to_all | solution.py:315
  84.8 0.8 reduce_max.9
Async XLA Ops:
  0.6 11.2 %copy-start = (s32[128,3072]{1,0:T(8,128)S(1)}, s32[128,3072]{1,0:T(8,128)}, u32[]{:S(2)}) copy-start(s32[128,3072]{1,0:T(8,128)} %bins_hbm.1) | copy-start | bytes 4718596
  2.6 23.8 %all-to-all-start = ((bf16[32,104,128]{2,1,0:T(8,128)(2,1)}), bf16[32,104,128]{2,1,0:T(8,128)(2,1)S(1)}, u32[]{:S(2)}, u32[]{:S(2)}) async-start(bf16[32,104,128]{2,1,0:T(8,128)(2,1)} %payload.1), calls=%async_computation | async-start | bytes 1703936 | tf_op jit(solution)/shard_map/all_to_all | solution.py:287
  12.9 17.0 %collective-permute-start = (bf16[2,4,4,3072]{3,2,1,0:T(4,128)(2,1)S(1)}, bf16[2,4,4,3072]{3,2,1,0:T(4,128)(2,1)S(1)}, u32[]{:S(2)}, u32[]{:S(2)}) collective-permute-start(bf16[2,4,4,3072]{3,2,1,0:T(4,128)(2,1)S(1)} %get-tuple-element.23), channel_id=1, source_target_pairs={{0,16},{16,0},{1,17},{17,1},{2,18},{18,2},{3,19},{19,3},{4,20},{20... | collective-permute-start | bytes 589832 | tf_op jit(solution)/shard_map/ppermute | solution.py:289
  14.2 19.2 %collective-permute-start.1 = (bf16[2,4,4,3072]{3,2,1,0:T(4,128)(2,1)S(1)}, bf16[2,4,4,3072]{3,2,1,0:T(4,128)(2,1)S(1)}, u32[]{:S(2)}, u32[]{:S(2)}) collective-permute-start(bf16[2,4,4,3072]{3,2,1,0:T(4,128)(2,1)S(1)} %get-tuple-element.27), channel_id=1, source_target_pairs={{0,128},{128,0},{1,129},{129,1},{2,130},{130,2},{3,131},{131,3},{4... | collective-permute-start | bytes 589832 | tf_op jit(solution)/shard_map/ppermute | solution.py:290
  16.9 16.5 %collective-permute-start.2 = (bf16[2,4,4,3072]{3,2,1,0:T(4,128)(2,1)S(1)}, bf16[2,4,4,3072]{3,2,1,0:T(4,128)(2,1)S(1)}, u32[]{:S(2)}, u32[]{:S(2)}) collective-permute-start(bf16[2,4,4,3072]{3,2,1,0:T(4,128)(2,1)S(1)} %get-tuple-element.28), channel_id=1, source_target_pairs={{0,144},{16,128},{128,16},{144,0},{1,145},{17,129},{129,17},{145,1... | collective-permute-start | bytes 589832 | tf_op jit(solution)/shard_map/ppermute | solution.py:291
  37.1 6.8 %collective-permute-start.3 = (f32[4,264,256]{2,1,0:T(8,128)S(1)}, f32[4,264,256]{2,1,0:T(8,128)S(1)}, u32[]{:S(2)}, u32[]{:S(2)}) collective-permute-start(f32[4,264,256]{2,1,0:T(8,128)S(1)} %left_sums.12), channel_id=1, source_target_pairs={{0,8},{8,0},{1,9},{9,1},{2,10},{10,2},{3,11},{11,3},{4,12},{12,4},... | collective-permute-start | bytes 3244040 | tf_op jit(solution)/shard_map/ppermute | solution.py:304
  44.3 13.6 %collective-permute-start.4 = (s16[288,256]{1,0:T(8,128)(2,1)S(1)}, s16[288,256]{1,0:T(8,128)(2,1)S(1)}, u32[]{:S(2)}, u32[]{:S(2)}) collective-permute-start(s16[288,256]{1,0:T(8,128)(2,1)S(1)} %get-tuple-element.37), channel_id=1, source_target_pairs={{0,64},{32,96},{64,0},{96,32},{1,65},{33,97},{65,1},{97,33},{2,66}... | collective-permute-start | bytes 442376 | tf_op jit(solution)/shard_map/ppermute | solution.py:310
  50.4 13.9 %collective-permute-start.5 = (s16[288,256]{1,0:T(8,128)(2,1)S(1)}, s16[288,256]{1,0:T(8,128)(2,1)S(1)}, u32[]{:S(2)}, u32[]{:S(2)}) collective-permute-start(s16[288,256]{1,0:T(8,128)(2,1)S(1)} %get-tuple-element.38), channel_id=1, source_target_pairs={{0,32},{32,64},{64,96},{96,0},{1,33},{33,65},{65,97},{97,1},{2,34}... | collective-permute-start | bytes 442376 | tf_op jit(solution)/shard_map/ppermute | solution.py:310
  51.6 12.7 %collective-permute-start.6 = (s16[288,256]{1,0:T(8,128)(2,1)S(1)}, s16[288,256]{1,0:T(8,128)(2,1)S(1)}, u32[]{:S(2)}, u32[]{:S(2)}) collective-permute-start(s16[288,256]{1,0:T(8,128)(2,1)S(1)} %get-tuple-element.39), channel_id=1, source_target_pairs={{0,96},{32,0},{64,32},{96,64},{1,97},{33,1},{65,33},{97,65},{2,98}... | collective-permute-start | bytes 442376 | tf_op jit(solution)/shard_map/ppermute | solution.py:310
